TPU v7x, 512 devices: a whole 4x8x8 slice. The times are simulated.
512 devices in a mesh: expert: 8 (over z_lo, x), fsdp: 64 (over z_hi, y, core).
Axes of the slice: x: 4, y: 8, z: 8 (z_hi: 4, z_lo: 2; z = z_hi * 2 + z_lo), core: 2. Of those that a mesh axis runs over, the one named last changes fastest.
Arguments:
- dense_rows: bfloat16 [128, 14336], P('fsdp', 'expert'), may hold values from -6 to 6
- noise: bfloat16 [8, 128, 14336], P('expert', 'fsdp'), may hold values from -6 to 6
- features: bfloat16 [8, 8192, 128], P('expert', 'fsdp'), may hold values from -16 to 16
- out_grads: bfloat16 [8, 8192, 14336], P('expert', 'fsdp'), may hold values from -1 to 1
Outputs:
- master: float32 [8, 128, 14336], P('expert', 'fsdp')
- first_moment: float32 [8, 128, 14336], P('expert', 'fsdp')
- second_moment: float32 [8, 128, 14336], P('expert', 'fsdp')
- expert_copy: bfloat16 [8, 128, 14336], P('expert')
All inputs are finite; a program needn't handle non-finite values.
Results may differ from a plain program's by a relative error of at most 0.004.
Values may be sent and summed in bfloat16 or wider, within the bound.
No kernel may reach another device: no remote copies, remote signals or barrier semaphores. Data moves between devices by JAX's collectives and lax.ppermute only.
A program may use at most 64 MiB of HBM per device.

v0:
```python
import jax
import jax.numpy as jnp
from jax import lax
from jax.sharding import PartitionSpec as P

noise_scale = 0.1
first_decay = 0.9
second_decay = 0.95
learn_rate = 0.2
weight_decay = 0.5
epsilon_adam = 1.0


def adamw(initial, gradient):
    first_moment = (1.0 - first_decay) * gradient
    second_moment = (1.0 - second_decay) * gradient * gradient
    update = (
        first_moment
        / (1.0 - first_decay)
        / (jnp.sqrt(second_moment / (1.0 - second_decay)) + epsilon_adam)
    )
    master = initial - learn_rate * (update + weight_decay * initial)
    return (master, first_moment, second_moment)


def body(dense_rows, noise, features, out_grads):
    dense_full = lax.all_gather(dense_rows, "expert", axis=1, tiled=True)
    initial = dense_full.astype(jnp.float32)[None] + noise_scale * noise.astype(jnp.float32)
    inputs_local = features[0]
    grads_local = out_grads[0]
    product = lax.dot_general(
        inputs_local, grads_local, (((0,), (0,)), ((), ())), preferred_element_type=jnp.float32
    )
    gradient = lax.psum_scatter(
        lax.optimization_barrier(product.astype(jnp.bfloat16)).astype(jnp.float32),
        "fsdp",
        scatter_dimension=0,
        tiled=True,
    )
    master, first_moment, second_moment = adamw(initial, gradient[None])
    expert_copy = lax.all_gather(master.astype(jnp.bfloat16), "fsdp", axis=1, tiled=True)
    return (master, first_moment, second_moment, expert_copy)


def solution(mesh):
    return jax.shard_map(
        body,
        mesh=mesh,
        in_specs=(
            P("fsdp", "expert"),
            P("expert", "fsdp", None),
            P("expert", "fsdp", None),
            P("expert", "fsdp", None),
        ),
        out_specs=(
            P("expert", "fsdp", None),
            P("expert", "fsdp", None),
            P("expert", "fsdp", None),
            P("expert", None, None),
        ),
        check_vma=False,
    )
```

profile of v0, /device:TPU:1, one launch (start us, length us, event | category | flops | bytes accessed | tf_op | source)
XLA Modules:
  0.0 503.9 jit_solution(10311162020342887844)
XLA Ops:
  7.2 0.0 copy-start
  7.2 0.0 all-gather.2.cloned.1.call-start
  7.2 0.7 copy-done
  7.9 5.0 convolution_convert_fusion
  12.9 0.0 copy-start.2
  12.9 0.0 copy-start.1
  13.0 339.0 %all-reduce.2 = f32[128,14336]{1,0:T(8,128)} all-reduce(bf16[128,14336]{1,0:T(8,128)(2,1)} %convolution_convert_fusion), channel_id=2, replica_groups=mesh['expert'=8,'fsdp'=64] {'fsdp'}, use_global_device_ids=true, to_apply=%region_0.0.clone | all-reduce | flops 1835008 | bytes 11010048
  352.0 0.0 copy-done.2
  352.0 29.0 %all_gather.6 = bf16[2,14336]{1,0:T(2,128)(2,1)S(1)} all-gather(bf16[2,1792]{1,0:T(2,128)(2,1)S(1)} %copy-done.2), channel_id=1, replica_groups=mesh['expert'=8,'fsdp'=64] {'expert'}, dimensions={1}, use_global_device_ids=true | all-gather | bytes 64512 | tf_op jit(solution)/shard_map/all_gather | solution.py:27
  381.0 1.3 dynamic-slice
  382.9 0.0 copy-done.1
  382.9 2.0 fusion.5
  384.9 0.7 copy.8
  385.7 0.0 all-gather.2.cloned.1.call-update
  385.7 1.8 fusion.3
  387.5 102.6 %all-gather.2.cloned.1.call-done = bf16[1,128,14336]{2,0,1:T(2,128)(2,1)} async-done(((bf16[1,2,14336]{2,0,1:T(2,128)(2,1)}), bf16[1,128,14336]{2,0,1:T(2,128)(2,1)}) %all-gather.2.cloned.1.call-update) | async-done | bytes 3670032 | tf_op jit(solution)/shard_map/all_gather | solution.py:41
  490.1 7.0 %copy.9 = bf16[1,128,14336]{2,1,0:T(8,128)(2,1)} copy(bf16[1,128,14336]{2,0,1:T(2,128)(2,1)} %all-gather.2.cloned.1.call-done) | data formatting | bytes 7340032
Async XLA Ops:
  7.2 0.8 copy-start
  7.2 482.9 %all-gather.2.cloned.1.call-start = ((), (), s32[]{:S(2)}) async-start(), calls=%async_computation | async-start | bytes 7454720 | tf_op jit(solution)/shard_map/all_gather | solution.py:41
  12.9 339.0 %copy-start.2 = (bf16[2,1792]{1,0:T(2,128)(2,1)S(1)}, bf16[2,1792]{1,0:T(2,128)(2,1)}, u32[]{:S(2)}) copy-start(bf16[2,1792]{1,0:T(2,128)(2,1)} %param.4) | copy-start | bytes 21508
  12.9 369.9 %copy-start.1 = (bf16[1,2,14336]{2,1,0:T(2,128)(2,1)S(1)}, bf16[1,2,14336]{2,1,0:T(2,128)(2,1)}, u32[]{:S(2)}) copy-start(bf16[1,2,14336]{2,1,0:T(2,128)(2,1)} %param.5) | copy-start | bytes 172036
Sparse Core Ops, SparseCore 0:
  385.8 104.2 all-gather.1
where the time goes:
time: 504 us
  blocking collectives  368 us (73%)
  waiting for transfers between devices  103 us (20%)
  between operations  14.7 us (3%)
  local copies, waits for them, and re-layouts  9.7 us (2%)
    unnamed x1, blocking collectives  339 us
    all_gather x1, waiting for transfers between devices, body(): lax.all_gather(master.astype(jnp.bfloat16), 'fsdp', axis=1, tiled=True)  103 us
    all_gather x1, blocking collectives, body(): dense_full = lax.all_gather(dense_rows, 'expert', axis=1, tiled=True)  29 us
  transfers between devices with their start and end apart: 1, of which 1 were waited for; matrix products, arithmetic and copies ran while one was open for 0% of the time, Pallas kernels for 0%

commit v1 on v0

v1 whole, which is shorter than its diff:
```python
import jax
import jax.numpy as jnp
from jax import lax
from jax.experimental import pallas as pl
from jax.experimental.pallas import tpu as pltpu
from jax.sharding import PartitionSpec as P

noise_scale = 0.1
first_decay = 0.9
second_decay = 0.95
learn_rate = 0.2
weight_decay = 0.5
epsilon_adam = 1.0

FF = 14336
HALF = FF // 2
ROWS = 128
TOK = 128
NZ, NY = 4, 8
F32 = jnp.float32
BF16 = jnp.bfloat16


def index(z, y, c):
    return (z * NY + y) * 2 + c


def perm(target):
    return [
        (index(z, y, c), index(*target(z, y, c)))
        for z in range(NZ)
        for y in range(NY)
        for c in range(2)
    ]


def send(x, target):
    return lax.ppermute(x, "fsdp", perm(target))


def along_y(z, y, c, k):
    return (z, 2 * ((y // 2) ^ k) + y % 2, c)


def along_z(z, y, c, k):
    return (z ^ k, y, c)


def wide(k):
    return lambda z, y, c: along_y(z, y, c, k) if c == 0 else along_z(z, y, c, k)


def narrow(k):
    return lambda z, y, c: along_z(z, y, c, k) if c == 0 else along_y(z, y, c, k)


def neighbour(z, y, c):
    return (z, y ^ 1, c)


def other_core(z, y, c):
    return (z, y, 1 - c)


def adamw(initial, gradient):
    first_moment = (1.0 - first_decay) * gradient
    second_moment = (1.0 - second_decay) * gradient * gradient
    update = (
        first_moment
        / (1.0 - first_decay)
        / (jnp.sqrt(second_moment / (1.0 - second_decay)) + epsilon_adam)
    )
    master = initial - learn_rate * (update + weight_decay * initial)
    return (master, first_moment, second_moment)


def cost(flops, nbytes):
    return pl.CostEstimate(flops=flops, bytes_accessed=nbytes, transcendentals=0)


def params(mib):
    return pltpu.CompilerParams(vmem_limit_bytes=mib << 20)


def shape(rows, dtype):
    return jax.ShapeDtypeStruct((rows, HALF), dtype)


def product_kernel(place, f_own, f_oth, g_own, g_oth, own, s1, s2, s3, left):
    @pl.when(pl.program_id(0) == 0)
    def _():
        c, o, t = place[0], place[1], place[2]
        slot = lax.broadcasted_iota(jnp.int32, (ROWS, ROWS), 0)
        row = lax.broadcasted_iota(jnp.int32, (ROWS, ROWS), 1)
        a = (slot >> 5) ^ o
        b = ((slot >> 3) & 3) ^ t
        block = jnp.where(c == 0, b * 4 + a, a * 4 + b)
        pick = (block * 8 + (slot & 7) == row).astype(F32).astype(BF16)
        for half, f in ((0, f_own), (1, f_oth)):
            left[half] = lax.dot_general(
                pick, f[...], (((1,), (1,)), ((), ())), preferred_element_type=F32
            ).astype(BF16)

    total = jnp.dot(left[0], g_own[...], preferred_element_type=F32).astype(BF16).astype(F32)
    total += jnp.dot(left[1], g_oth[...], preferred_element_type=F32).astype(BF16).astype(F32)
    own[...] = total[:32]
    for k, s in ((1, s1), (2, s2), (3, s3)):
        s[...] = total[32 * k : 32 * k + 32].astype(BF16)


def product(place, f_own, f_oth, grads, g_oth):
    n = 1792
    steps = HALF // n
    small = pl.BlockSpec((TOK, ROWS), lambda i, place: (0, 0))
    part = pl.BlockSpec((32, n), lambda i, place: (0, i))
    return pl.pallas_call(
        product_kernel,
        grid_spec=pltpu.PrefetchScalarGridSpec(
            num_scalar_prefetch=1,
            grid=(steps,),
            in_specs=[
                small,
                small,
                pl.BlockSpec((TOK, n), lambda i, place: (0, place[0] * steps + i)),
                pl.BlockSpec((TOK, n), lambda i, place: (0, i)),
            ],
            out_specs=[part] * 4,
            scratch_shapes=[pltpu.VMEM((2, ROWS, TOK), BF16)],
        ),
        out_shape=[shape(32, F32)] + [shape(32, BF16)] * 3,
        cost_estimate=cost(4 * ROWS * TOK * HALF, 6 * TOK * HALF),
        compiler_params=params(12),
    )(place, f_own, f_oth, grads, g_oth)


def first_sum_kernel(own, r1, r2, r3, keep, t1, t2, t3):
    total = own[...] + (r1[...].astype(F32) + r2[...].astype(F32) + r3[...].astype(F32))
    keep[...] = total[:8]
    for j, t in ((1, t1), (2, t2), (3, t3)):
        t[...] = total[8 * j : 8 * j + 8].astype(BF16)


def first_sum(own, parts):
    n = 1792
    part = pl.BlockSpec((32, n), lambda i: (0, i))
    out = pl.BlockSpec((8, n), lambda i: (0, i))
    return pl.pallas_call(
        first_sum_kernel,
        grid=(HALF // n,),
        in_specs=[part] * 4,
        out_specs=[out] * 4,
        out_shape=[shape(8, F32)] + [shape(8, BF16)] * 3,
        cost_estimate=cost(4 * 32 * HALF, 12 * 32 * HALF),
        compiler_params=params(12),
    )(own, *parts)


def second_sum_kernel(own, r1, r2, r3, out):
    total = own[...] + (r1[...].astype(F32) + r2[...].astype(F32) + r3[...].astype(F32))
    out[...] = total.astype(BF16)


def second_sum(own, parts):
    return pl.pallas_call(
        second_sum_kernel,
        out_shape=shape(8, BF16),
        cost_estimate=cost(4 * 8 * HALF, 12 * 8 * HALF),
        compiler_params=params(12),
    )(own, *parts)


def update_kernel(place, mine, theirs, dense, noise, copy, keep, give):
    c, p = place[0], place[3]
    gradient = mine[...].astype(F32) + theirs[...].astype(F32)
    initial = dense[...].astype(F32) + noise_scale * noise[...].astype(F32)
    copy[...] = adamw(initial, gradient)[0].astype(BF16)

    def rows_of(core):
        lower = jnp.where(core == 0, gradient[0:2], gradient[2:4])
        upper = jnp.where(core == 0, gradient[4:6], gradient[6:8])
        return jnp.where(p == 0, lower, upper)

    keep[...] = rows_of(c)
    give[...] = rows_of(1 - c)


def update(place, mine, theirs, dense, noise):
    return pl.pallas_call(
        update_kernel,
        in_specs=[pl.BlockSpec(memory_space=pltpu.SMEM)]
        + [pl.BlockSpec(memory_space=pltpu.VMEM)] * 4,
        out_shape=[shape(8, BF16), shape(2, F32), shape(2, F32)],
        cost_estimate=cost(20 * 8 * HALF, 12 * 8 * HALF),
        compiler_params=params(12),
    )(place, mine, theirs, dense, noise)


def assemble_kernel(place, *refs):
    blocks, out, sem = refs[:8], refs[8], refs[9]
    c, o, t = place[0], place[1], place[2]
    copies = []
    for half in range(2):
        for k in range(4):
            for j in range(4):
                if half == 0:
                    a, b, core = o ^ k, t ^ j, c
                else:
                    a, b, core = t ^ k, o ^ j, 1 - c
                block = jnp.where(core == 0, b * 4 + a, a * 4 + b)
                copies.append(
                    pltpu.make_async_copy(
                        blocks[half * 4 + k].at[pl.ds(8 * j, 8)],
                        out.at[
                            pl.ds(pl.multiple_of(block * 8, 8), 8),
                            pl.ds(pl.multiple_of(core * HALF, 128), HALF),
                        ],
                        sem.at[len(copies)],
                    )
                )
    for copy in copies:
        copy.start()
    for copy in copies:
        copy.wait()


def assemble(place, blocks):
    return pl.pallas_call(
        assemble_kernel,
        in_specs=[pl.BlockSpec(memory_space=pltpu.SMEM)]
        + [pl.BlockSpec(memory_space=pl.ANY)] * 8,
        out_specs=pl.BlockSpec(memory_space=pl.ANY),
        out_shape=jax.ShapeDtypeStruct((ROWS, FF), BF16),
        scratch_shapes=[pltpu.SemaphoreType.DMA((32,))],
        cost_estimate=cost(0, 4 * ROWS * FF),
        compiler_params=params(12),
    )(place, *blocks)


def in_order(bit, mine, theirs, axis):
    lower = jnp.where(bit == 0, mine, theirs)
    upper = jnp.where(bit == 0, theirs, mine)
    return jnp.concatenate([lower, upper], axis)


def body(dense_rows, noise, features, out_grads):
    f, e = lax.axis_index("fsdp"), lax.axis_index("expert")
    c, y, z = f % 2, (f // 2) % NY, f // (2 * NY)
    q, p = y // 2, y % 2
    o, t = jnp.where(c == 0, q, z), jnp.where(c == 0, z, q)
    place = jnp.stack([c, o, t, p]).astype(jnp.int32)

    grads = out_grads[0]
    f_in = send(features[0], other_core)
    g_in = send(lax.dynamic_slice(grads, (0, (1 - c) * HALF), (TOK, HALF)), other_core)

    dense = dense_rows
    for bit in (1, 2, 4):
        theirs = lax.ppermute(dense, "expert", [(i, i ^ bit) for i in range(8)])
        dense = in_order(e & bit, dense, theirs, 1)
    both = jnp.stack([dense, noise[0]])
    near = lax.dynamic_slice(both, (0, 0, c * HALF), (2, 2, HALF))
    far = lax.dynamic_slice(both, (0, 0, (1 - c) * HALF), (2, 2, HALF))
    wider = in_order(c, near, send(far, other_core), 1)
    wider = in_order(p, wider, send(wider, neighbour), 1)

    own, *chunks = product(place, features[0], f_in, grads, g_in)
    got = [send(x, wide(k)) for k, x in zip((3, 2, 1), chunks[::-1])]
    own, *chunks = first_sum(own, got)
    got = [send(x, narrow(k)) for k, x in zip((3, 2, 1), chunks[::-1])]
    mine = second_sum(own, got)
    theirs = send(mine, neighbour)
    copy, keep, give = update(place, mine, theirs, wider[0], wider[1])

    gathered = [copy] + [send(copy, narrow(k)) for k in (1, 2, 3)]
    gathered = jnp.concatenate(gathered, 0)
    blocks = [gathered] + [send(gathered, wide(k)) for k in (1, 2, 3)]
    blocks += [send(x, other_core) for x in blocks]
    expert_copy = assemble(place, blocks)

    gradient = in_order(c, keep, send(give, other_core), 1)
    initial = dense.astype(F32) + noise_scale * noise[0].astype(F32)
    master, first_moment, second_moment = adamw(initial, gradient)
    return (master[None], first_moment[None], second_moment[None], expert_copy[None])


def solution(mesh):
    return jax.shard_map(
        body,
        mesh=mesh,
        in_specs=(
            P("fsdp", "expert"),
            P("expert", "fsdp", None),
            P("expert", "fsdp", None),
            P("expert", "fsdp", None),
        ),
        out_specs=(
            P("expert", "fsdp", None),
            P("expert", "fsdp", None),
            P("expert", "fsdp", None),
            P("expert", None, None),
        ),
        check_vma=False,
    )
```

time: 504 us -> 158 us (0.31)
  blocking collectives: 368 us -> 0 us
  starting transfers between devices: 0.04 us -> 105 us
  waiting for transfers between devices: 103 us -> 34.8 us
  between operations: 14.7 us -> 1.22 us
  Pallas kernels: 0 us -> 7.58 us
    unnamed x1 -> x0, blocking collectives: 339 us -> none
    ppermute x0 -> x25, starting transfers between devices: none -> 105 us  [the longest x22 91.7 us: send(): return lax.ppermute(x, 'fsdp', perm(target))]
    all_gather x1 -> x0, waiting for transfers between devices: 103 us -> none  [body(): lax.all_gather(master.astype(jnp.bfloat16), 'fsdp', axis=1, tiled=True)]
    ppermute x0 -> x25, waiting for transfers between devices: none -> 34.8 us  [the longest x22 32.6 us: send(): return lax.ppermute(x, 'fsdp', perm(target))]
    all_gather x1 -> x0, blocking collectives: 29 us -> none  [body(): dense_full = lax.all_gather(dense_rows, 'expert', axis=1, tiled=True)]
    pallas_call x0 -> x5, Pallas kernels: none -> 7.58 us  [the longest x1 3.6 us: product(): pl.pallas_call(product_kernel, grid_spec=pltpu.PrefetchScalarGridSpec(num...]
    unnamed x8 -> x9, local copies, waits for them, and re-layouts: 8.96 us -> 2.07 us
  transfers between devices with their start and end apart: 1 -> 25, of which waited for: 1 -> 10; matrix products, arithmetic and copies ran while one was open for 0% -> 3% of each run, Pallas kernels for 0% -> 0%
where the time goes in v1:
time: 158 us; the launch traced here: 156 us
  starting transfers between devices  105 us (66%)
  waiting for transfers between devices  34.8 us (22%)
  Pallas kernels  7.58 us (5%)
  local copies, waits for them, and re-layouts  4.93 us (3%)
  other arithmetic  2.83 us (2%)
    ppermute x22, starting transfers between devices, send(): return lax.ppermute(x, 'fsdp', perm(target))  91.7 us
    ppermute x22, waiting for transfers between devices, send(): return lax.ppermute(x, 'fsdp', perm(target))  32.6 us
    ppermute x3, starting transfers between devices, body(): theirs = lax.ppermute(dense, 'expert', [(i, i ^ bit) for i in range(8)])  13.2 us
    pallas_call x1, Pallas kernels, product(): pl.pallas_call(product_kernel, grid_spec=pltpu.PrefetchScalarGridSpec(num...  3.6 us
  transfers between devices with their start and end apart: 25, of which 10 were waited for; matrix products, arithmetic and copies ran while one was open for 3% of the time, Pallas kernels for 0%

profile of v1, /device:TPU:1, one launch (start us, length us, event | category | flops | bytes accessed | tf_op | source)
XLA Modules:
  0.0 156.3 jit_solution(1442086317003948602)
XLA Ops:
  0.7 4.1 %collective-permute-start = (bf16[2,1792]{1,0:T(2,128)(2,1)}, bf16[2,1792]{1,0:T(2,128)(2,1)S(1)}, u32[]{:S(2)}, u32[]{:S(2)}) collective-permute-start(bf16[2,1792]{1,0:T(2,128)(2,1)} %param.4), channel_id=1, source_target_pairs={{0,64},{64,0},{128,192},{192,128},{256,320},{320,256},{384,448},{4... | collective-permute-start | bytes 21512 | tf_op jit(solution)/shard_map/ppermute | solution.py:258
  6.7 4.9 %collective-permute-start.1 = (bf16[2,3584]{1,0:T(2,128)(2,1)S(1)}, bf16[2,3584]{1,0:T(2,128)(2,1)S(1)}, u32[]{:S(2)}, u32[]{:S(2)}) collective-permute-start(bf16[2,3584]{1,0:T(2,128)(2,1)S(1)} %pad_maximum_fusion.4), channel_id=1, source_target_pairs={{0,128},{64,192},{128,0},{192,64},{256,384},{320,448},{384,256},{4... | collective-permute-start | bytes 43016 | tf_op jit(solution)/shard_map/ppermute | solution.py:258
  12.8 4.2 %collective-permute-start.2 = (bf16[2,7168]{1,0:T(2,128)(2,1)S(1)}, bf16[2,7168]{1,0:T(2,128)(2,1)S(1)}, u32[]{:S(2)}, u32[]{:S(2)}) collective-permute-start(bf16[2,7168]{1,0:T(2,128)(2,1)S(1)} %pad_maximum_fusion.3), channel_id=1, source_target_pairs={{0,256},{64,320},{128,384},{192,448},{256,0},{320,64},{384,128},{4... | collective-permute-start | bytes 86024 | tf_op jit(solution)/shard_map/ppermute | solution.py:258
  17.0 2.9 %dynamic-slice_bitcast_fusion = bf16[128,7168]{1,0:T(8,128)(2,1)} fusion(bf16[1,128,14336]{2,1,0:T(8,128)(2,1)} %param.7, s32[]{:T(128)S(6)} %select_n.128), kind=kLoop, calls=%fused_computation | loop fusion | bytes 3670020 | tf_op jit(solution)/shard_map/dynamic_slice | solution.py:254
  19.8 8.2 %collective-permute-start.4 = (bf16[128,7168]{1,0:T(8,128)(2,1)}, bf16[128,7168]{1,0:T(8,128)(2,1)S(1)}, u32[]{:S(2)}, u32[]{:S(2)}) collective-permute-start(bf16[128,7168]{1,0:T(8,128)(2,1)} %dynamic-slice_bitcast_fusion), channel_id=1, source_target_pairs={{0,1},{1,0},{2,3},{3,2},{4,5},{5,4},{6,7},{7,6},{8,9},{9,8},{10,11... | collective-permute-start | bytes 5505032 | tf_op jit(solution)/shard_map/ppermute | solution.py:38
  35.8 3.6 %shard_map.75 = (f32[32,7168]{1,0:T(8,128)S(1)}, bf16[32,7168]{1,0:T(8,128)(2,1)S(1)}, bf16[32,7168]{1,0:T(8,128)(2,1)}, bf16[32,7168]{1,0:T(8,128)(2,1)}) custom-call(s32[4]{0:T(128)S(1)} %pad_add_fusion.place, bf16[128,128]{1,0:T(8,128)(2,1)S(1)} %bitcast.23, bf16[128,128]{1,0:T(8,128)(2,1)S(1)} %collective-permute-done.3.f_oth, ...), custom_call_target="tpu_custom_call" | custom-call | flops 469762048 | bytes 5505024 | tf_op jit(solution)/shard_map/pallas_call | solution.py:116
  39.4 6.7 %collective-permute-start.5 = (bf16[32,7168]{1,0:T(8,128)(2,1)}, bf16[32,7168]{1,0:T(8,128)(2,1)S(1)}, u32[]{:S(2)}, u32[]{:S(2)}) collective-permute-start(bf16[32,7168]{1,0:T(8,128)(2,1)} %get-tuple-element.16), channel_id=1, source_target_pairs={{0,12},{1,49},{2,14},{3,51},{4,8},{5,53},{6,10},{7,55},{8,4},{9,57... | collective-permute-start | bytes 1376264 | tf_op jit(solution)/shard_map/ppermute | solution.py:38
  48.0 4.0 %collective-permute-start.7 = (bf16[32,7168]{1,0:T(8,128)(2,1)S(1)}, bf16[32,7168]{1,0:T(8,128)(2,1)S(1)}, u32[]{:S(2)}, u32[]{:S(2)}) collective-permute-start(bf16[32,7168]{1,0:T(8,128)(2,1)S(1)} %get-tuple-element.18), channel_id=1, source_target_pairs={{0,4},{1,17},{2,6},{3,19},{4,0},{5,21},{6,2},{7,23},{8,12},{9,25},... | collective-permute-start | bytes 1376264 | tf_op jit(solution)/shard_map/ppermute | solution.py:38
  52.2 3.2 %collective-permute-start.13 = (bf16[2,4,7168]{2,1,0:T(4,128)(2,1)S(1)}, bf16[2,4,7168]{2,1,0:T(4,128)(2,1)S(1)}, u32[]{:S(2)}, u32[]{:S(2)}) collective-permute-start(bf16[2,4,7168]{2,1,0:T(4,128)(2,1)S(1)} %pad_maximum_fusion.1), channel_id=1, source_target_pairs={{0,2},{1,3},{2,0},{3,1},{4,6},{5,7},{6,4},{7,5},{8,10},{9,11},{10,... | collective-permute-start | bytes 344072 | tf_op jit(solution)/shard_map/ppermute | solution.py:38
  55.4 11.2 %collective-permute-done.5.r1 = bf16[32,7168]{1,0:T(8,128)(2,1)S(1)} collective-permute-done((bf16[32,7168]{1,0:T(8,128)(2,1)}, bf16[32,7168]{1,0:T(8,128)(2,1)S(1)}, u32[]{:S(2)}, u32[]{:S(2)}) %collective-permute-start.5) | collective-permute-done | bytes 458784 | tf_op jit(solution)/shard_map/ppermute | solution.py:38
  66.6 5.5 %collective-permute-done.7.r3 = bf16[32,7168]{1,0:T(8,128)(2,1)S(1)} collective-permute-done((bf16[32,7168]{1,0:T(8,128)(2,1)S(1)}, bf16[32,7168]{1,0:T(8,128)(2,1)S(1)}, u32[]{:S(2)}, u32[]{:S(2)}) %collective-permute-start.7) | collective-permute-done | bytes 458784 | tf_op jit(solution)/shard_map/ppermute | solution.py:38
  72.6 4.0 %collective-permute-start.10 = (bf16[8,7168]{1,0:T(8,128)(2,1)S(1)}, bf16[8,7168]{1,0:T(8,128)(2,1)S(1)}, u32[]{:S(2)}, u32[]{:S(2)}) collective-permute-start(bf16[8,7168]{1,0:T(8,128)(2,1)S(1)} %get-tuple-element.22), channel_id=1, source_target_pairs={{0,16},{1,5},{2,18},{3,7},{4,20},{5,1},{6,22},{7,3},{8,24},{9,13},... | collective-permute-start | bytes 344072 | tf_op jit(solution)/shard_map/ppermute | solution.py:38
  76.6 5.4 %collective-permute-start.8 = (bf16[8,7168]{1,0:T(8,128)(2,1)S(1)}, bf16[8,7168]{1,0:T(8,128)(2,1)S(1)}, u32[]{:S(2)}, u32[]{:S(2)}) collective-permute-start(bf16[8,7168]{1,0:T(8,128)(2,1)S(1)} %get-tuple-element.20), channel_id=1, source_target_pairs={{0,48},{1,13},{2,50},{3,15},{4,52},{5,9},{6,54},{7,11},{8,56},{9,5... | collective-permute-start | bytes 344072 | tf_op jit(solution)/shard_map/ppermute | solution.py:38
  85.0 6.9 %collective-permute-done.9.r2 = bf16[8,7168]{1,0:T(8,128)(2,1)S(1)} collective-permute-done((bf16[8,7168]{1,0:T(8,128)(2,1)S(1)}, bf16[8,7168]{1,0:T(8,128)(2,1)S(1)}, u32[]{:S(2)}, u32[]{:S(2)}) %collective-permute-start.9) | collective-permute-done | bytes 114720 | tf_op jit(solution)/shard_map/ppermute | solution.py:38
  94.6 2.9 %collective-permute-done.11.theirs = bf16[8,7168]{1,0:T(8,128)(2,1)S(1)} collective-permute-done((bf16[8,7168]{1,0:T(8,128)(2,1)S(1)}, bf16[8,7168]{1,0:T(8,128)(2,1)S(1)}, u32[]{:S(2)}, u32[]{:S(2)}) %collective-permute-start.11) | collective-permute-done | bytes 114720 | tf_op jit(solution)/shard_map/ppermute | solution.py:38
  100.5 4.6 %collective-permute-start.16 = (bf16[8,7168]{1,0:T(8,128)(2,1)S(1)}, bf16[8,7168]{1,0:T(8,128)(2,1)S(1)}, u32[]{:S(2)}, u32[]{:S(2)}) collective-permute-start(bf16[8,7168]{1,0:T(8,128)(2,1)S(1)} %get-tuple-element.25), channel_id=1, source_target_pairs={{0,32},{1,9},{2,34},{3,11},{4,36},{5,13},{6,38},{7,15},{8,40},{9,1... | collective-permute-start | bytes 344072 | tf_op jit(solution)/shard_map/ppermute | solution.py:38
  105.1 4.6 %collective-permute-start.17 = (bf16[8,7168]{1,0:T(8,128)(2,1)S(1)}, bf16[8,7168]{1,0:T(8,128)(2,1)S(1)}, u32[]{:S(2)}, u32[]{:S(2)}) collective-permute-start(bf16[8,7168]{1,0:T(8,128)(2,1)S(1)} %get-tuple-element.25), channel_id=1, source_target_pairs={{0,48},{1,13},{2,50},{3,15},{4,52},{5,9},{6,54},{7,11},{8,56},{9,5... | collective-permute-start | bytes 344072 | tf_op jit(solution)/shard_map/ppermute | solution.py:38
  109.8 5.1 %collective-permute-start.14 = (f32[2,7168]{1,0:T(2,128)S(1)}, f32[2,7168]{1,0:T(2,128)S(1)}, u32[]{:S(2)}, u32[]{:S(2)}) collective-permute-start(f32[2,7168]{1,0:T(2,128)S(1)} %get-tuple-element.24), channel_id=1, source_target_pairs={{0,1},{1,0},{2,3},{3,2},{4,5},{5,4},{6,7},{7,6},{8,9},{9,8},{10,11... | collective-permute-start | bytes 172040 | tf_op jit(solution)/shard_map/ppermute | solution.py:38
  115.0 4.4 %collective-permute-start.18 = (bf16[32,7168]{1,0:T(8,128)(2,1)S(1)}, bf16[32,7168]{1,0:T(8,128)(2,1)S(1)}, u32[]{:S(2)}, u32[]{:S(2)}) collective-permute-start(bf16[32,7168]{1,0:T(8,128)(2,1)S(1)} %constant_dynamic-update-slice_fusion.refs_0_), channel_id=1, source_target_pairs={{0,4},{1,17},{2,6},{3,19},{4,0},{5,21},{6,2},{7,23},{8,12},{9,25},... | collective-permute-start | bytes 1376264 | tf_op jit(solution)/shard_map/ppermute | solution.py:38
  121.7 4.9 %collective-permute-start.20 = (bf16[32,7168]{1,0:T(8,128)(2,1)S(1)}, bf16[32,7168]{1,0:T(8,128)(2,1)S(1)}, u32[]{:S(2)}, u32[]{:S(2)}) collective-permute-start(bf16[32,7168]{1,0:T(8,128)(2,1)S(1)} %constant_dynamic-update-slice_fusion.refs_0_), channel_id=1, source_target_pairs={{0,12},{1,49},{2,14},{3,51},{4,8},{5,53},{6,10},{7,55},{8,4},{9,57... | collective-permute-start | bytes 1376264 | tf_op jit(solution)/shard_map/ppermute | solution.py:38
  126.6 6.5 %collective-permute-start.21 = (bf16[32,7168]{1,0:T(8,128)(2,1)S(1)}, bf16[32,7168]{1,0:T(8,128)(2,1)S(1)}, u32[]{:S(2)}, u32[]{:S(2)}) collective-permute-start(bf16[32,7168]{1,0:T(8,128)(2,1)S(1)} %constant_dynamic-update-slice_fusion.refs_0_), channel_id=1, source_target_pairs={{0,1},{1,0},{2,3},{3,2},{4,5},{5,4},{6,7},{7,6},{8,9},{9,8},{10,11... | collective-permute-start | bytes 1376264 | tf_op jit(solution)/shard_map/ppermute | solution.py:38
  133.1 4.4 %collective-permute-done.18.refs_1_ = bf16[32,7168]{1,0:T(8,128)(2,1)S(1)} collective-permute-done((bf16[32,7168]{1,0:T(8,128)(2,1)S(1)}, bf16[32,7168]{1,0:T(8,128)(2,1)S(1)}, u32[]{:S(2)}, u32[]{:S(2)}) %collective-permute-start.18) | collective-permute-done | bytes 458784 | tf_op jit(solution)/shard_map/ppermute | solution.py:38
  137.5 7.6 %collective-permute-start.22 = (bf16[32,7168]{1,0:T(8,128)(2,1)S(1)}, bf16[32,7168]{1,0:T(8,128)(2,1)S(1)}, u32[]{:S(2)}, u32[]{:S(2)}) collective-permute-start(bf16[32,7168]{1,0:T(8,128)(2,1)S(1)} %collective-permute-done.18.refs_1_), channel_id=1, source_target_pairs={{0,1},{1,0},{2,3},{3,2},{4,5},{5,4},{6,7},{7,6},{8,9},{9,8},{10,11... | collective-permute-start | bytes 1376264 | tf_op jit(solution)/shard_map/ppermute | solution.py:38
  147.1 5.2 %collective-permute-start.24 = (bf16[32,7168]{1,0:T(8,128)(2,1)S(1)}, bf16[32,7168]{1,0:T(8,128)(2,1)S(1)}, u32[]{:S(2)}, u32[]{:S(2)}) collective-permute-start(bf16[32,7168]{1,0:T(8,128)(2,1)S(1)} %collective-permute-done.20.refs_3_), channel_id=1, source_target_pairs={{0,1},{1,0},{2,3},{3,2},{4,5},{5,4},{6,7},{7,6},{8,9},{9,8},{10,11... | collective-permute-start | bytes 1376264 | tf_op jit(solution)/shard_map/ppermute | solution.py:38
  (57 shorter events, 30.0 us)
Async XLA Ops:
  0.7 5.3 %collective-permute-start = (bf16[2,1792]{1,0:T(2,128)(2,1)}, bf16[2,1792]{1,0:T(2,128)(2,1)S(1)}, u32[]{:S(2)}, u32[]{:S(2)}) collective-permute-start(bf16[2,1792]{1,0:T(2,128)(2,1)} %param.4), channel_id=1, source_target_pairs={{0,64},{64,0},{128,192},{192,128},{256,320},{320,256},{384,448},{4... | collective-permute-start | bytes 21512 | tf_op jit(solution)/shard_map/ppermute | solution.py:258
  6.7 6.0 %collective-permute-start.1 = (bf16[2,3584]{1,0:T(2,128)(2,1)S(1)}, bf16[2,3584]{1,0:T(2,128)(2,1)S(1)}, u32[]{:S(2)}, u32[]{:S(2)}) collective-permute-start(bf16[2,3584]{1,0:T(2,128)(2,1)S(1)} %pad_maximum_fusion.4), channel_id=1, source_target_pairs={{0,128},{64,192},{128,0},{192,64},{256,384},{320,448},{384,256},{4... | collective-permute-start | bytes 43016 | tf_op jit(solution)/shard_map/ppermute | solution.py:258
  12.8 17.3 %collective-permute-start.2 = (bf16[2,7168]{1,0:T(2,128)(2,1)S(1)}, bf16[2,7168]{1,0:T(2,128)(2,1)S(1)}, u32[]{:S(2)}, u32[]{:S(2)}) collective-permute-start(bf16[2,7168]{1,0:T(2,128)(2,1)S(1)} %pad_maximum_fusion.3), channel_id=1, source_target_pairs={{0,256},{64,320},{128,384},{192,448},{256,0},{320,64},{384,128},{4... | collective-permute-start | bytes 86024 | tf_op jit(solution)/shard_map/ppermute | solution.py:258
  19.8 13.9 %collective-permute-start.4 = (bf16[128,7168]{1,0:T(8,128)(2,1)}, bf16[128,7168]{1,0:T(8,128)(2,1)S(1)}, u32[]{:S(2)}, u32[]{:S(2)}) collective-permute-start(bf16[128,7168]{1,0:T(8,128)(2,1)} %dynamic-slice_bitcast_fusion), channel_id=1, source_target_pairs={{0,1},{1,0},{2,3},{3,2},{4,5},{5,4},{6,7},{7,6},{8,9},{9,8},{10,11... | collective-permute-start | bytes 5505032 | tf_op jit(solution)/shard_map/ppermute | solution.py:38
  28.0 5.7 %collective-permute-start.3 = (bf16[128,128]{1,0:T(8,128)(2,1)S(1)}, bf16[128,128]{1,0:T(8,128)(2,1)S(1)}, u32[]{:S(2)}, u32[]{:S(2)}) collective-permute-start(bf16[128,128]{1,0:T(8,128)(2,1)S(1)} %bitcast.22), channel_id=1, source_target_pairs={{0,1},{1,0},{2,3},{3,2},{4,5},{5,4},{6,7},{7,6},{8,9},{9,8},{10,11... | collective-permute-start | bytes 98312 | tf_op jit(solution)/shard_map/ppermute | solution.py:38
  39.4 27.2 %collective-permute-start.5 = (bf16[32,7168]{1,0:T(8,128)(2,1)}, bf16[32,7168]{1,0:T(8,128)(2,1)S(1)}, u32[]{:S(2)}, u32[]{:S(2)}) collective-permute-start(bf16[32,7168]{1,0:T(8,128)(2,1)} %get-tuple-element.16), channel_id=1, source_target_pairs={{0,12},{1,49},{2,14},{3,51},{4,8},{5,53},{6,10},{7,55},{8,4},{9,57... | collective-permute-start | bytes 1376264 | tf_op jit(solution)/shard_map/ppermute | solution.py:38
  46.1 20.5 %collective-permute-start.6 = (bf16[32,7168]{1,0:T(8,128)(2,1)}, bf16[32,7168]{1,0:T(8,128)(2,1)S(1)}, u32[]{:S(2)}, u32[]{:S(2)}) collective-permute-start(bf16[32,7168]{1,0:T(8,128)(2,1)} %get-tuple-element.17), channel_id=1, source_target_pairs={{0,8},{1,33},{2,10},{3,35},{4,12},{5,37},{6,14},{7,39},{8,0},{9,41... | collective-permute-start | bytes 1376264 | tf_op jit(solution)/shard_map/ppermute | solution.py:38
  48.0 24.1 %collective-permute-start.7 = (bf16[32,7168]{1,0:T(8,128)(2,1)S(1)}, bf16[32,7168]{1,0:T(8,128)(2,1)S(1)}, u32[]{:S(2)}, u32[]{:S(2)}) collective-permute-start(bf16[32,7168]{1,0:T(8,128)(2,1)S(1)} %get-tuple-element.18), channel_id=1, source_target_pairs={{0,4},{1,17},{2,6},{3,19},{4,0},{5,21},{6,2},{7,23},{8,12},{9,25},... | collective-permute-start | bytes 1376264 | tf_op jit(solution)/shard_map/ppermute | solution.py:38
  52.2 32.0 %collective-permute-start.13 = (bf16[2,4,7168]{2,1,0:T(4,128)(2,1)S(1)}, bf16[2,4,7168]{2,1,0:T(4,128)(2,1)S(1)}, u32[]{:S(2)}, u32[]{:S(2)}) collective-permute-start(bf16[2,4,7168]{2,1,0:T(4,128)(2,1)S(1)} %pad_maximum_fusion.1), channel_id=1, source_target_pairs={{0,2},{1,3},{2,0},{3,1},{4,6},{5,7},{6,4},{7,5},{8,10},{9,11},{10,... | collective-permute-start | bytes 344072 | tf_op jit(solution)/shard_map/ppermute | solution.py:38
  72.6 11.8 %collective-permute-start.10 = (bf16[8,7168]{1,0:T(8,128)(2,1)S(1)}, bf16[8,7168]{1,0:T(8,128)(2,1)S(1)}, u32[]{:S(2)}, u32[]{:S(2)}) collective-permute-start(bf16[8,7168]{1,0:T(8,128)(2,1)S(1)} %get-tuple-element.22), channel_id=1, source_target_pairs={{0,16},{1,5},{2,18},{3,7},{4,20},{5,1},{6,22},{7,3},{8,24},{9,13},... | collective-permute-start | bytes 344072 | tf_op jit(solution)/shard_map/ppermute | solution.py:38
  76.6 8.4 %collective-permute-start.8 = (bf16[8,7168]{1,0:T(8,128)(2,1)S(1)}, bf16[8,7168]{1,0:T(8,128)(2,1)S(1)}, u32[]{:S(2)}, u32[]{:S(2)}) collective-permute-start(bf16[8,7168]{1,0:T(8,128)(2,1)S(1)} %get-tuple-element.20), channel_id=1, source_target_pairs={{0,48},{1,13},{2,50},{3,15},{4,52},{5,9},{6,54},{7,11},{8,56},{9,5... | collective-permute-start | bytes 344072 | tf_op jit(solution)/shard_map/ppermute | solution.py:38
  82.0 9.9 %collective-permute-start.9 = (bf16[8,7168]{1,0:T(8,128)(2,1)S(1)}, bf16[8,7168]{1,0:T(8,128)(2,1)S(1)}, u32[]{:S(2)}, u32[]{:S(2)}) collective-permute-start(bf16[8,7168]{1,0:T(8,128)(2,1)S(1)} %get-tuple-element.21), channel_id=1, source_target_pairs={{0,32},{1,9},{2,34},{3,11},{4,36},{5,13},{6,38},{7,15},{8,40},{9,1... | collective-permute-start | bytes 344072 | tf_op jit(solution)/shard_map/ppermute | solution.py:38
  92.0 5.5 %collective-permute-start.11 = (bf16[8,7168]{1,0:T(8,128)(2,1)S(1)}, bf16[8,7168]{1,0:T(8,128)(2,1)S(1)}, u32[]{:S(2)}, u32[]{:S(2)}) collective-permute-start(bf16[8,7168]{1,0:T(8,128)(2,1)S(1)} %shard_map.77.mine), channel_id=1, source_target_pairs={{0,2},{1,3},{2,0},{3,1},{4,6},{5,7},{6,4},{7,5},{8,10},{9,11},{10,... | collective-permute-start | bytes 344072 | tf_op jit(solution)/shard_map/ppermute | solution.py:38
  98.3 16.6 %collective-permute-start.15 = (bf16[8,7168]{1,0:T(8,128)(2,1)S(1)}, bf16[8,7168]{1,0:T(8,128)(2,1)S(1)}, u32[]{:S(2)}, u32[]{:S(2)}) collective-permute-start(bf16[8,7168]{1,0:T(8,128)(2,1)S(1)} %get-tuple-element.25), channel_id=1, source_target_pairs={{0,16},{1,5},{2,18},{3,7},{4,20},{5,1},{6,22},{7,3},{8,24},{9,13},... | collective-permute-start | bytes 344072 | tf_op jit(solution)/shard_map/ppermute | solution.py:38
  100.5 14.4 %collective-permute-start.16 = (bf16[8,7168]{1,0:T(8,128)(2,1)S(1)}, bf16[8,7168]{1,0:T(8,128)(2,1)S(1)}, u32[]{:S(2)}, u32[]{:S(2)}) collective-permute-start(bf16[8,7168]{1,0:T(8,128)(2,1)S(1)} %get-tuple-element.25), channel_id=1, source_target_pairs={{0,32},{1,9},{2,34},{3,11},{4,36},{5,13},{6,38},{7,15},{8,40},{9,1... | collective-permute-start | bytes 344072 | tf_op jit(solution)/shard_map/ppermute | solution.py:38
  105.1 9.8 %collective-permute-start.17 = (bf16[8,7168]{1,0:T(8,128)(2,1)S(1)}, bf16[8,7168]{1,0:T(8,128)(2,1)S(1)}, u32[]{:S(2)}, u32[]{:S(2)}) collective-permute-start(bf16[8,7168]{1,0:T(8,128)(2,1)S(1)} %get-tuple-element.25), channel_id=1, source_target_pairs={{0,48},{1,13},{2,50},{3,15},{4,52},{5,9},{6,54},{7,11},{8,56},{9,5... | collective-permute-start | bytes 344072 | tf_op jit(solution)/shard_map/ppermute | solution.py:38
  109.8 16.8 %collective-permute-start.14 = (f32[2,7168]{1,0:T(2,128)S(1)}, f32[2,7168]{1,0:T(2,128)S(1)}, u32[]{:S(2)}, u32[]{:S(2)}) collective-permute-start(f32[2,7168]{1,0:T(2,128)S(1)} %get-tuple-element.24), channel_id=1, source_target_pairs={{0,1},{1,0},{2,3},{3,2},{4,5},{5,4},{6,7},{7,6},{8,9},{9,8},{10,11... | collective-permute-start | bytes 172040 | tf_op jit(solution)/shard_map/ppermute | solution.py:38
  115.0 22.5 %collective-permute-start.18 = (bf16[32,7168]{1,0:T(8,128)(2,1)S(1)}, bf16[32,7168]{1,0:T(8,128)(2,1)S(1)}, u32[]{:S(2)}, u32[]{:S(2)}) collective-permute-start(bf16[32,7168]{1,0:T(8,128)(2,1)S(1)} %constant_dynamic-update-slice_fusion.refs_0_), channel_id=1, source_target_pairs={{0,4},{1,17},{2,6},{3,19},{4,0},{5,21},{6,2},{7,23},{8,12},{9,25},... | collective-permute-start | bytes 1376264 | tf_op jit(solution)/shard_map/ppermute | solution.py:38
  119.4 25.7 %collective-permute-start.19 = (bf16[32,7168]{1,0:T(8,128)(2,1)S(1)}, bf16[32,7168]{1,0:T(8,128)(2,1)S(1)}, u32[]{:S(2)}, u32[]{:S(2)}) collective-permute-start(bf16[32,7168]{1,0:T(8,128)(2,1)S(1)} %constant_dynamic-update-slice_fusion.refs_0_), channel_id=1, source_target_pairs={{0,8},{1,33},{2,10},{3,35},{4,12},{5,37},{6,14},{7,39},{8,0},{9,41... | collective-permute-start | bytes 1376264 | tf_op jit(solution)/shard_map/ppermute | solution.py:38
  121.7 25.4 %collective-permute-start.20 = (bf16[32,7168]{1,0:T(8,128)(2,1)S(1)}, bf16[32,7168]{1,0:T(8,128)(2,1)S(1)}, u32[]{:S(2)}, u32[]{:S(2)}) collective-permute-start(bf16[32,7168]{1,0:T(8,128)(2,1)S(1)} %constant_dynamic-update-slice_fusion.refs_0_), channel_id=1, source_target_pairs={{0,12},{1,49},{2,14},{3,51},{4,8},{5,53},{6,10},{7,55},{8,4},{9,57... | collective-permute-start | bytes 1376264 | tf_op jit(solution)/shard_map/ppermute | solution.py:38
  126.6 26.8 %collective-permute-start.21 = (bf16[32,7168]{1,0:T(8,128)(2,1)S(1)}, bf16[32,7168]{1,0:T(8,128)(2,1)S(1)}, u32[]{:S(2)}, u32[]{:S(2)}) collective-permute-start(bf16[32,7168]{1,0:T(8,128)(2,1)S(1)} %constant_dynamic-update-slice_fusion.refs_0_), channel_id=1, source_target_pairs={{0,1},{1,0},{2,3},{3,2},{4,5},{5,4},{6,7},{7,6},{8,9},{9,8},{10,11... | collective-permute-start | bytes 1376264 | tf_op jit(solution)/shard_map/ppermute | solution.py:38
  137.5 16.0 %collective-permute-start.22 = (bf16[32,7168]{1,0:T(8,128)(2,1)S(1)}, bf16[32,7168]{1,0:T(8,128)(2,1)S(1)}, u32[]{:S(2)}, u32[]{:S(2)}) collective-permute-start(bf16[32,7168]{1,0:T(8,128)(2,1)S(1)} %collective-permute-done.18.refs_1_), channel_id=1, source_target_pairs={{0,1},{1,0},{2,3},{3,2},{4,5},{5,4},{6,7},{7,6},{8,9},{9,8},{10,11... | collective-permute-start | bytes 1376264 | tf_op jit(solution)/shard_map/ppermute | solution.py:38
  145.1 8.3 %collective-permute-start.23 = (bf16[32,7168]{1,0:T(8,128)(2,1)S(1)}, bf16[32,7168]{1,0:T(8,128)(2,1)S(1)}, u32[]{:S(2)}, u32[]{:S(2)}) collective-permute-start(bf16[32,7168]{1,0:T(8,128)(2,1)S(1)} %collective-permute-done.19.refs_2_), channel_id=1, source_target_pairs={{0,1},{1,0},{2,3},{3,2},{4,5},{5,4},{6,7},{7,6},{8,9},{9,8},{10,11... | collective-permute-start | bytes 1376264 | tf_op jit(solution)/shard_map/ppermute | solution.py:38
  147.1 6.6 %collective-permute-start.24 = (bf16[32,7168]{1,0:T(8,128)(2,1)S(1)}, bf16[32,7168]{1,0:T(8,128)(2,1)S(1)}, u32[]{:S(2)}, u32[]{:S(2)}) collective-permute-start(bf16[32,7168]{1,0:T(8,128)(2,1)S(1)} %collective-permute-done.20.refs_3_), channel_id=1, source_target_pairs={{0,1},{1,0},{2,3},{3,2},{4,5},{5,4},{6,7},{7,6},{8,9},{9,8},{10,11... | collective-permute-start | bytes 1376264 | tf_op jit(solution)/shard_map/ppermute | solution.py:38
  (4 other events, 62.2 us)

commit v2 on v1

v2 whole, which is shorter than its diff:
```python
import functools

import jax
import jax.numpy as jnp
from jax import lax
from jax.experimental import pallas as pl
from jax.experimental.pallas import tpu as pltpu
from jax.sharding import PartitionSpec as P

noise_scale = 0.1
first_decay = 0.9
second_decay = 0.95
learn_rate = 0.2
weight_decay = 0.5
epsilon_adam = 1.0

FF = 14336
HALF = FF // 2
ROWS = 128
TOK = 128
NZ, NY = 4, 8
F32 = jnp.float32
BF16 = jnp.bfloat16


def index(z, y, c):
    return (z * NY + y) * 2 + c


def perm(target):
    return [
        (index(z, y, c), index(*target(z, y, c)))
        for z in range(NZ)
        for y in range(NY)
        for c in range(2)
    ]


def send(x, target):
    return lax.ppermute(x, "fsdp", perm(target))


def along_y(z, y, c, k):
    return (z, 2 * ((y // 2) ^ k) + y % 2, c)


def along_z(z, y, c, k):
    return (z ^ k, y, c)


def wide(k):
    return lambda z, y, c: along_y(z, y, c, k) if c == 0 else along_z(z, y, c, k)


MIDDLE = [[index(z, 2 * q + p, 0) for z in range(NZ) for p in range(2)] for q in range(4)] + [
    [index(z, y, 1) for y in range(NY)] for z in range(NZ)
]


def swap(x):
    return lax.all_to_all(x, "fsdp", 0, 0, axis_index_groups=MIDDLE, tiled=True)


def other_core(z, y, c):
    return (z, y, 1 - c)


def adamw(initial, gradient):
    first_moment = (1.0 - first_decay) * gradient
    second_moment = (1.0 - second_decay) * gradient * gradient
    update = (
        first_moment
        / (1.0 - first_decay)
        / (jnp.sqrt(second_moment / (1.0 - second_decay)) + epsilon_adam)
    )
    master = initial - learn_rate * (update + weight_decay * initial)
    return (master, first_moment, second_moment)


def cost(flops, nbytes):
    return pl.CostEstimate(flops=flops, bytes_accessed=nbytes, transcendentals=0)


def params(mib):
    return pltpu.CompilerParams(vmem_limit_bytes=mib << 20)


def shape(rows, dtype):
    return jax.ShapeDtypeStruct((rows, HALF), dtype)


VMEM = pl.BlockSpec(memory_space=pltpu.VMEM)
HBM = pl.BlockSpec(memory_space=pltpu.HBM)
SMEM = pl.BlockSpec(memory_space=pltpu.SMEM)
TILE = 896
FOLD = HALF // 2
FIRST = 60
FAR_FIRST = (2, 1, 3)


def in_slots(c, o, features):
    slot = lax.broadcasted_iota(jnp.int32, (ROWS, ROWS), 0)
    row = lax.broadcasted_iota(jnp.int32, (ROWS, ROWS), 1)
    a = (slot >> 5) ^ o
    b = (slot >> 3) & 3
    block = jnp.where(c == 0, b * 4 + a, a * 4 + b)
    pick = (block * 8 + (slot & 7) == row).astype(F32).astype(BF16)
    return lax.dot_general(
        pick, features, (((1,), (1,)), ((), ())), preferred_element_type=F32
    ).astype(BF16)


def product_kernel(far, place, features, grads, out, part, sem):
    c, o, t = place[0], place[1], place[2]
    core, first = (1 - c, t) if far else (c, o)
    copies = [
        pltpu.make_async_copy(
            grads.at[:, pl.ds(pl.multiple_of(core * HALF + n, 128), TILE)],
            part.at[:, pl.ds(n, TILE)],
            sem.at[n // TILE],
        )
        for n in range(0, HALF, TILE)
    ]
    for copy in copies:
        copy.start()
    left = in_slots(core, first, features[...])
    for i, copy in enumerate(copies):
        copy.wait()
        n = slice(i * TILE, (i + 1) * TILE)
        out[:, n] = jnp.dot(left, part[:, n], preferred_element_type=F32).astype(BF16)


def product(far, place, features, grads):
    return pl.pallas_call(
        functools.partial(product_kernel, far),
        in_specs=[SMEM, VMEM, HBM],
        out_specs=VMEM,
        out_shape=shape(ROWS, BF16),
        scratch_shapes=[pltpu.VMEM((TOK, HALF), BF16), pltpu.SemaphoreType.DMA((HALF // TILE,))],
        cost_estimate=cost(2 * ROWS * TOK * HALF, 4 * TOK * HALF),
        compiler_params=params(FIRST if far else 12),
    )(place, features, grads)


def chip_sum_kernel(near, far, own, s1, s2, s3):
    for k, s in ((0, own), (1, s1), (2, s2), (3, s3)):
        n = slice(32 * k, 32 * k + 32)
        s[...] = (near[n, :].astype(F32) + far[n, :].astype(F32)).astype(s.dtype)


def chip_sum(near, far):
    return pl.pallas_call(
        chip_sum_kernel,
        in_specs=[VMEM] * 2,
        out_specs=[VMEM] * 4,
        out_shape=[shape(32, F32)] + [shape(32, BF16)] * 3,
        cost_estimate=cost(ROWS * HALF, 6 * ROWS * HALF),
        compiler_params=params(12),
    )(near, far)


def first_sum_kernel(own, r1, r2, r3, total, out):
    for m in range(0, 32, 4):
        parts = []
        for h in range(2):
            n = (slice(m, m + 4), slice(h * FOLD, (h + 1) * FOLD))
            rest = r1[n].astype(F32) + r2[n].astype(F32) + r3[n].astype(F32)
            parts.append(own[n] + rest)
        value = jnp.concatenate(parts, 0)
        total[2 * m : 2 * m + 8, :] = value
        out[2 * m : 2 * m + 8, :] = value.astype(BF16)


def first_sum(own, parts):
    return pl.pallas_call(
        first_sum_kernel,
        in_specs=[VMEM] * 4,
        out_specs=[VMEM] * 2,
        out_shape=[jax.ShapeDtypeStruct((64, FOLD), d) for d in (F32, BF16)],
        cost_estimate=cost(4 * 32 * HALF, 12 * 32 * HALF),
        compiler_params=params(12),
    )(own, *parts)


def update_kernel(place, total, parts, mine, theirs, copy, keep, give):
    c = place[0]
    own = place[2] * 2 + place[3]
    gradient = total[pl.ds(pl.multiple_of(8 * own, 8), 8), :]
    for m in range(8):
        part = parts[8 * m : 8 * m + 8, :].astype(F32)
        gradient += jnp.where(own == m, 0.0, part)

    def folded(i):
        near, far = mine[i].astype(F32), theirs[i].astype(F32)
        low, high = jnp.where(c == 0, near, far), jnp.where(c == 0, far, near)
        rows = [x[:, h * FOLD : (h + 1) * FOLD] for h in range(2) for x in (low, high)]
        return jnp.concatenate(rows, 0)

    initial = folded(0) + noise_scale * folded(1)
    master = adamw(initial, gradient)[0].astype(BF16)
    for m in range(8):
        copy[8 * m : 8 * m + 8, :] = master
    for h in range(2):
        low, high = gradient[4 * h : 4 * h + 2], gradient[4 * h + 2 : 4 * h + 4]
        n = slice(h * FOLD, (h + 1) * FOLD)
        keep[:, n] = jnp.where(c == 0, low, high)
        give[:, n] = jnp.where(c == 0, high, low)


def update(place, total, parts, mine, theirs):
    return pl.pallas_call(
        update_kernel,
        in_specs=[SMEM] + [VMEM] * 4,
        out_specs=[VMEM] * 3,
        out_shape=[jax.ShapeDtypeStruct((64, FOLD), BF16), shape(2, F32), shape(2, F32)],
        cost_estimate=cost(20 * 8 * FOLD, 40 * 8 * FOLD),
        compiler_params=params(12),
    )(place, total, parts, mine, theirs)


def unfold_kernel(folded, out):
    for t in range(4):
        for h in range(2):
            n = 16 * t + 4 * h
            value = [folded[n + 8 * p : n + 8 * p + 4, :].astype(F32) for p in range(2)]
            out[8 * t : 8 * t + 8, h * FOLD : (h + 1) * FOLD] = jnp.concatenate(value, 0).astype(BF16)


def unfold(folded):
    return pl.pallas_call(
        unfold_kernel,
        in_specs=[VMEM],
        out_specs=VMEM,
        out_shape=shape(32, BF16),
        cost_estimate=cost(0, 4 * 32 * HALF),
        compiler_params=params(12),
    )(folded)


def assemble_kernel(place, *refs):
    blocks, out, sem = refs[:8], refs[8], refs[9]
    c, o, t = place[0], place[1], place[2]
    copies = []
    for half in range(2):
        for k in range(4):
            for j in range(4):
                if half == 0:
                    a, b, core = o ^ ((0,) + FAR_FIRST)[k], j, c
                else:
                    a, b, core = t ^ ((0,) + FAR_FIRST)[k], j, 1 - c
                block = jnp.where(core == 0, b * 4 + a, a * 4 + b)
                copies.append(
                    pltpu.make_async_copy(
                        blocks[half * 4 + k].at[pl.ds(8 * j, 8)],
                        out.at[
                            pl.ds(pl.multiple_of(block * 8, 8), 8),
                            pl.ds(pl.multiple_of(core * HALF, 128), HALF),
                        ],
                        sem.at[len(copies)],
                    )
                )
    for copy in copies:
        copy.start()
    for copy in copies:
        copy.wait()


def assemble(place, blocks):
    return pl.pallas_call(
        assemble_kernel,
        in_specs=[SMEM] + [pl.BlockSpec(memory_space=pl.ANY)] * 8,
        out_specs=HBM,
        out_shape=jax.ShapeDtypeStruct((ROWS, FF), BF16),
        scratch_shapes=[pltpu.SemaphoreType.DMA((32,))],
        cost_estimate=cost(0, 4 * ROWS * FF),
        compiler_params=params(12),
    )(place, *blocks)


def in_order(bit, mine, theirs, axis):
    lower = jnp.where(bit == 0, mine, theirs)
    upper = jnp.where(bit == 0, theirs, mine)
    return jnp.concatenate([lower, upper], axis)


def body(dense_rows, noise, features, out_grads):
    f, e = lax.axis_index("fsdp"), lax.axis_index("expert")
    c, y, z = f % 2, (f // 2) % NY, f // (2 * NY)
    q, p = y // 2, y % 2
    o, t = jnp.where(c == 0, q, z), jnp.where(c == 0, z, q)
    place = jnp.stack([c, o, t, p]).astype(jnp.int32)

    grads = out_grads[0]
    far = send(product(True, place, features[0], grads), other_core)
    near = product(False, place, features[0], grads)
    own, *chunks = chip_sum(near, far)
    got = [send(chunks[k - 1], wide(k)) for k in FAR_FIRST]
    total, rounded = first_sum(own, got)

    dense = lax.all_to_all(jnp.stack([dense_rows] * 8), "expert", 0, 0, tiled=True)
    dense = dense.swapaxes(0, 1).reshape(2, FF)
    both = jnp.stack([dense, noise[0]])
    mine = lax.dynamic_slice(both, (0, 0, c * HALF), (2, 2, HALF))
    theirs = send(lax.dynamic_slice(both, (0, 0, (1 - c) * HALF), (2, 2, HALF)), other_core)

    copy, keep, give = update(place, total, swap(rounded), mine, theirs)
    gathered = unfold(swap(copy))
    blocks = [gathered] + [send(gathered, wide(k)) for k in FAR_FIRST]
    blocks += [send(x, other_core) for x in blocks]
    expert_copy = assemble(place, blocks)

    gradient = in_order(c, keep, send(give, other_core), 1)
    initial = dense.astype(F32) + noise_scale * noise[0].astype(F32)
    master, first_moment, second_moment = adamw(initial, gradient)
    return (master[None], first_moment[None], second_moment[None], expert_copy[None])


def solution(mesh):
    return jax.shard_map(
        body,
        mesh=mesh,
        in_specs=(
            P("fsdp", "expert"),
            P("expert", "fsdp", None),
            P("expert", "fsdp", None),
            P("expert", "fsdp", None),
        ),
        out_specs=(
            P("expert", "fsdp", None),
            P("expert", "fsdp", None),
            P("expert", "fsdp", None),
            P("expert", None, None),
        ),
        check_vma=False,
    )
```

time: 158 us -> 126 us (0.80)
  starting transfers between devices: 105 us -> 62.8 us
  waiting for transfers between devices: 34.8 us -> 44.4 us
  Pallas kernels: 7.58 us -> 14.6 us
  local copies, waits for them, and re-layouts: 4.93 us -> 0.68 us
    ppermute x22 -> x13, starting transfers between devices: 91.7 us -> 47.6 us  [send(): return lax.ppermute(x, 'fsdp', perm(target))]
    all_to_all x0 -> x3, waiting for transfers between devices: none -> 21.3 us  [the longest x2 19.1 us: swap(): return lax.all_to_all(x, 'fsdp', 0, 0, axis_index_groups=MIDDLE, tiled=True)]
    all_to_all x0 -> x3, starting transfers between devices: none -> 15.2 us  [the longest x2 10.4 us: swap(): return lax.all_to_all(x, 'fsdp', 0, 0, axis_index_groups=MIDDLE, tiled=True)]
    ppermute x3 -> x0, starting transfers between devices: 13.2 us -> none  [body(): theirs = lax.ppermute(dense, 'expert', [(i, i ^ bit) for i in range(8)])]
    ppermute x22 -> x13, waiting for transfers between devices: 32.6 us -> 23.1 us  [send(): return lax.ppermute(x, 'fsdp', perm(target))]
    pallas_call x5 -> x7, Pallas kernels: 7.58 us -> 14.6 us  [the longest x2 7.96 us: product(): pl.pallas_call(functools.partial(product_kernel, far), in_specs=[SMEM, VM...]
    dynamic_slice x1 -> x0, local copies, waits for them, and re-layouts: 2.85 us -> none  [body(): lax.dynamic_slice(grads, (0, (1 - c) * HALF), (TOK, HALF))]
    ppermute x3 -> x0, waiting for transfers between devices: 2.29 us -> none  [body(): theirs = lax.ppermute(dense, 'expert', [(i, i ^ bit) for i in range(8)])]
  transfers between devices with their start and end apart: 25 -> 16, of which waited for: 10 -> 9; matrix products, arithmetic and copies ran while one was open for 3% -> 2% of each run, Pallas kernels for 0% -> 3%
where the time goes in v2:
time: 126 us; the launch traced here: 125 us
  starting transfers between devices  62.8 us (50%)
  waiting for transfers between devices  44.4 us (35%)
  Pallas kernels  14.6 us (12%)
  other arithmetic  1.9 us (2%)
    ppermute x13, starting transfers between devices, send(): return lax.ppermute(x, 'fsdp', perm(target))  47.6 us
    ppermute x13, waiting for transfers between devices, send(): return lax.ppermute(x, 'fsdp', perm(target))  23.1 us
    all_to_all x2, waiting for transfers between devices, swap(): return lax.all_to_all(x, 'fsdp', 0, 0, axis_index_groups=MIDDLE, tiled=True)  19.1 us
    all_to_all x2, starting transfers between devices, swap(): return lax.all_to_all(x, 'fsdp', 0, 0, axis_index_groups=MIDDLE, tiled=True)  10.4 us
    pallas_call x2, Pallas kernels, product(): pl.pallas_call(functools.partial(product_kernel, far), in_specs=[SMEM, VM...  7.96 us
    all_to_all x1, starting transfers between devices, body(): lax.all_to_all(jnp.stack([dense_rows] * 8), 'expert', 0, 0, tiled=True)  4.75 us
    pallas_call x1, Pallas kernels, assemble(): pl.pallas_call(assemble_kernel, in_specs=[SMEM] + [pl.BlockSpec(memory_sp...  2.64 us
  transfers between devices with their start and end apart: 16, of which 9 were waited for; matrix products, arithmetic and copies ran while one was open for 2% of the time, Pallas kernels for 3%

profile of v2, /device:TPU:1, one launch (start us, length us, event | category | flops | bytes accessed | tf_op | source)
XLA Modules:
  0.0 125.2 jit_solution(1676112555356155226)
XLA Ops:
  1.3 5.1 %shard_map.76 = bf16[128,7168]{1,0:T(8,128)(2,1)} custom-call(s32[4]{0:T(128)} %pad_add_fusion.place, bf16[128,128]{1,0:T(8,128)(2,1)} %bitcast.22, bf16[128,14336]{1,0:T(8,128)(2,1)} %bitcast.18), custom_call_target="tpu_custom_call" | custom-call | flops 234881024 | bytes 3670016 | tf_op jit(solution)/shard_map/pallas_call | solution.py:134
  6.4 8.8 %collective-permute-start = (bf16[128,7168]{1,0:T(8,128)(2,1)}, bf16[128,7168]{1,0:T(8,128)(2,1)S(1)}, u32[]{:S(2)}, u32[]{:S(2)}) collective-permute-start(bf16[128,7168]{1,0:T(8,128)(2,1)} %shard_map.76), channel_id=1, source_target_pairs={{0,1},{1,0},{2,3},{3,2},{4,5},{5,4},{6,7},{7,6},{8,9},{9,8},{10,11... | collective-permute-start | bytes 5505032 | tf_op jit(solution)/shard_map/ppermute | solution.py:40
  15.3 2.8 %shard_map.75.near = bf16[128,7168]{1,0:T(8,128)(2,1)S(1)} custom-call(s32[4]{0:T(128)S(1)} %copy-done.2, bf16[128,128]{1,0:T(8,128)(2,1)S(1)} %bitcast.23, bf16[128,14336]{1,0:T(8,128)(2,1)S(1)} %bitcast.19), custom_call_target="tpu_custom_call" | custom-call | flops 234881024 | bytes 3670016 | tf_op jit(solution)/shard_map/pallas_call | solution.py:134
  19.9 5.4 %collective-permute-start.1 = (bf16[32,7168]{1,0:T(8,128)(2,1)}, bf16[32,7168]{1,0:T(8,128)(2,1)S(1)}, u32[]{:S(2)}, u32[]{:S(2)}) collective-permute-start(bf16[32,7168]{1,0:T(8,128)(2,1)} %get-tuple-element.14), channel_id=1, source_target_pairs={{0,8},{1,33},{2,10},{3,35},{4,12},{5,37},{6,14},{7,39},{8,0},{9,41... | collective-permute-start | bytes 1376264 | tf_op jit(solution)/shard_map/ppermute | solution.py:40
  25.3 4.0 %collective-permute-start.2 = (bf16[32,7168]{1,0:T(8,128)(2,1)S(1)}, bf16[32,7168]{1,0:T(8,128)(2,1)S(1)}, u32[]{:S(2)}, u32[]{:S(2)}) collective-permute-start(bf16[32,7168]{1,0:T(8,128)(2,1)S(1)} %get-tuple-element.15), channel_id=1, source_target_pairs={{0,4},{1,17},{2,6},{3,19},{4,0},{5,21},{6,2},{7,23},{8,12},{9,25},... | collective-permute-start | bytes 1376264 | tf_op jit(solution)/shard_map/ppermute | solution.py:40
  29.4 2.1 %collective-permute-start.3 = (bf16[32,7168]{1,0:T(8,128)(2,1)S(1)}, bf16[32,7168]{1,0:T(8,128)(2,1)S(1)}, u32[]{:S(2)}, u32[]{:S(2)}) collective-permute-start(bf16[32,7168]{1,0:T(8,128)(2,1)S(1)} %get-tuple-element.16), channel_id=1, source_target_pairs={{0,12},{1,49},{2,14},{3,51},{4,8},{5,53},{6,10},{7,55},{8,4},{9,57... | collective-permute-start | bytes 1376264 | tf_op jit(solution)/shard_map/ppermute | solution.py:40
  32.1 4.7 %all-to-all-start = ((bf16[8,2,1792]{2,1,0:T(2,128)(2,1)}), bf16[8,2,1792]{2,1,0:T(2,128)(2,1)S(1)}, u32[]{:S(2)}, u32[]{:S(2)}) async-start(bf16[8,2,1792]{2,1,0:T(2,128)(2,1)} %stack.14), calls=%async_computation | async-start | bytes 114688 | tf_op jit(solution)/shard_map/all_to_all | solution.py:300
  36.9 10.1 %collective-permute-done.2.r2 = bf16[32,7168]{1,0:T(8,128)(2,1)S(1)} collective-permute-done((bf16[32,7168]{1,0:T(8,128)(2,1)S(1)}, bf16[32,7168]{1,0:T(8,128)(2,1)S(1)}, u32[]{:S(2)}, u32[]{:S(2)}) %collective-permute-start.2) | collective-permute-done | bytes 458784 | tf_op jit(solution)/shard_map/ppermute | solution.py:40
  48.1 2.1 %all-to-all-done = bf16[8,2,1792]{2,1,0:T(2,128)(2,1)S(1)} async-done(((bf16[8,2,1792]{2,1,0:T(2,128)(2,1)}), bf16[8,2,1792]{2,1,0:T(2,128)(2,1)S(1)}, u32[]{:S(2)}, u32[]{:S(2)}) %all-to-all-start) | async-done | bytes 57376 | tf_op jit(solution)/shard_map/all_to_all | solution.py:300
  50.3 6.8 %all-to-all-start.1 = ((bf16[8,8,3584]{2,1,0:T(8,128)(2,1)}), bf16[8,8,3584]{2,1,0:T(8,128)(2,1)S(1)}, u32[]{:S(2)}, u32[]{:S(2)}) async-start(bf16[8,8,3584]{2,1,0:T(8,128)(2,1)} %bitcast.8), calls=%async_computation.1 | async-start | bytes 917504 | tf_op jit(solution)/shard_map/all_to_all | solution.py:61
  57.2 1.9 %collective-permute-start.4 = (bf16[2,2,7168]{2,1,0:T(2,128)(2,1)S(1)}, bf16[2,2,7168]{2,1,0:T(2,128)(2,1)S(1)}, u32[]{:S(2)}, u32[]{:S(2)}) collective-permute-start(bf16[2,2,7168]{2,1,0:T(2,128)(2,1)S(1)} %get-tuple-element.27), channel_id=1, source_target_pairs={{0,1},{1,0},{2,3},{3,2},{4,5},{5,4},{6,7},{7,6},{8,9},{9,8},{10,11... | collective-permute-start | bytes 172040 | tf_op jit(solution)/shard_map/ppermute | solution.py:40
  60.4 8.5 %all-to-all-done.1 = bf16[8,8,3584]{2,1,0:T(8,128)(2,1)S(1)} async-done(((bf16[8,8,3584]{2,1,0:T(8,128)(2,1)}), bf16[8,8,3584]{2,1,0:T(8,128)(2,1)S(1)}, u32[]{:S(2)}, u32[]{:S(2)}) %all-to-all-start.1) | async-done | bytes 458784 | tf_op jit(solution)/shard_map/all_to_all | solution.py:61
  70.5 3.6 %all-to-all-start.2 = ((bf16[8,8,3584]{2,1,0:T(8,128)(2,1)}), bf16[8,8,3584]{2,1,0:T(8,128)(2,1)S(1)}, u32[]{:S(2)}, u32[]{:S(2)}) async-start(bf16[8,8,3584]{2,1,0:T(8,128)(2,1)} %bitcast.13), calls=%async_computation.2 | async-start | bytes 917504 | tf_op jit(solution)/shard_map/all_to_all | solution.py:61
  74.1 3.1 %collective-permute-start.5 = (f32[2,7168]{1,0:T(2,128)S(1)}, f32[2,7168]{1,0:T(2,128)S(1)}, u32[]{:S(2)}, u32[]{:S(2)}) collective-permute-start(f32[2,7168]{1,0:T(2,128)S(1)} %get-tuple-element.20), channel_id=1, source_target_pairs={{0,1},{1,0},{2,3},{3,2},{4,5},{5,4},{6,7},{7,6},{8,9},{9,8},{10,11... | collective-permute-start | bytes 172040 | tf_op jit(solution)/shard_map/ppermute | solution.py:40
  77.2 10.6 %all-to-all-done.2 = bf16[8,8,3584]{2,1,0:T(8,128)(2,1)S(1)} async-done(((bf16[8,8,3584]{2,1,0:T(8,128)(2,1)}), bf16[8,8,3584]{2,1,0:T(8,128)(2,1)S(1)}, u32[]{:S(2)}, u32[]{:S(2)}) %all-to-all-start.2) | async-done | bytes 458784 | tf_op jit(solution)/shard_map/all_to_all | solution.py:61
  87.9 6.8 %collective-permute-start.6 = (bf16[32,7168]{1,0:T(8,128)(2,1)S(1)}, bf16[32,7168]{1,0:T(8,128)(2,1)S(1)}, u32[]{:S(2)}, u32[]{:S(2)}) collective-permute-start(bf16[32,7168]{1,0:T(8,128)(2,1)S(1)} %shard_map.80.refs_0_), channel_id=1, source_target_pairs={{0,8},{1,33},{2,10},{3,35},{4,12},{5,37},{6,14},{7,39},{8,0},{9,41... | collective-permute-start | bytes 1376264 | tf_op jit(solution)/shard_map/ppermute | solution.py:40
  94.7 1.9 %collective-permute-start.7 = (bf16[32,7168]{1,0:T(8,128)(2,1)S(1)}, bf16[32,7168]{1,0:T(8,128)(2,1)S(1)}, u32[]{:S(2)}, u32[]{:S(2)}) collective-permute-start(bf16[32,7168]{1,0:T(8,128)(2,1)S(1)} %shard_map.80.refs_0_), channel_id=1, source_target_pairs={{0,4},{1,17},{2,6},{3,19},{4,0},{5,21},{6,2},{7,23},{8,12},{9,25},... | collective-permute-start | bytes 1376264 | tf_op jit(solution)/shard_map/ppermute | solution.py:40
  96.7 2.6 %collective-permute-start.8 = (bf16[32,7168]{1,0:T(8,128)(2,1)S(1)}, bf16[32,7168]{1,0:T(8,128)(2,1)S(1)}, u32[]{:S(2)}, u32[]{:S(2)}) collective-permute-start(bf16[32,7168]{1,0:T(8,128)(2,1)S(1)} %shard_map.80.refs_0_), channel_id=1, source_target_pairs={{0,12},{1,49},{2,14},{3,51},{4,8},{5,53},{6,10},{7,55},{8,4},{9,57... | collective-permute-start | bytes 1376264 | tf_op jit(solution)/shard_map/ppermute | solution.py:40
  99.4 3.0 %collective-permute-start.9 = (bf16[32,7168]{1,0:T(8,128)(2,1)S(1)}, bf16[32,7168]{1,0:T(8,128)(2,1)S(1)}, u32[]{:S(2)}, u32[]{:S(2)}) collective-permute-start(bf16[32,7168]{1,0:T(8,128)(2,1)S(1)} %shard_map.80.refs_0_), channel_id=1, source_target_pairs={{0,1},{1,0},{2,3},{3,2},{4,5},{5,4},{6,7},{7,6},{8,9},{9,8},{10,11... | collective-permute-start | bytes 1376264 | tf_op jit(solution)/shard_map/ppermute | solution.py:40
  102.4 4.0 %collective-permute-done.6.refs_1_ = bf16[32,7168]{1,0:T(8,128)(2,1)S(1)} collective-permute-done((bf16[32,7168]{1,0:T(8,128)(2,1)S(1)}, bf16[32,7168]{1,0:T(8,128)(2,1)S(1)}, u32[]{:S(2)}, u32[]{:S(2)}) %collective-permute-start.6) | collective-permute-done | bytes 458784 | tf_op jit(solution)/shard_map/ppermute | solution.py:40
  106.4 3.1 %collective-permute-start.10 = (bf16[32,7168]{1,0:T(8,128)(2,1)S(1)}, bf16[32,7168]{1,0:T(8,128)(2,1)S(1)}, u32[]{:S(2)}, u32[]{:S(2)}) collective-permute-start(bf16[32,7168]{1,0:T(8,128)(2,1)S(1)} %collective-permute-done.6.refs_1_), channel_id=1, source_target_pairs={{0,1},{1,0},{2,3},{3,2},{4,5},{5,4},{6,7},{7,6},{8,9},{9,8},{10,11... | collective-permute-start | bytes 1376264 | tf_op jit(solution)/shard_map/ppermute | solution.py:40
  109.4 6.5 %collective-permute-done.7.refs_2_ = bf16[32,7168]{1,0:T(8,128)(2,1)S(1)} collective-permute-done((bf16[32,7168]{1,0:T(8,128)(2,1)S(1)}, bf16[32,7168]{1,0:T(8,128)(2,1)S(1)}, u32[]{:S(2)}, u32[]{:S(2)}) %collective-permute-start.7) | collective-permute-done | bytes 458784 | tf_op jit(solution)/shard_map/ppermute | solution.py:40
  115.9 3.0 %collective-permute-start.11 = (bf16[32,7168]{1,0:T(8,128)(2,1)S(1)}, bf16[32,7168]{1,0:T(8,128)(2,1)S(1)}, u32[]{:S(2)}, u32[]{:S(2)}) collective-permute-start(bf16[32,7168]{1,0:T(8,128)(2,1)S(1)} %collective-permute-done.7.refs_2_), channel_id=1, source_target_pairs={{0,1},{1,0},{2,3},{3,2},{4,5},{5,4},{6,7},{7,6},{8,9},{9,8},{10,11... | collective-permute-start | bytes 1376264 | tf_op jit(solution)/shard_map/ppermute | solution.py:40
  122.6 2.6 %shard_map.81 = bf16[128,14336]{1,0:T(8,128)(2,1)} custom-call(s32[4]{0:T(128)S(1)} %copy-done.2, bf16[32,7168]{1,0:T(8,128)(2,1)S(1)} %shard_map.80.refs_0_, bf16[32,7168]{1,0:T(8,128)(2,1)S(1)} %collective-permute-done.6.refs_1_, bf16[32,7168]{1,0:T(8,128)(2,1)S(1)} %collective-permute-done.7.refs_2_, bf16[32,7168]{1,0:T(8,128)(2,1)S(1)} %collective-permute-done.8.refs_3_, ...), custom_call_target="tpu_custom_call" | custom-call | bytes 7340032 | tf_op jit(solution)/shard_map/pallas_call | solution.py:269
  (30 shorter events, 11.1 us)
Async XLA Ops:
  1.3 13.9 %copy-start = (bf16[1,128,14336]{2,1,0:T(8,128)(2,1)S(1)}, bf16[1,128,14336]{2,1,0:T(8,128)(2,1)}, u32[]{:S(2)}) copy-start(bf16[1,128,14336]{2,1,0:T(8,128)(2,1)} %param.7) | copy-start | bytes 11010052
  1.3 13.9 %copy-start.1 = (bf16[1,128,128]{2,1,0:T(8,128)(2,1)S(1)}, bf16[1,128,128]{2,1,0:T(8,128)(2,1)}, u32[]{:S(2)}) copy-start(bf16[1,128,128]{2,1,0:T(8,128)(2,1)} %param.6) | copy-start | bytes 98308
  1.3 13.9 %copy-start.2 = (s32[4]{0:T(128)S(1)}, s32[4]{0:T(128)}, u32[]{:S(2)}) copy-start(s32[4]{0:T(128)} %pad_add_fusion.place) | copy-start | bytes 52
  6.4 12.4 %collective-permute-start = (bf16[128,7168]{1,0:T(8,128)(2,1)}, bf16[128,7168]{1,0:T(8,128)(2,1)S(1)}, u32[]{:S(2)}, u32[]{:S(2)}) collective-permute-start(bf16[128,7168]{1,0:T(8,128)(2,1)} %shard_map.76), channel_id=1, source_target_pairs={{0,1},{1,0},{2,3},{3,2},{4,5},{5,4},{6,7},{7,6},{8,9},{9,8},{10,11... | collective-permute-start | bytes 5505032 | tf_op jit(solution)/shard_map/ppermute | solution.py:40
  18.1 13.3 %copy-start.4 = (bf16[2,1792]{1,0:T(2,128)(2,1)S(1)}, bf16[2,1792]{1,0:T(2,128)(2,1)}, u32[]{:S(2)}) copy-start(bf16[2,1792]{1,0:T(2,128)(2,1)} %param.4) | copy-start | bytes 21508
  19.9 37.2 %copy-start.3 = (bf16[1,2,14336]{2,1,0:T(2,128)(2,1)S(1)}, bf16[1,2,14336]{2,1,0:T(2,128)(2,1)}, u32[]{:S(2)}) copy-start(bf16[1,2,14336]{2,1,0:T(2,128)(2,1)} %param.5) | copy-start | bytes 172036
  19.9 16.9 %collective-permute-start.1 = (bf16[32,7168]{1,0:T(8,128)(2,1)}, bf16[32,7168]{1,0:T(8,128)(2,1)S(1)}, u32[]{:S(2)}, u32[]{:S(2)}) collective-permute-start(bf16[32,7168]{1,0:T(8,128)(2,1)} %get-tuple-element.14), channel_id=1, source_target_pairs={{0,8},{1,33},{2,10},{3,35},{4,12},{5,37},{6,14},{7,39},{8,0},{9,41... | collective-permute-start | bytes 1376264 | tf_op jit(solution)/shard_map/ppermute | solution.py:40
  25.3 21.6 %collective-permute-start.2 = (bf16[32,7168]{1,0:T(8,128)(2,1)S(1)}, bf16[32,7168]{1,0:T(8,128)(2,1)S(1)}, u32[]{:S(2)}, u32[]{:S(2)}) collective-permute-start(bf16[32,7168]{1,0:T(8,128)(2,1)S(1)} %get-tuple-element.15), channel_id=1, source_target_pairs={{0,4},{1,17},{2,6},{3,19},{4,0},{5,21},{6,2},{7,23},{8,12},{9,25},... | collective-permute-start | bytes 1376264 | tf_op jit(solution)/shard_map/ppermute | solution.py:40
  29.4 17.6 %collective-permute-start.3 = (bf16[32,7168]{1,0:T(8,128)(2,1)S(1)}, bf16[32,7168]{1,0:T(8,128)(2,1)S(1)}, u32[]{:S(2)}, u32[]{:S(2)}) collective-permute-start(bf16[32,7168]{1,0:T(8,128)(2,1)S(1)} %get-tuple-element.16), channel_id=1, source_target_pairs={{0,12},{1,49},{2,14},{3,51},{4,8},{5,53},{6,10},{7,55},{8,4},{9,57... | collective-permute-start | bytes 1376264 | tf_op jit(solution)/shard_map/ppermute | solution.py:40
  32.1 18.2 %all-to-all-start = ((bf16[8,2,1792]{2,1,0:T(2,128)(2,1)}), bf16[8,2,1792]{2,1,0:T(2,128)(2,1)S(1)}, u32[]{:S(2)}, u32[]{:S(2)}) async-start(bf16[8,2,1792]{2,1,0:T(2,128)(2,1)} %stack.14), calls=%async_computation | async-start | bytes 114688 | tf_op jit(solution)/shard_map/all_to_all | solution.py:300
  50.3 18.6 %all-to-all-start.1 = ((bf16[8,8,3584]{2,1,0:T(8,128)(2,1)}), bf16[8,8,3584]{2,1,0:T(8,128)(2,1)S(1)}, u32[]{:S(2)}, u32[]{:S(2)}) async-start(bf16[8,8,3584]{2,1,0:T(8,128)(2,1)} %bitcast.8), calls=%async_computation.1 | async-start | bytes 917504 | tf_op jit(solution)/shard_map/all_to_all | solution.py:61
  57.2 3.1 %collective-permute-start.4 = (bf16[2,2,7168]{2,1,0:T(2,128)(2,1)S(1)}, bf16[2,2,7168]{2,1,0:T(2,128)(2,1)S(1)}, u32[]{:S(2)}, u32[]{:S(2)}) collective-permute-start(bf16[2,2,7168]{2,1,0:T(2,128)(2,1)S(1)} %get-tuple-element.27), channel_id=1, source_target_pairs={{0,1},{1,0},{2,3},{3,2},{4,5},{5,4},{6,7},{7,6},{8,9},{9,8},{10,11... | collective-permute-start | bytes 172040 | tf_op jit(solution)/shard_map/ppermute | solution.py:40
  70.5 17.3 %all-to-all-start.2 = ((bf16[8,8,3584]{2,1,0:T(8,128)(2,1)}), bf16[8,8,3584]{2,1,0:T(8,128)(2,1)S(1)}, u32[]{:S(2)}, u32[]{:S(2)}) async-start(bf16[8,8,3584]{2,1,0:T(8,128)(2,1)} %bitcast.13), calls=%async_computation.2 | async-start | bytes 917504 | tf_op jit(solution)/shard_map/all_to_all | solution.py:61
  74.1 25.2 %collective-permute-start.5 = (f32[2,7168]{1,0:T(2,128)S(1)}, f32[2,7168]{1,0:T(2,128)S(1)}, u32[]{:S(2)}, u32[]{:S(2)}) collective-permute-start(f32[2,7168]{1,0:T(2,128)S(1)} %get-tuple-element.20), channel_id=1, source_target_pairs={{0,1},{1,0},{2,3},{3,2},{4,5},{5,4},{6,7},{7,6},{8,9},{9,8},{10,11... | collective-permute-start | bytes 172040 | tf_op jit(solution)/shard_map/ppermute | solution.py:40
  87.9 18.4 %collective-permute-start.6 = (bf16[32,7168]{1,0:T(8,128)(2,1)S(1)}, bf16[32,7168]{1,0:T(8,128)(2,1)S(1)}, u32[]{:S(2)}, u32[]{:S(2)}) collective-permute-start(bf16[32,7168]{1,0:T(8,128)(2,1)S(1)} %shard_map.80.refs_0_), channel_id=1, source_target_pairs={{0,8},{1,33},{2,10},{3,35},{4,12},{5,37},{6,14},{7,39},{8,0},{9,41... | collective-permute-start | bytes 1376264 | tf_op jit(solution)/shard_map/ppermute | solution.py:40
  94.7 21.1 %collective-permute-start.7 = (bf16[32,7168]{1,0:T(8,128)(2,1)S(1)}, bf16[32,7168]{1,0:T(8,128)(2,1)S(1)}, u32[]{:S(2)}, u32[]{:S(2)}) collective-permute-start(bf16[32,7168]{1,0:T(8,128)(2,1)S(1)} %shard_map.80.refs_0_), channel_id=1, source_target_pairs={{0,4},{1,17},{2,6},{3,19},{4,0},{5,21},{6,2},{7,23},{8,12},{9,25},... | collective-permute-start | bytes 1376264 | tf_op jit(solution)/shard_map/ppermute | solution.py:40
  96.7 22.2 %collective-permute-start.8 = (bf16[32,7168]{1,0:T(8,128)(2,1)S(1)}, bf16[32,7168]{1,0:T(8,128)(2,1)S(1)}, u32[]{:S(2)}, u32[]{:S(2)}) collective-permute-start(bf16[32,7168]{1,0:T(8,128)(2,1)S(1)} %shard_map.80.refs_0_), channel_id=1, source_target_pairs={{0,12},{1,49},{2,14},{3,51},{4,8},{5,53},{6,10},{7,55},{8,4},{9,57... | collective-permute-start | bytes 1376264 | tf_op jit(solution)/shard_map/ppermute | solution.py:40
  99.4 22.5 %collective-permute-start.9 = (bf16[32,7168]{1,0:T(8,128)(2,1)S(1)}, bf16[32,7168]{1,0:T(8,128)(2,1)S(1)}, u32[]{:S(2)}, u32[]{:S(2)}) collective-permute-start(bf16[32,7168]{1,0:T(8,128)(2,1)S(1)} %shard_map.80.refs_0_), channel_id=1, source_target_pairs={{0,1},{1,0},{2,3},{3,2},{4,5},{5,4},{6,7},{7,6},{8,9},{9,8},{10,11... | collective-permute-start | bytes 1376264 | tf_op jit(solution)/shard_map/ppermute | solution.py:40
  106.4 15.6 %collective-permute-start.10 = (bf16[32,7168]{1,0:T(8,128)(2,1)S(1)}, bf16[32,7168]{1,0:T(8,128)(2,1)S(1)}, u32[]{:S(2)}, u32[]{:S(2)}) collective-permute-start(bf16[32,7168]{1,0:T(8,128)(2,1)S(1)} %collective-permute-done.6.refs_1_), channel_id=1, source_target_pairs={{0,1},{1,0},{2,3},{3,2},{4,5},{5,4},{6,7},{7,6},{8,9},{9,8},{10,11... | collective-permute-start | bytes 1376264 | tf_op jit(solution)/shard_map/ppermute | solution.py:40
  115.9 6.0 %collective-permute-start.11 = (bf16[32,7168]{1,0:T(8,128)(2,1)S(1)}, bf16[32,7168]{1,0:T(8,128)(2,1)S(1)}, u32[]{:S(2)}, u32[]{:S(2)}) collective-permute-start(bf16[32,7168]{1,0:T(8,128)(2,1)S(1)} %collective-permute-done.7.refs_2_), channel_id=1, source_target_pairs={{0,1},{1,0},{2,3},{3,2},{4,5},{5,4},{6,7},{7,6},{8,9},{9,8},{10,11... | collective-permute-start | bytes 1376264 | tf_op jit(solution)/shard_map/ppermute | solution.py:40
  118.9 3.7 %collective-permute-start.12 = (bf16[32,7168]{1,0:T(8,128)(2,1)S(1)}, bf16[32,7168]{1,0:T(8,128)(2,1)S(1)}, u32[]{:S(2)}, u32[]{:S(2)}) collective-permute-start(bf16[32,7168]{1,0:T(8,128)(2,1)S(1)} %collective-permute-done.8.refs_3_), channel_id=1, source_target_pairs={{0,1},{1,0},{2,3},{3,2},{4,5},{5,4},{6,7},{7,6},{8,9},{9,8},{10,11... | collective-permute-start | bytes 1376264 | tf_op jit(solution)/shard_map/ppermute | solution.py:40

commit v3 on v2

--- a/solution.py
+++ b/solution.py
@@ -77,6 +77,12 @@
     return (master, first_moment, second_moment)
 
 
+def place():
+    f = lax.axis_index("fsdp")
+    c, q, z = f & 1, (f >> 2) & 3, f >> 4
+    return c, jnp.where(c == 0, q, z), jnp.where(c == 0, z, q)
+
+
 def cost(flops, nbytes):
     return pl.CostEstimate(flops=flops, bytes_accessed=nbytes, transcendentals=0)
 
@@ -91,11 +97,8 @@
 
 VMEM = pl.BlockSpec(memory_space=pltpu.VMEM)
 HBM = pl.BlockSpec(memory_space=pltpu.HBM)
-SMEM = pl.BlockSpec(memory_space=pltpu.SMEM)
 TILE = 896
 FOLD = HALF // 2
-FIRST = 60
-FAR_FIRST = (2, 1, 3)
 
 
 def in_slots(c, o, features):
@@ -110,36 +113,78 @@
     ).astype(BF16)
 
 
-def product_kernel(far, place, features, grads, out, part, sem):
-    c, o, t = place[0], place[1], place[2]
-    core, first = (1 - c, t) if far else (c, o)
-    copies = [
+def tiles(source, column, target, sem):
+    return [
         pltpu.make_async_copy(
-            grads.at[:, pl.ds(pl.multiple_of(core * HALF + n, 128), TILE)],
-            part.at[:, pl.ds(n, TILE)],
+            source.at[:, pl.ds(pl.multiple_of(column + n, 128), TILE)],
+            target.at[:, pl.ds(n, TILE)],
             sem.at[n // TILE],
         )
         for n in range(0, HALF, TILE)
     ]
+
+
+def far_product_kernel(features, grads, out, local, part, value, sem, out_sem):
+    c, _, t = place()
+    core = 1 - c
+    first = pltpu.make_async_copy(features, local, sem.at[HALF // TILE])
+    first.start()
+    copies = tiles(grads, core * HALF, part, sem)
     for copy in copies:
         copy.start()
-    left = in_slots(core, first, features[...])
+    first.wait()
+    left = in_slots(core, t, local[...])
+    results = tiles(value, 0, out, out_sem)
+    for i, (copy, result) in enumerate(zip(copies, results)):
+        copy.wait()
+        n = slice(i * TILE, (i + 1) * TILE)
+        value[:, n] = jnp.dot(left, part[:, n], preferred_element_type=F32).astype(BF16)
+        result.start()
+    for result in results:
+        result.wait()
+
+
+def far_product(features, grads):
+    count = HALF // TILE
+    return pl.pallas_call(
+        far_product_kernel,
+        in_specs=[HBM, HBM],
+        out_specs=HBM,
+        out_shape=shape(ROWS, BF16),
+        scratch_shapes=[
+            pltpu.VMEM((TOK, ROWS), BF16),
+            pltpu.VMEM((TOK, HALF), BF16),
+            pltpu.VMEM((ROWS, HALF), BF16),
+            pltpu.SemaphoreType.DMA((count + 1,)),
+            pltpu.SemaphoreType.DMA((count,)),
+        ],
+        cost_estimate=cost(2 * ROWS * TOK * HALF, 4 * TOK * HALF),
+        compiler_params=params(60),
+    )(features, grads)
+
+
+def near_product_kernel(features, grads, out, part, sem):
+    c, o, _ = place()
+    copies = tiles(grads, c * HALF, part, sem)
+    for copy in copies:
+        copy.start()
+    left = in_slots(c, o, features[...])
     for i, copy in enumerate(copies):
         copy.wait()
         n = slice(i * TILE, (i + 1) * TILE)
         out[:, n] = jnp.dot(left, part[:, n], preferred_element_type=F32).astype(BF16)
 
 
-def product(far, place, features, grads):
-    return pl.pallas_call(
-        functools.partial(product_kernel, far),
-        in_specs=[SMEM, VMEM, HBM],
+def near_product(features, grads):
+    return pl.pallas_call(
+        near_product_kernel,
+        in_specs=[VMEM, HBM],
         out_specs=VMEM,
         out_shape=shape(ROWS, BF16),
         scratch_shapes=[pltpu.VMEM((TOK, HALF), BF16), pltpu.SemaphoreType.DMA((HALF // TILE,))],
         cost_estimate=cost(2 * ROWS * TOK * HALF, 4 * TOK * HALF),
-        compiler_params=params(FIRST if far else 12),
-    )(place, features, grads)
+        compiler_params=params(12),
+    )(features, grads)
 
 
 def chip_sum_kernel(near, far, own, s1, s2, s3):
@@ -182,9 +227,9 @@
     )(own, *parts)
 
 
-def update_kernel(place, total, parts, mine, theirs, copy, keep, give):
-    c = place[0]
-    own = place[2] * 2 + place[3]
+def update_kernel(total, parts, mine, theirs, copy, keep, give):
+    c, _, t = place()
+    own = t * 2 + ((lax.axis_index("fsdp") >> 1) & 1)
     gradient = total[pl.ds(pl.multiple_of(8 * own, 8), 8), :]
     for m in range(8):
         part = parts[8 * m : 8 * m + 8, :].astype(F32)
@@ -207,15 +252,15 @@
         give[:, n] = jnp.where(c == 0, high, low)
 
 
-def update(place, total, parts, mine, theirs):
+def update(total, parts, mine, theirs):
     return pl.pallas_call(
         update_kernel,
-        in_specs=[SMEM] + [VMEM] * 4,
+        in_specs=[VMEM] * 4,
         out_specs=[VMEM] * 3,
         out_shape=[jax.ShapeDtypeStruct((64, FOLD), BF16), shape(2, F32), shape(2, F32)],
         cost_estimate=cost(20 * 8 * FOLD, 40 * 8 * FOLD),
         compiler_params=params(12),
-    )(place, total, parts, mine, theirs)
+    )(total, parts, mine, theirs)
 
 
 def unfold_kernel(folded, out):
@@ -237,44 +282,43 @@
     )(folded)
 
 
-def assemble_kernel(place, *refs):
-    blocks, out, sem = refs[:8], refs[8], refs[9]
-    c, o, t = place[0], place[1], place[2]
+def assemble_kernel(pieces, *refs):
+    c, o, t = place()
+    blocks, out, sem = refs[: len(pieces)], refs[-2], refs[-1]
     copies = []
-    for half in range(2):
-        for k in range(4):
-            for j in range(4):
-                if half == 0:
-                    a, b, core = o ^ ((0,) + FAR_FIRST)[k], j, c
-                else:
-                    a, b, core = t ^ ((0,) + FAR_FIRST)[k], j, 1 - c
-                block = jnp.where(core == 0, b * 4 + a, a * 4 + b)
-                copies.append(
-                    pltpu.make_async_copy(
-                        blocks[half * 4 + k].at[pl.ds(8 * j, 8)],
-                        out.at[
-                            pl.ds(pl.multiple_of(block * 8, 8), 8),
-                            pl.ds(pl.multiple_of(core * HALF, 128), HALF),
-                        ],
-                        sem.at[len(copies)],
-                    )
+    for block, (half, k) in zip(blocks, pieces):
+        core, a = (c, o ^ k) if half == 0 else (1 - c, t ^ k)
+        for j in range(4):
+            row = jnp.where(core == 0, j * 4 + a, a * 4 + j) * 8
+            copies.append(
+                pltpu.make_async_copy(
+                    block.at[pl.ds(8 * j, 8)],
+                    out.at[
+                        pl.ds(pl.multiple_of(row, 8), 8),
+                        pl.ds(pl.multiple_of(core * HALF, 128), HALF),
+                    ],
+                    sem.at[len(copies)],
                 )
+            )
     for copy in copies:
         copy.start()
     for copy in copies:
         copy.wait()
 
 
-def assemble(place, blocks):
-    return pl.pallas_call(
-        assemble_kernel,
-        in_specs=[SMEM] + [pl.BlockSpec(memory_space=pl.ANY)] * 8,
+def assemble(pieces, blocks, result=None):
+    operands = list(blocks) if result is None else list(blocks) + [result]
+    return pl.pallas_call(
+        functools.partial(assemble_kernel, pieces),
+        in_specs=[pl.BlockSpec(memory_space=pl.ANY)] * len(blocks)
+        + [HBM] * (len(operands) - len(blocks)),
         out_specs=HBM,
         out_shape=jax.ShapeDtypeStruct((ROWS, FF), BF16),
-        scratch_shapes=[pltpu.SemaphoreType.DMA((32,))],
-        cost_estimate=cost(0, 4 * ROWS * FF),
-        compiler_params=params(12),
-    )(place, *blocks)
+        scratch_shapes=[pltpu.SemaphoreType.DMA((4 * len(pieces),))],
+        input_output_aliases={} if result is None else {len(blocks): 0},
+        cost_estimate=cost(0, len(pieces) * ROWS * HALF),
+        compiler_params=params(12),
+    )(*operands)
 
 
 def in_order(bit, mine, theirs, axis):
@@ -284,17 +328,13 @@
 
 
 def body(dense_rows, noise, features, out_grads):
-    f, e = lax.axis_index("fsdp"), lax.axis_index("expert")
-    c, y, z = f % 2, (f // 2) % NY, f // (2 * NY)
-    q, p = y // 2, y % 2
-    o, t = jnp.where(c == 0, q, z), jnp.where(c == 0, z, q)
-    place = jnp.stack([c, o, t, p]).astype(jnp.int32)
+    c = lax.axis_index("fsdp") & 1
 
     grads = out_grads[0]
-    far = send(product(True, place, features[0], grads), other_core)
-    near = product(False, place, features[0], grads)
+    far = send(far_product(features[0], grads), other_core)
+    near = near_product(features[0], grads)
     own, *chunks = chip_sum(near, far)
-    got = [send(chunks[k - 1], wide(k)) for k in FAR_FIRST]
+    got = [send(chunks[k - 1], wide(k)) for k in (2, 1, 3)]
     total, rounded = first_sum(own, got)
 
     dense = lax.all_to_all(jnp.stack([dense_rows] * 8), "expert", 0, 0, tiled=True)
@@ -303,11 +343,13 @@
     mine = lax.dynamic_slice(both, (0, 0, c * HALF), (2, 2, HALF))
     theirs = send(lax.dynamic_slice(both, (0, 0, (1 - c) * HALF), (2, 2, HALF)), other_core)
 
-    copy, keep, give = update(place, total, swap(rounded), mine, theirs)
-    gathered = unfold(swap(copy))
-    blocks = [gathered] + [send(gathered, wide(k)) for k in FAR_FIRST]
-    blocks += [send(x, other_core) for x in blocks]
-    expert_copy = assemble(place, blocks)
+    copy, keep, give = update(total, swap(rounded), mine, theirs)
+    own = unfold(swap(copy))
+    r1, r3, r2 = (send(own, wide(k)) for k in (1, 3, 2))
+    x0, x1, x3, x2 = (send(x, other_core) for x in (own, r1, r3, r2))
+    early = assemble(((0, 0), (0, 1), (1, 0), (1, 1)), (own, r1, x0, x1))
+    expert_copy = assemble(((0, 2), (0, 3), (1, 2), (1, 3)), (r2, r3, x2, x3), early)
+    give, _ = lax.optimization_barrier((give, r1))
 
     gradient = in_order(c, keep, send(give, other_core), 1)
     initial = dense.astype(F32) + noise_scale * noise[0].astype(F32)

time: 126 us -> 121 us (0.960)
  blocking collectives: 0 us -> 17.1 us
  waiting for transfers between devices: 44.4 us -> 31.4 us
  starting transfers between devices: 62.8 us -> 57 us
  Pallas kernels: 14.6 us -> 11.4 us
    all_to_all x0 -> x1, blocking collectives: none -> 17.1 us  [swap(): return lax.all_to_all(x, 'fsdp', 0, 0, axis_index_groups=MIDDLE, tiled=True)]
    all_to_all x2 -> x1, waiting for transfers between devices: 19.1 us -> 8.53 us  [swap(): return lax.all_to_all(x, 'fsdp', 0, 0, axis_index_groups=MIDDLE, tiled=True)]
    all_to_all x2 -> x1, starting transfers between devices: 10.4 us -> 6.82 us  [swap(): return lax.all_to_all(x, 'fsdp', 0, 0, axis_index_groups=MIDDLE, tiled=True)]
    pallas_call x4 -> x5, Pallas kernels: 12.2 us -> 9.01 us  [the longest x1 3.69 us: far_product(): pl.pallas_call(far_product_kernel, in_specs=[HBM, HBM], out_specs=HBM, ou...]
    ppermute x13, waiting for transfers between devices: 23.1 us -> 20.8 us  [send(): return lax.ppermute(x, 'fsdp', perm(target))]
    ppermute x13, starting transfers between devices: 47.6 us -> 45.5 us  [send(): return lax.ppermute(x, 'fsdp', perm(target))]
  transfers between devices with their start and end apart: 16 -> 15, of which waited for: 9 -> 7; matrix products, arithmetic and copies ran while one was open for 2% -> 2% of each run, Pallas kernels for 3% -> 4%
where the time goes in v3:
time: 121 us; the launch traced here: 120 us
  starting transfers between devices  57 us (47%)
  waiting for transfers between devices  31.4 us (26%)
  blocking collectives  17.1 us (14%)
  Pallas kernels  11.4 us (9%)
  other arithmetic  1.29 us (1%)
    ppermute x13, starting transfers between devices, send(): return lax.ppermute(x, 'fsdp', perm(target))  45.5 us
    ppermute x13, waiting for transfers between devices, send(): return lax.ppermute(x, 'fsdp', perm(target))  20.8 us
    all_to_all x1, blocking collectives, swap(): return lax.all_to_all(x, 'fsdp', 0, 0, axis_index_groups=MIDDLE, tiled=True)  17.1 us
    all_to_all x1, waiting for transfers between devices, swap(): return lax.all_to_all(x, 'fsdp', 0, 0, axis_index_groups=MIDDLE, tiled=True)  8.53 us
    all_to_all x1, starting transfers between devices, swap(): return lax.all_to_all(x, 'fsdp', 0, 0, axis_index_groups=MIDDLE, tiled=True)  6.82 us
    all_to_all x1, starting transfers between devices, body(): lax.all_to_all(jnp.stack([dense_rows] * 8), 'expert', 0, 0, tiled=True)  4.74 us
    pallas_call x1, Pallas kernels, far_product(): pl.pallas_call(far_product_kernel, in_specs=[HBM, HBM], out_specs=HBM, ou...  3.69 us
    pallas_call x2, Pallas kernels, assemble(): pl.pallas_call(functools.partial(assemble_kernel, pieces), in_specs=[pl.B...  2.72 us
  transfers between devices with their start and end apart: 15, of which 7 were waited for; matrix products, arithmetic and copies ran while one was open for 2% of the time, Pallas kernels for 4%

profile of v3, /device:TPU:1, one launch (start us, length us, event | category | flops | bytes accessed | tf_op | source)
XLA Modules:
  0.0 119.8 jit_solution(10210473267437415692)
XLA Ops:
  0.7 3.7 %shard_map.76 = bf16[128,7168]{1,0:T(8,128)(2,1)} custom-call(bf16[128,128]{1,0:T(8,128)(2,1)} %bitcast.19, bf16[128,14336]{1,0:T(8,128)(2,1)} %bitcast.14), custom_call_target="tpu_custom_call" | custom-call | flops 234881024 | bytes 3670016 | tf_op jit(solution)/shard_map/pallas_call | solution.py:149
  4.4 8.8 %collective-permute-start = (bf16[128,7168]{1,0:T(8,128)(2,1)}, bf16[128,7168]{1,0:T(8,128)(2,1)S(1)}, u32[]{:S(2)}, u32[]{:S(2)}) collective-permute-start(bf16[128,7168]{1,0:T(8,128)(2,1)} %shard_map.76), channel_id=1, source_target_pairs={{0,1},{1,0},{2,3},{3,2},{4,5},{5,4},{6,7},{7,6},{8,9},{9,8},{10,11... | collective-permute-start | bytes 5505032 | tf_op jit(solution)/shard_map/ppermute | solution.py:40
  13.2 2.3 %shard_map.75.near = bf16[128,7168]{1,0:T(8,128)(2,1)S(1)} custom-call(bf16[128,128]{1,0:T(8,128)(2,1)S(1)} %bitcast.20, bf16[128,14336]{1,0:T(8,128)(2,1)S(1)} %bitcast.15), custom_call_target="tpu_custom_call" | custom-call | flops 234881024 | bytes 3670016 | tf_op jit(solution)/shard_map/pallas_call | solution.py:179
  17.9 5.2 %collective-permute-start.1 = (bf16[32,7168]{1,0:T(8,128)(2,1)}, bf16[32,7168]{1,0:T(8,128)(2,1)S(1)}, u32[]{:S(2)}, u32[]{:S(2)}) collective-permute-start(bf16[32,7168]{1,0:T(8,128)(2,1)} %get-tuple-element.15), channel_id=1, source_target_pairs={{0,8},{1,33},{2,10},{3,35},{4,12},{5,37},{6,14},{7,39},{8,0},{9,41... | collective-permute-start | bytes 1376264 | tf_op jit(solution)/shard_map/ppermute | solution.py:40
  23.1 4.0 %collective-permute-start.2 = (bf16[32,7168]{1,0:T(8,128)(2,1)S(1)}, bf16[32,7168]{1,0:T(8,128)(2,1)S(1)}, u32[]{:S(2)}, u32[]{:S(2)}) collective-permute-start(bf16[32,7168]{1,0:T(8,128)(2,1)S(1)} %get-tuple-element.16), channel_id=1, source_target_pairs={{0,4},{1,17},{2,6},{3,19},{4,0},{5,21},{6,2},{7,23},{8,12},{9,25},... | collective-permute-start | bytes 1376264 | tf_op jit(solution)/shard_map/ppermute | solution.py:40
  27.1 2.1 %collective-permute-start.3 = (bf16[32,7168]{1,0:T(8,128)(2,1)S(1)}, bf16[32,7168]{1,0:T(8,128)(2,1)S(1)}, u32[]{:S(2)}, u32[]{:S(2)}) collective-permute-start(bf16[32,7168]{1,0:T(8,128)(2,1)S(1)} %get-tuple-element.17), channel_id=1, source_target_pairs={{0,12},{1,49},{2,14},{3,51},{4,8},{5,53},{6,10},{7,55},{8,4},{9,57... | collective-permute-start | bytes 1376264 | tf_op jit(solution)/shard_map/ppermute | solution.py:40
  29.9 4.7 %all-to-all-start = ((bf16[8,2,1792]{2,1,0:T(2,128)(2,1)}), bf16[8,2,1792]{2,1,0:T(2,128)(2,1)S(1)}, u32[]{:S(2)}, u32[]{:S(2)}) async-start(bf16[8,2,1792]{2,1,0:T(2,128)(2,1)} %stack.4), calls=%async_computation | async-start | bytes 114688 | tf_op jit(solution)/shard_map/all_to_all | solution.py:340
  34.7 10.1 %collective-permute-done.2.r2 = bf16[32,7168]{1,0:T(8,128)(2,1)S(1)} collective-permute-done((bf16[32,7168]{1,0:T(8,128)(2,1)S(1)}, bf16[32,7168]{1,0:T(8,128)(2,1)S(1)}, u32[]{:S(2)}, u32[]{:S(2)}) %collective-permute-start.2) | collective-permute-done | bytes 458784 | tf_op jit(solution)/shard_map/ppermute | solution.py:40
  45.9 2.1 %all-to-all-done = bf16[8,2,1792]{2,1,0:T(2,128)(2,1)S(1)} async-done(((bf16[8,2,1792]{2,1,0:T(2,128)(2,1)}), bf16[8,2,1792]{2,1,0:T(2,128)(2,1)S(1)}, u32[]{:S(2)}, u32[]{:S(2)}) %all-to-all-start) | async-done | bytes 57376 | tf_op jit(solution)/shard_map/all_to_all | solution.py:340
  48.1 6.8 %all-to-all-start.1 = ((bf16[8,8,3584]{2,1,0:T(8,128)(2,1)}), bf16[8,8,3584]{2,1,0:T(8,128)(2,1)S(1)}, u32[]{:S(2)}, u32[]{:S(2)}) async-start(bf16[8,8,3584]{2,1,0:T(8,128)(2,1)} %bitcast.4), calls=%async_computation.1 | async-start | bytes 917504 | tf_op jit(solution)/shard_map/all_to_all | solution.py:61
  55.0 1.9 %collective-permute-start.4 = (bf16[2,2,7168]{2,1,0:T(2,128)(2,1)S(1)}, bf16[2,2,7168]{2,1,0:T(2,128)(2,1)S(1)}, u32[]{:S(2)}, u32[]{:S(2)}) collective-permute-start(bf16[2,2,7168]{2,1,0:T(2,128)(2,1)S(1)} %get-tuple-element.29), channel_id=1, source_target_pairs={{0,1},{1,0},{2,3},{3,2},{4,5},{5,4},{6,7},{7,6},{8,9},{9,8},{10,11... | collective-permute-start | bytes 172040 | tf_op jit(solution)/shard_map/ppermute | solution.py:40
  58.1 8.5 %all-to-all-done.1 = bf16[8,8,3584]{2,1,0:T(8,128)(2,1)S(1)} async-done(((bf16[8,8,3584]{2,1,0:T(8,128)(2,1)}), bf16[8,8,3584]{2,1,0:T(8,128)(2,1)S(1)}, u32[]{:S(2)}, u32[]{:S(2)}) %all-to-all-start.1) | async-done | bytes 458784 | tf_op jit(solution)/shard_map/all_to_all | solution.py:61
  67.0 17.1 %all_to_all.27 = bf16[8,8,3584]{2,1,0:T(8,128)(2,1)S(1)} all-to-all(bf16[8,8,3584]{2,1,0:T(8,128)(2,1)S(1)} %bitcast.18), channel_id=1, replica_groups={{0,2,16,18,32,34,48,50},{4,6,20,22,36,38,52,54},{8,10,24,26,40,42,56,58..., dimensions={0} | all-to-all | bytes 917504 | tf_op jit(solution)/shard_map/all_to_all | solution.py:61
  84.2 2.7 %collective-permute-start.5 = (bf16[32,7168]{1,0:T(8,128)(2,1)S(1)}, bf16[32,7168]{1,0:T(8,128)(2,1)S(1)}, u32[]{:S(2)}, u32[]{:S(2)}) collective-permute-start(bf16[32,7168]{1,0:T(8,128)(2,1)S(1)} %shard_map.80.refs_0_), channel_id=1, source_target_pairs={{0,4},{1,17},{2,6},{3,19},{4,0},{5,21},{6,2},{7,23},{8,12},{9,25},... | collective-permute-start | bytes 1376264 | tf_op jit(solution)/shard_map/ppermute | solution.py:40
  86.9 4.7 %collective-permute-start.8 = (bf16[32,7168]{1,0:T(8,128)(2,1)S(1)}, bf16[32,7168]{1,0:T(8,128)(2,1)S(1)}, u32[]{:S(2)}, u32[]{:S(2)}) collective-permute-start(bf16[32,7168]{1,0:T(8,128)(2,1)S(1)} %shard_map.80.refs_0_), channel_id=1, source_target_pairs={{0,12},{1,49},{2,14},{3,51},{4,8},{5,53},{6,10},{7,55},{8,4},{9,57... | collective-permute-start | bytes 1376264 | tf_op jit(solution)/shard_map/ppermute | solution.py:40
  91.6 3.9 %collective-permute-start.7 = (bf16[32,7168]{1,0:T(8,128)(2,1)S(1)}, bf16[32,7168]{1,0:T(8,128)(2,1)S(1)}, u32[]{:S(2)}, u32[]{:S(2)}) collective-permute-start(bf16[32,7168]{1,0:T(8,128)(2,1)S(1)} %shard_map.80.refs_0_), channel_id=1, source_target_pairs={{0,8},{1,33},{2,10},{3,35},{4,12},{5,37},{6,14},{7,39},{8,0},{9,41... | collective-permute-start | bytes 1376264 | tf_op jit(solution)/shard_map/ppermute | solution.py:40
  95.6 3.3 %collective-permute-done.5.refs_1_ = bf16[32,7168]{1,0:T(8,128)(2,1)S(1)} collective-permute-done((bf16[32,7168]{1,0:T(8,128)(2,1)S(1)}, bf16[32,7168]{1,0:T(8,128)(2,1)S(1)}, u32[]{:S(2)}, u32[]{:S(2)}) %collective-permute-start.5) | collective-permute-done | bytes 458784 | tf_op jit(solution)/shard_map/ppermute | solution.py:40
  98.9 3.4 %collective-permute-start.6 = (f32[2,7168]{1,0:T(2,128)S(1)}, f32[2,7168]{1,0:T(2,128)S(1)}, u32[]{:S(2)}, u32[]{:S(2)}) collective-permute-start(f32[2,7168]{1,0:T(2,128)S(1)} %get-tuple-element.23), channel_id=1, source_target_pairs={{0,1},{1,0},{2,3},{3,2},{4,5},{5,4},{6,7},{7,6},{8,9},{9,8},{10,11... | collective-permute-start | bytes 172040 | tf_op jit(solution)/shard_map/ppermute | solution.py:40
  102.3 1.9 %collective-permute-start.11 = (bf16[32,7168]{1,0:T(8,128)(2,1)S(1)}, bf16[32,7168]{1,0:T(8,128)(2,1)S(1)}, u32[]{:S(2)}, u32[]{:S(2)}) collective-permute-start(bf16[32,7168]{1,0:T(8,128)(2,1)S(1)} %shard_map.80.refs_0_), channel_id=1, source_target_pairs={{0,1},{1,0},{2,3},{3,2},{4,5},{5,4},{6,7},{7,6},{8,9},{9,8},{10,11... | collective-permute-start | bytes 1376264 | tf_op jit(solution)/shard_map/ppermute | solution.py:40
  104.2 2.4 %collective-permute-start.12 = (bf16[32,7168]{1,0:T(8,128)(2,1)S(1)}, bf16[32,7168]{1,0:T(8,128)(2,1)S(1)}, u32[]{:S(2)}, u32[]{:S(2)}) collective-permute-start(bf16[32,7168]{1,0:T(8,128)(2,1)S(1)} %collective-permute-done.5.refs_1_), channel_id=1, source_target_pairs={{0,1},{1,0},{2,3},{3,2},{4,5},{5,4},{6,7},{7,6},{8,9},{9,8},{10,11... | collective-permute-start | bytes 1376264 | tf_op jit(solution)/shard_map/ppermute | solution.py:40
  106.7 4.9 %collective-permute-done.8.refs_1_ = bf16[32,7168]{1,0:T(8,128)(2,1)S(1)} collective-permute-done((bf16[32,7168]{1,0:T(8,128)(2,1)S(1)}, bf16[32,7168]{1,0:T(8,128)(2,1)S(1)}, u32[]{:S(2)}, u32[]{:S(2)}) %collective-permute-start.8) | collective-permute-done | bytes 458784 | tf_op jit(solution)/shard_map/ppermute | solution.py:40
  111.5 1.9 %collective-permute-start.10 = (bf16[32,7168]{1,0:T(8,128)(2,1)S(1)}, bf16[32,7168]{1,0:T(8,128)(2,1)S(1)}, u32[]{:S(2)}, u32[]{:S(2)}) collective-permute-start(bf16[32,7168]{1,0:T(8,128)(2,1)S(1)} %collective-permute-done.8.refs_1_), channel_id=1, source_target_pairs={{0,1},{1,0},{2,3},{3,2},{4,5},{5,4},{6,7},{7,6},{8,9},{9,8},{10,11... | collective-permute-start | bytes 1376264 | tf_op jit(solution)/shard_map/ppermute | solution.py:40
  113.5 2.4 %collective-permute-start.9 = (bf16[32,7168]{1,0:T(8,128)(2,1)S(1)}, bf16[32,7168]{1,0:T(8,128)(2,1)S(1)}, u32[]{:S(2)}, u32[]{:S(2)}) collective-permute-start(bf16[32,7168]{1,0:T(8,128)(2,1)S(1)} %collective-permute-done.7.refs_0_), channel_id=1, source_target_pairs={{0,1},{1,0},{2,3},{3,2},{4,5},{5,4},{6,7},{7,6},{8,9},{9,8},{10,11... | collective-permute-start | bytes 1376264 | tf_op jit(solution)/shard_map/ppermute | solution.py:40
  118.5 1.4 %shard_map.82 = bf16[128,14336]{1,0:T(8,128)(2,1)} custom-call(bf16[32,7168]{1,0:T(8,128)(2,1)S(1)} %collective-permute-done.7.refs_0_, bf16[32,7168]{1,0:T(8,128)(2,1)S(1)} %collective-permute-done.8.refs_1_, bf16[32,7168]{1,0:T(8,128)(2,1)S(1)} %collective-permute-done.9.refs_2_, ...), custom_call_target="tpu_custom_call", output_to_operand_aliasing={{}: (4, {})} | custom-call | bytes 3670016 | tf_op jit(solution)/shard_map/pallas_call | solution.py:311
  (27 shorter events, 8.5 us)
Async XLA Ops:
  0.6 12.5 %copy-start = (bf16[1,128,14336]{2,1,0:T(8,128)(2,1)S(1)}, bf16[1,128,14336]{2,1,0:T(8,128)(2,1)}, u32[]{:S(2)}) copy-start(bf16[1,128,14336]{2,1,0:T(8,128)(2,1)} %param.7) | copy-start | bytes 11010052
  0.6 12.5 %copy-start.1 = (bf16[1,128,128]{2,1,0:T(8,128)(2,1)S(1)}, bf16[1,128,128]{2,1,0:T(8,128)(2,1)}, u32[]{:S(2)}) copy-start(bf16[1,128,128]{2,1,0:T(8,128)(2,1)} %param.6) | copy-start | bytes 98308
  4.3 24.9 %copy-start.3 = (bf16[2,1792]{1,0:T(2,128)(2,1)S(1)}, bf16[2,1792]{1,0:T(2,128)(2,1)}, u32[]{:S(2)}) copy-start(bf16[2,1792]{1,0:T(2,128)(2,1)} %param.4) | copy-start | bytes 21508
  4.4 12.4 %collective-permute-start = (bf16[128,7168]{1,0:T(8,128)(2,1)}, bf16[128,7168]{1,0:T(8,128)(2,1)S(1)}, u32[]{:S(2)}, u32[]{:S(2)}) collective-permute-start(bf16[128,7168]{1,0:T(8,128)(2,1)} %shard_map.76), channel_id=1, source_target_pairs={{0,1},{1,0},{2,3},{3,2},{4,5},{5,4},{6,7},{7,6},{8,9},{9,8},{10,11... | collective-permute-start | bytes 5505032 | tf_op jit(solution)/shard_map/ppermute | solution.py:40
  15.5 39.4 %copy-start.2 = (bf16[1,2,14336]{2,1,0:T(2,128)(2,1)S(1)}, bf16[1,2,14336]{2,1,0:T(2,128)(2,1)}, u32[]{:S(2)}) copy-start(bf16[1,2,14336]{2,1,0:T(2,128)(2,1)} %param.5) | copy-start | bytes 172036
  17.9 16.8 %collective-permute-start.1 = (bf16[32,7168]{1,0:T(8,128)(2,1)}, bf16[32,7168]{1,0:T(8,128)(2,1)S(1)}, u32[]{:S(2)}, u32[]{:S(2)}) collective-permute-start(bf16[32,7168]{1,0:T(8,128)(2,1)} %get-tuple-element.15), channel_id=1, source_target_pairs={{0,8},{1,33},{2,10},{3,35},{4,12},{5,37},{6,14},{7,39},{8,0},{9,41... | collective-permute-start | bytes 1376264 | tf_op jit(solution)/shard_map/ppermute | solution.py:40
  23.1 21.6 %collective-permute-start.2 = (bf16[32,7168]{1,0:T(8,128)(2,1)S(1)}, bf16[32,7168]{1,0:T(8,128)(2,1)S(1)}, u32[]{:S(2)}, u32[]{:S(2)}) collective-permute-start(bf16[32,7168]{1,0:T(8,128)(2,1)S(1)} %get-tuple-element.16), channel_id=1, source_target_pairs={{0,4},{1,17},{2,6},{3,19},{4,0},{5,21},{6,2},{7,23},{8,12},{9,25},... | collective-permute-start | bytes 1376264 | tf_op jit(solution)/shard_map/ppermute | solution.py:40
  27.1 17.6 %collective-permute-start.3 = (bf16[32,7168]{1,0:T(8,128)(2,1)S(1)}, bf16[32,7168]{1,0:T(8,128)(2,1)S(1)}, u32[]{:S(2)}, u32[]{:S(2)}) collective-permute-start(bf16[32,7168]{1,0:T(8,128)(2,1)S(1)} %get-tuple-element.17), channel_id=1, source_target_pairs={{0,12},{1,49},{2,14},{3,51},{4,8},{5,53},{6,10},{7,55},{8,4},{9,57... | collective-permute-start | bytes 1376264 | tf_op jit(solution)/shard_map/ppermute | solution.py:40
  29.9 18.2 %all-to-all-start = ((bf16[8,2,1792]{2,1,0:T(2,128)(2,1)}), bf16[8,2,1792]{2,1,0:T(2,128)(2,1)S(1)}, u32[]{:S(2)}, u32[]{:S(2)}) async-start(bf16[8,2,1792]{2,1,0:T(2,128)(2,1)} %stack.4), calls=%async_computation | async-start | bytes 114688 | tf_op jit(solution)/shard_map/all_to_all | solution.py:340
  48.1 18.6 %all-to-all-start.1 = ((bf16[8,8,3584]{2,1,0:T(8,128)(2,1)}), bf16[8,8,3584]{2,1,0:T(8,128)(2,1)S(1)}, u32[]{:S(2)}, u32[]{:S(2)}) async-start(bf16[8,8,3584]{2,1,0:T(8,128)(2,1)} %bitcast.4), calls=%async_computation.1 | async-start | bytes 917504 | tf_op jit(solution)/shard_map/all_to_all | solution.py:61
  55.0 3.1 %collective-permute-start.4 = (bf16[2,2,7168]{2,1,0:T(2,128)(2,1)S(1)}, bf16[2,2,7168]{2,1,0:T(2,128)(2,1)S(1)}, u32[]{:S(2)}, u32[]{:S(2)}) collective-permute-start(bf16[2,2,7168]{2,1,0:T(2,128)(2,1)S(1)} %get-tuple-element.29), channel_id=1, source_target_pairs={{0,1},{1,0},{2,3},{3,2},{4,5},{5,4},{6,7},{7,6},{8,9},{9,8},{10,11... | collective-permute-start | bytes 172040 | tf_op jit(solution)/shard_map/ppermute | solution.py:40
  84.2 14.8 %collective-permute-start.5 = (bf16[32,7168]{1,0:T(8,128)(2,1)S(1)}, bf16[32,7168]{1,0:T(8,128)(2,1)S(1)}, u32[]{:S(2)}, u32[]{:S(2)}) collective-permute-start(bf16[32,7168]{1,0:T(8,128)(2,1)S(1)} %shard_map.80.refs_0_), channel_id=1, source_target_pairs={{0,4},{1,17},{2,6},{3,19},{4,0},{5,21},{6,2},{7,23},{8,12},{9,25},... | collective-permute-start | bytes 1376264 | tf_op jit(solution)/shard_map/ppermute | solution.py:40
  86.9 24.7 %collective-permute-start.8 = (bf16[32,7168]{1,0:T(8,128)(2,1)S(1)}, bf16[32,7168]{1,0:T(8,128)(2,1)S(1)}, u32[]{:S(2)}, u32[]{:S(2)}) collective-permute-start(bf16[32,7168]{1,0:T(8,128)(2,1)S(1)} %shard_map.80.refs_0_), channel_id=1, source_target_pairs={{0,12},{1,49},{2,14},{3,51},{4,8},{5,53},{6,10},{7,55},{8,4},{9,57... | collective-permute-start | bytes 1376264 | tf_op jit(solution)/shard_map/ppermute | solution.py:40
  91.6 21.8 %collective-permute-start.7 = (bf16[32,7168]{1,0:T(8,128)(2,1)S(1)}, bf16[32,7168]{1,0:T(8,128)(2,1)S(1)}, u32[]{:S(2)}, u32[]{:S(2)}) collective-permute-start(bf16[32,7168]{1,0:T(8,128)(2,1)S(1)} %shard_map.80.refs_0_), channel_id=1, source_target_pairs={{0,8},{1,33},{2,10},{3,35},{4,12},{5,37},{6,14},{7,39},{8,0},{9,41... | collective-permute-start | bytes 1376264 | tf_op jit(solution)/shard_map/ppermute | solution.py:40
  98.9 17.0 %collective-permute-start.6 = (f32[2,7168]{1,0:T(2,128)S(1)}, f32[2,7168]{1,0:T(2,128)S(1)}, u32[]{:S(2)}, u32[]{:S(2)}) collective-permute-start(f32[2,7168]{1,0:T(2,128)S(1)} %get-tuple-element.23), channel_id=1, source_target_pairs={{0,1},{1,0},{2,3},{3,2},{4,5},{5,4},{6,7},{7,6},{8,9},{9,8},{10,11... | collective-permute-start | bytes 172040 | tf_op jit(solution)/shard_map/ppermute | solution.py:40
  102.3 14.8 %collective-permute-start.11 = (bf16[32,7168]{1,0:T(8,128)(2,1)S(1)}, bf16[32,7168]{1,0:T(8,128)(2,1)S(1)}, u32[]{:S(2)}, u32[]{:S(2)}) collective-permute-start(bf16[32,7168]{1,0:T(8,128)(2,1)S(1)} %shard_map.80.refs_0_), channel_id=1, source_target_pairs={{0,1},{1,0},{2,3},{3,2},{4,5},{5,4},{6,7},{7,6},{8,9},{9,8},{10,11... | collective-permute-start | bytes 1376264 | tf_op jit(solution)/shard_map/ppermute | solution.py:40
  104.2 12.8 %collective-permute-start.12 = (bf16[32,7168]{1,0:T(8,128)(2,1)S(1)}, bf16[32,7168]{1,0:T(8,128)(2,1)S(1)}, u32[]{:S(2)}, u32[]{:S(2)}) collective-permute-start(bf16[32,7168]{1,0:T(8,128)(2,1)S(1)} %collective-permute-done.5.refs_1_), channel_id=1, source_target_pairs={{0,1},{1,0},{2,3},{3,2},{4,5},{5,4},{6,7},{7,6},{8,9},{9,8},{10,11... | collective-permute-start | bytes 1376264 | tf_op jit(solution)/shard_map/ppermute | solution.py:40
  111.5 6.9 %collective-permute-start.10 = (bf16[32,7168]{1,0:T(8,128)(2,1)S(1)}, bf16[32,7168]{1,0:T(8,128)(2,1)S(1)}, u32[]{:S(2)}, u32[]{:S(2)}) collective-permute-start(bf16[32,7168]{1,0:T(8,128)(2,1)S(1)} %collective-permute-done.8.refs_1_), channel_id=1, source_target_pairs={{0,1},{1,0},{2,3},{3,2},{4,5},{5,4},{6,7},{7,6},{8,9},{9,8},{10,11... | collective-permute-start | bytes 1376264 | tf_op jit(solution)/shard_map/ppermute | solution.py:40
  113.5 5.0 %collective-permute-start.9 = (bf16[32,7168]{1,0:T(8,128)(2,1)S(1)}, bf16[32,7168]{1,0:T(8,128)(2,1)S(1)}, u32[]{:S(2)}, u32[]{:S(2)}) collective-permute-start(bf16[32,7168]{1,0:T(8,128)(2,1)S(1)} %collective-permute-done.7.refs_0_), channel_id=1, source_target_pairs={{0,1},{1,0},{2,3},{3,2},{4,5},{5,4},{6,7},{7,6},{8,9},{9,8},{10,11... | collective-permute-start | bytes 1376264 | tf_op jit(solution)/shard_map/ppermute | solution.py:40

commit v4 on v3

--- a/solution.py
+++ b/solution.py
@@ -97,7 +97,7 @@
 
 VMEM = pl.BlockSpec(memory_space=pltpu.VMEM)
 HBM = pl.BlockSpec(memory_space=pltpu.HBM)
-TILE = 896
+TILE = 3584
 FOLD = HALF // 2
 
 

time: 121 us -> 121 us (level)
  Pallas kernels: 11.4 us -> 9.7 us
  transfers between devices with their start and end apart: 15 -> 15, of which waited for: 7 -> 7; matrix products, arithmetic and copies ran while one was open for 2% -> 2% of each run, Pallas kernels for 4% -> 3%
where the time goes in v4:
time: 121 us; the launch traced here: 119 us
  starting transfers between devices  57 us (47%)
  waiting for transfers between devices  32.6 us (27%)
  blocking collectives  17.1 us (14%)
  Pallas kernels  9.7 us (8%)
  other arithmetic  1.29 us (1%)
    ppermute x13, starting transfers between devices, send(): return lax.ppermute(x, 'fsdp', perm(target))  45.5 us
    ppermute x13, waiting for transfers between devices, send(): return lax.ppermute(x, 'fsdp', perm(target))  21.9 us
    all_to_all x1, blocking collectives, swap(): return lax.all_to_all(x, 'fsdp', 0, 0, axis_index_groups=MIDDLE, tiled=True)  17.1 us
    all_to_all x1, waiting for transfers between devices, swap(): return lax.all_to_all(x, 'fsdp', 0, 0, axis_index_groups=MIDDLE, tiled=True)  8.53 us
    all_to_all x1, starting transfers between devices, swap(): return lax.all_to_all(x, 'fsdp', 0, 0, axis_index_groups=MIDDLE, tiled=True)  6.82 us
    all_to_all x1, starting transfers between devices, body(): lax.all_to_all(jnp.stack([dense_rows] * 8), 'expert', 0, 0, tiled=True)  4.74 us
    pallas_call x1, Pallas kernels, far_product(): pl.pallas_call(far_product_kernel, in_specs=[HBM, HBM], out_specs=HBM, ou...  3.11 us
    pallas_call x2, Pallas kernels, assemble(): pl.pallas_call(functools.partial(assemble_kernel, pieces), in_specs=[pl.B...  2.72 us
  transfers between devices with their start and end apart: 15, of which 7 were waited for; matrix products, arithmetic and copies ran while one was open for 2% of the time, Pallas kernels for 3%

profile of v4, /device:TPU:1, one launch (start us, length us, event | category | flops | bytes accessed | tf_op | source)
XLA Modules:
  0.0 119.3 jit_solution(12299756338499252167)
XLA Ops:
  0.7 3.1 %shard_map.76 = bf16[128,7168]{1,0:T(8,128)(2,1)} custom-call(bf16[128,128]{1,0:T(8,128)(2,1)} %bitcast.19, bf16[128,14336]{1,0:T(8,128)(2,1)} %bitcast.14), custom_call_target="tpu_custom_call" | custom-call | flops 234881024 | bytes 3670016 | tf_op jit(solution)/shard_map/pallas_call | solution.py:149
  3.8 8.8 %collective-permute-start = (bf16[128,7168]{1,0:T(8,128)(2,1)}, bf16[128,7168]{1,0:T(8,128)(2,1)S(1)}, u32[]{:S(2)}, u32[]{:S(2)}) collective-permute-start(bf16[128,7168]{1,0:T(8,128)(2,1)} %shard_map.76), channel_id=1, source_target_pairs={{0,1},{1,0},{2,3},{3,2},{4,5},{5,4},{6,7},{7,6},{8,9},{9,8},{10,11... | collective-permute-start | bytes 5505032 | tf_op jit(solution)/shard_map/ppermute | solution.py:40
  13.8 2.4 %collective-permute-done.far = bf16[128,7168]{1,0:T(8,128)(2,1)S(1)} collective-permute-done((bf16[128,7168]{1,0:T(8,128)(2,1)}, bf16[128,7168]{1,0:T(8,128)(2,1)S(1)}, u32[]{:S(2)}, u32[]{:S(2)}) %collective-permute-start) | collective-permute-done | bytes 1835040 | tf_op jit(solution)/shard_map/ppermute | solution.py:40
  17.3 5.2 %collective-permute-start.1 = (bf16[32,7168]{1,0:T(8,128)(2,1)}, bf16[32,7168]{1,0:T(8,128)(2,1)S(1)}, u32[]{:S(2)}, u32[]{:S(2)}) collective-permute-start(bf16[32,7168]{1,0:T(8,128)(2,1)} %get-tuple-element.15), channel_id=1, source_target_pairs={{0,8},{1,33},{2,10},{3,35},{4,12},{5,37},{6,14},{7,39},{8,0},{9,41... | collective-permute-start | bytes 1376264 | tf_op jit(solution)/shard_map/ppermute | solution.py:40
  22.5 4.0 %collective-permute-start.2 = (bf16[32,7168]{1,0:T(8,128)(2,1)S(1)}, bf16[32,7168]{1,0:T(8,128)(2,1)S(1)}, u32[]{:S(2)}, u32[]{:S(2)}) collective-permute-start(bf16[32,7168]{1,0:T(8,128)(2,1)S(1)} %get-tuple-element.16), channel_id=1, source_target_pairs={{0,4},{1,17},{2,6},{3,19},{4,0},{5,21},{6,2},{7,23},{8,12},{9,25},... | collective-permute-start | bytes 1376264 | tf_op jit(solution)/shard_map/ppermute | solution.py:40
  26.6 2.1 %collective-permute-start.3 = (bf16[32,7168]{1,0:T(8,128)(2,1)S(1)}, bf16[32,7168]{1,0:T(8,128)(2,1)S(1)}, u32[]{:S(2)}, u32[]{:S(2)}) collective-permute-start(bf16[32,7168]{1,0:T(8,128)(2,1)S(1)} %get-tuple-element.17), channel_id=1, source_target_pairs={{0,12},{1,49},{2,14},{3,51},{4,8},{5,53},{6,10},{7,55},{8,4},{9,57... | collective-permute-start | bytes 1376264 | tf_op jit(solution)/shard_map/ppermute | solution.py:40
  29.3 4.7 %all-to-all-start = ((bf16[8,2,1792]{2,1,0:T(2,128)(2,1)}), bf16[8,2,1792]{2,1,0:T(2,128)(2,1)S(1)}, u32[]{:S(2)}, u32[]{:S(2)}) async-start(bf16[8,2,1792]{2,1,0:T(2,128)(2,1)} %stack.4), calls=%async_computation | async-start | bytes 114688 | tf_op jit(solution)/shard_map/all_to_all | solution.py:340
  34.1 10.1 %collective-permute-done.2.r2 = bf16[32,7168]{1,0:T(8,128)(2,1)S(1)} collective-permute-done((bf16[32,7168]{1,0:T(8,128)(2,1)S(1)}, bf16[32,7168]{1,0:T(8,128)(2,1)S(1)}, u32[]{:S(2)}, u32[]{:S(2)}) %collective-permute-start.2) | collective-permute-done | bytes 458784 | tf_op jit(solution)/shard_map/ppermute | solution.py:40
  45.4 2.1 %all-to-all-done = bf16[8,2,1792]{2,1,0:T(2,128)(2,1)S(1)} async-done(((bf16[8,2,1792]{2,1,0:T(2,128)(2,1)}), bf16[8,2,1792]{2,1,0:T(2,128)(2,1)S(1)}, u32[]{:S(2)}, u32[]{:S(2)}) %all-to-all-start) | async-done | bytes 57376 | tf_op jit(solution)/shard_map/all_to_all | solution.py:340
  47.5 6.8 %all-to-all-start.1 = ((bf16[8,8,3584]{2,1,0:T(8,128)(2,1)}), bf16[8,8,3584]{2,1,0:T(8,128)(2,1)S(1)}, u32[]{:S(2)}, u32[]{:S(2)}) async-start(bf16[8,8,3584]{2,1,0:T(8,128)(2,1)} %bitcast.4), calls=%async_computation.1 | async-start | bytes 917504 | tf_op jit(solution)/shard_map/all_to_all | solution.py:61
  54.4 1.9 %collective-permute-start.4 = (bf16[2,2,7168]{2,1,0:T(2,128)(2,1)S(1)}, bf16[2,2,7168]{2,1,0:T(2,128)(2,1)S(1)}, u32[]{:S(2)}, u32[]{:S(2)}) collective-permute-start(bf16[2,2,7168]{2,1,0:T(2,128)(2,1)S(1)} %get-tuple-element.29), channel_id=1, source_target_pairs={{0,1},{1,0},{2,3},{3,2},{4,5},{5,4},{6,7},{7,6},{8,9},{9,8},{10,11... | collective-permute-start | bytes 172040 | tf_op jit(solution)/shard_map/ppermute | solution.py:40
  57.6 8.5 %all-to-all-done.1 = bf16[8,8,3584]{2,1,0:T(8,128)(2,1)S(1)} async-done(((bf16[8,8,3584]{2,1,0:T(8,128)(2,1)}), bf16[8,8,3584]{2,1,0:T(8,128)(2,1)S(1)}, u32[]{:S(2)}, u32[]{:S(2)}) %all-to-all-start.1) | async-done | bytes 458784 | tf_op jit(solution)/shard_map/all_to_all | solution.py:61
  66.4 17.1 %all_to_all.27 = bf16[8,8,3584]{2,1,0:T(8,128)(2,1)S(1)} all-to-all(bf16[8,8,3584]{2,1,0:T(8,128)(2,1)S(1)} %bitcast.18), channel_id=1, replica_groups={{0,2,16,18,32,34,48,50},{4,6,20,22,36,38,52,54},{8,10,24,26,40,42,56,58..., dimensions={0} | all-to-all | bytes 917504 | tf_op jit(solution)/shard_map/all_to_all | solution.py:61
  83.6 2.7 %collective-permute-start.5 = (bf16[32,7168]{1,0:T(8,128)(2,1)S(1)}, bf16[32,7168]{1,0:T(8,128)(2,1)S(1)}, u32[]{:S(2)}, u32[]{:S(2)}) collective-permute-start(bf16[32,7168]{1,0:T(8,128)(2,1)S(1)} %shard_map.80.refs_0_), channel_id=1, source_target_pairs={{0,4},{1,17},{2,6},{3,19},{4,0},{5,21},{6,2},{7,23},{8,12},{9,25},... | collective-permute-start | bytes 1376264 | tf_op jit(solution)/shard_map/ppermute | solution.py:40
  86.3 4.7 %collective-permute-start.8 = (bf16[32,7168]{1,0:T(8,128)(2,1)S(1)}, bf16[32,7168]{1,0:T(8,128)(2,1)S(1)}, u32[]{:S(2)}, u32[]{:S(2)}) collective-permute-start(bf16[32,7168]{1,0:T(8,128)(2,1)S(1)} %shard_map.80.refs_0_), channel_id=1, source_target_pairs={{0,12},{1,49},{2,14},{3,51},{4,8},{5,53},{6,10},{7,55},{8,4},{9,57... | collective-permute-start | bytes 1376264 | tf_op jit(solution)/shard_map/ppermute | solution.py:40
  91.1 3.9 %collective-permute-start.7 = (bf16[32,7168]{1,0:T(8,128)(2,1)S(1)}, bf16[32,7168]{1,0:T(8,128)(2,1)S(1)}, u32[]{:S(2)}, u32[]{:S(2)}) collective-permute-start(bf16[32,7168]{1,0:T(8,128)(2,1)S(1)} %shard_map.80.refs_0_), channel_id=1, source_target_pairs={{0,8},{1,33},{2,10},{3,35},{4,12},{5,37},{6,14},{7,39},{8,0},{9,41... | collective-permute-start | bytes 1376264 | tf_op jit(solution)/shard_map/ppermute | solution.py:40
  95.0 3.4 %collective-permute-done.5.refs_1_ = bf16[32,7168]{1,0:T(8,128)(2,1)S(1)} collective-permute-done((bf16[32,7168]{1,0:T(8,128)(2,1)S(1)}, bf16[32,7168]{1,0:T(8,128)(2,1)S(1)}, u32[]{:S(2)}, u32[]{:S(2)}) %collective-permute-start.5) | collective-permute-done | bytes 458784 | tf_op jit(solution)/shard_map/ppermute | solution.py:40
  98.4 3.4 %collective-permute-start.6 = (f32[2,7168]{1,0:T(2,128)S(1)}, f32[2,7168]{1,0:T(2,128)S(1)}, u32[]{:S(2)}, u32[]{:S(2)}) collective-permute-start(f32[2,7168]{1,0:T(2,128)S(1)} %get-tuple-element.23), channel_id=1, source_target_pairs={{0,1},{1,0},{2,3},{3,2},{4,5},{5,4},{6,7},{7,6},{8,9},{9,8},{10,11... | collective-permute-start | bytes 172040 | tf_op jit(solution)/shard_map/ppermute | solution.py:40
  101.7 1.9 %collective-permute-start.11 = (bf16[32,7168]{1,0:T(8,128)(2,1)S(1)}, bf16[32,7168]{1,0:T(8,128)(2,1)S(1)}, u32[]{:S(2)}, u32[]{:S(2)}) collective-permute-start(bf16[32,7168]{1,0:T(8,128)(2,1)S(1)} %shard_map.80.refs_0_), channel_id=1, source_target_pairs={{0,1},{1,0},{2,3},{3,2},{4,5},{5,4},{6,7},{7,6},{8,9},{9,8},{10,11... | collective-permute-start | bytes 1376264 | tf_op jit(solution)/shard_map/ppermute | solution.py:40
  103.7 2.4 %collective-permute-start.12 = (bf16[32,7168]{1,0:T(8,128)(2,1)S(1)}, bf16[32,7168]{1,0:T(8,128)(2,1)S(1)}, u32[]{:S(2)}, u32[]{:S(2)}) collective-permute-start(bf16[32,7168]{1,0:T(8,128)(2,1)S(1)} %collective-permute-done.5.refs_1_), channel_id=1, source_target_pairs={{0,1},{1,0},{2,3},{3,2},{4,5},{5,4},{6,7},{7,6},{8,9},{9,8},{10,11... | collective-permute-start | bytes 1376264 | tf_op jit(solution)/shard_map/ppermute | solution.py:40
  106.1 4.9 %collective-permute-done.8.refs_1_ = bf16[32,7168]{1,0:T(8,128)(2,1)S(1)} collective-permute-done((bf16[32,7168]{1,0:T(8,128)(2,1)S(1)}, bf16[32,7168]{1,0:T(8,128)(2,1)S(1)}, u32[]{:S(2)}, u32[]{:S(2)}) %collective-permute-start.8) | collective-permute-done | bytes 458784 | tf_op jit(solution)/shard_map/ppermute | solution.py:40
  111.0 1.9 %collective-permute-start.10 = (bf16[32,7168]{1,0:T(8,128)(2,1)S(1)}, bf16[32,7168]{1,0:T(8,128)(2,1)S(1)}, u32[]{:S(2)}, u32[]{:S(2)}) collective-permute-start(bf16[32,7168]{1,0:T(8,128)(2,1)S(1)} %collective-permute-done.8.refs_1_), channel_id=1, source_target_pairs={{0,1},{1,0},{2,3},{3,2},{4,5},{5,4},{6,7},{7,6},{8,9},{9,8},{10,11... | collective-permute-start | bytes 1376264 | tf_op jit(solution)/shard_map/ppermute | solution.py:40
  112.9 2.4 %collective-permute-start.9 = (bf16[32,7168]{1,0:T(8,128)(2,1)S(1)}, bf16[32,7168]{1,0:T(8,128)(2,1)S(1)}, u32[]{:S(2)}, u32[]{:S(2)}) collective-permute-start(bf16[32,7168]{1,0:T(8,128)(2,1)S(1)} %collective-permute-done.7.refs_0_), channel_id=1, source_target_pairs={{0,1},{1,0},{2,3},{3,2},{4,5},{5,4},{6,7},{7,6},{8,9},{9,8},{10,11... | collective-permute-start | bytes 1376264 | tf_op jit(solution)/shard_map/ppermute | solution.py:40
  117.9 1.4 %shard_map.82 = bf16[128,14336]{1,0:T(8,128)(2,1)} custom-call(bf16[32,7168]{1,0:T(8,128)(2,1)S(1)} %collective-permute-done.7.refs_0_, bf16[32,7168]{1,0:T(8,128)(2,1)S(1)} %collective-permute-done.8.refs_1_, bf16[32,7168]{1,0:T(8,128)(2,1)S(1)} %collective-permute-done.9.refs_2_, ...), custom_call_target="tpu_custom_call", output_to_operand_aliasing={{}: (4, {})} | custom-call | bytes 3670016 | tf_op jit(solution)/shard_map/pallas_call | solution.py:311
  (27 shorter events, 8.4 us)
Async XLA Ops:
  0.6 12.0 %copy-start = (bf16[1,128,14336]{2,1,0:T(8,128)(2,1)S(1)}, bf16[1,128,14336]{2,1,0:T(8,128)(2,1)}, u32[]{:S(2)}) copy-start(bf16[1,128,14336]{2,1,0:T(8,128)(2,1)} %param.7) | copy-start | bytes 11010052
  0.6 12.0 %copy-start.1 = (bf16[1,128,128]{2,1,0:T(8,128)(2,1)S(1)}, bf16[1,128,128]{2,1,0:T(8,128)(2,1)}, u32[]{:S(2)}) copy-start(bf16[1,128,128]{2,1,0:T(8,128)(2,1)} %param.6) | copy-start | bytes 98308
  3.8 24.9 %copy-start.3 = (bf16[2,1792]{1,0:T(2,128)(2,1)S(1)}, bf16[2,1792]{1,0:T(2,128)(2,1)}, u32[]{:S(2)}) copy-start(bf16[2,1792]{1,0:T(2,128)(2,1)} %param.4) | copy-start | bytes 21508
  3.8 12.4 %collective-permute-start = (bf16[128,7168]{1,0:T(8,128)(2,1)}, bf16[128,7168]{1,0:T(8,128)(2,1)S(1)}, u32[]{:S(2)}, u32[]{:S(2)}) collective-permute-start(bf16[128,7168]{1,0:T(8,128)(2,1)} %shard_map.76), channel_id=1, source_target_pairs={{0,1},{1,0},{2,3},{3,2},{4,5},{5,4},{6,7},{7,6},{8,9},{9,8},{10,11... | collective-permute-start | bytes 5505032 | tf_op jit(solution)/shard_map/ppermute | solution.py:40
  13.8 40.6 %copy-start.2 = (bf16[1,2,14336]{2,1,0:T(2,128)(2,1)S(1)}, bf16[1,2,14336]{2,1,0:T(2,128)(2,1)}, u32[]{:S(2)}) copy-start(bf16[1,2,14336]{2,1,0:T(2,128)(2,1)} %param.5) | copy-start | bytes 172036
  17.3 16.8 %collective-permute-start.1 = (bf16[32,7168]{1,0:T(8,128)(2,1)}, bf16[32,7168]{1,0:T(8,128)(2,1)S(1)}, u32[]{:S(2)}, u32[]{:S(2)}) collective-permute-start(bf16[32,7168]{1,0:T(8,128)(2,1)} %get-tuple-element.15), channel_id=1, source_target_pairs={{0,8},{1,33},{2,10},{3,35},{4,12},{5,37},{6,14},{7,39},{8,0},{9,41... | collective-permute-start | bytes 1376264 | tf_op jit(solution)/shard_map/ppermute | solution.py:40
  22.5 21.6 %collective-permute-start.2 = (bf16[32,7168]{1,0:T(8,128)(2,1)S(1)}, bf16[32,7168]{1,0:T(8,128)(2,1)S(1)}, u32[]{:S(2)}, u32[]{:S(2)}) collective-permute-start(bf16[32,7168]{1,0:T(8,128)(2,1)S(1)} %get-tuple-element.16), channel_id=1, source_target_pairs={{0,4},{1,17},{2,6},{3,19},{4,0},{5,21},{6,2},{7,23},{8,12},{9,25},... | collective-permute-start | bytes 1376264 | tf_op jit(solution)/shard_map/ppermute | solution.py:40
  26.6 17.6 %collective-permute-start.3 = (bf16[32,7168]{1,0:T(8,128)(2,1)S(1)}, bf16[32,7168]{1,0:T(8,128)(2,1)S(1)}, u32[]{:S(2)}, u32[]{:S(2)}) collective-permute-start(bf16[32,7168]{1,0:T(8,128)(2,1)S(1)} %get-tuple-element.17), channel_id=1, source_target_pairs={{0,12},{1,49},{2,14},{3,51},{4,8},{5,53},{6,10},{7,55},{8,4},{9,57... | collective-permute-start | bytes 1376264 | tf_op jit(solution)/shard_map/ppermute | solution.py:40
  29.3 18.2 %all-to-all-start = ((bf16[8,2,1792]{2,1,0:T(2,128)(2,1)}), bf16[8,2,1792]{2,1,0:T(2,128)(2,1)S(1)}, u32[]{:S(2)}, u32[]{:S(2)}) async-start(bf16[8,2,1792]{2,1,0:T(2,128)(2,1)} %stack.4), calls=%async_computation | async-start | bytes 114688 | tf_op jit(solution)/shard_map/all_to_all | solution.py:340
  47.5 18.6 %all-to-all-start.1 = ((bf16[8,8,3584]{2,1,0:T(8,128)(2,1)}), bf16[8,8,3584]{2,1,0:T(8,128)(2,1)S(1)}, u32[]{:S(2)}, u32[]{:S(2)}) async-start(bf16[8,8,3584]{2,1,0:T(8,128)(2,1)} %bitcast.4), calls=%async_computation.1 | async-start | bytes 917504 | tf_op jit(solution)/shard_map/all_to_all | solution.py:61
  54.4 3.1 %collective-permute-start.4 = (bf16[2,2,7168]{2,1,0:T(2,128)(2,1)S(1)}, bf16[2,2,7168]{2,1,0:T(2,128)(2,1)S(1)}, u32[]{:S(2)}, u32[]{:S(2)}) collective-permute-start(bf16[2,2,7168]{2,1,0:T(2,128)(2,1)S(1)} %get-tuple-element.29), channel_id=1, source_target_pairs={{0,1},{1,0},{2,3},{3,2},{4,5},{5,4},{6,7},{7,6},{8,9},{9,8},{10,11... | collective-permute-start | bytes 172040 | tf_op jit(solution)/shard_map/ppermute | solution.py:40
  83.6 14.8 %collective-permute-start.5 = (bf16[32,7168]{1,0:T(8,128)(2,1)S(1)}, bf16[32,7168]{1,0:T(8,128)(2,1)S(1)}, u32[]{:S(2)}, u32[]{:S(2)}) collective-permute-start(bf16[32,7168]{1,0:T(8,128)(2,1)S(1)} %shard_map.80.refs_0_), channel_id=1, source_target_pairs={{0,4},{1,17},{2,6},{3,19},{4,0},{5,21},{6,2},{7,23},{8,12},{9,25},... | collective-permute-start | bytes 1376264 | tf_op jit(solution)/shard_map/ppermute | solution.py:40
  86.3 24.7 %collective-permute-start.8 = (bf16[32,7168]{1,0:T(8,128)(2,1)S(1)}, bf16[32,7168]{1,0:T(8,128)(2,1)S(1)}, u32[]{:S(2)}, u32[]{:S(2)}) collective-permute-start(bf16[32,7168]{1,0:T(8,128)(2,1)S(1)} %shard_map.80.refs_0_), channel_id=1, source_target_pairs={{0,12},{1,49},{2,14},{3,51},{4,8},{5,53},{6,10},{7,55},{8,4},{9,57... | collective-permute-start | bytes 1376264 | tf_op jit(solution)/shard_map/ppermute | solution.py:40
  91.1 21.8 %collective-permute-start.7 = (bf16[32,7168]{1,0:T(8,128)(2,1)S(1)}, bf16[32,7168]{1,0:T(8,128)(2,1)S(1)}, u32[]{:S(2)}, u32[]{:S(2)}) collective-permute-start(bf16[32,7168]{1,0:T(8,128)(2,1)S(1)} %shard_map.80.refs_0_), channel_id=1, source_target_pairs={{0,8},{1,33},{2,10},{3,35},{4,12},{5,37},{6,14},{7,39},{8,0},{9,41... | collective-permute-start | bytes 1376264 | tf_op jit(solution)/shard_map/ppermute | solution.py:40
  98.4 16.9 %collective-permute-start.6 = (f32[2,7168]{1,0:T(2,128)S(1)}, f32[2,7168]{1,0:T(2,128)S(1)}, u32[]{:S(2)}, u32[]{:S(2)}) collective-permute-start(f32[2,7168]{1,0:T(2,128)S(1)} %get-tuple-element.23), channel_id=1, source_target_pairs={{0,1},{1,0},{2,3},{3,2},{4,5},{5,4},{6,7},{7,6},{8,9},{9,8},{10,11... | collective-permute-start | bytes 172040 | tf_op jit(solution)/shard_map/ppermute | solution.py:40
  101.7 14.8 %collective-permute-start.11 = (bf16[32,7168]{1,0:T(8,128)(2,1)S(1)}, bf16[32,7168]{1,0:T(8,128)(2,1)S(1)}, u32[]{:S(2)}, u32[]{:S(2)}) collective-permute-start(bf16[32,7168]{1,0:T(8,128)(2,1)S(1)} %shard_map.80.refs_0_), channel_id=1, source_target_pairs={{0,1},{1,0},{2,3},{3,2},{4,5},{5,4},{6,7},{7,6},{8,9},{9,8},{10,11... | collective-permute-start | bytes 1376264 | tf_op jit(solution)/shard_map/ppermute | solution.py:40
  103.7 12.8 %collective-permute-start.12 = (bf16[32,7168]{1,0:T(8,128)(2,1)S(1)}, bf16[32,7168]{1,0:T(8,128)(2,1)S(1)}, u32[]{:S(2)}, u32[]{:S(2)}) collective-permute-start(bf16[32,7168]{1,0:T(8,128)(2,1)S(1)} %collective-permute-done.5.refs_1_), channel_id=1, source_target_pairs={{0,1},{1,0},{2,3},{3,2},{4,5},{5,4},{6,7},{7,6},{8,9},{9,8},{10,11... | collective-permute-start | bytes 1376264 | tf_op jit(solution)/shard_map/ppermute | solution.py:40
  111.0 6.9 %collective-permute-start.10 = (bf16[32,7168]{1,0:T(8,128)(2,1)S(1)}, bf16[32,7168]{1,0:T(8,128)(2,1)S(1)}, u32[]{:S(2)}, u32[]{:S(2)}) collective-permute-start(bf16[32,7168]{1,0:T(8,128)(2,1)S(1)} %collective-permute-done.8.refs_1_), channel_id=1, source_target_pairs={{0,1},{1,0},{2,3},{3,2},{4,5},{5,4},{6,7},{7,6},{8,9},{9,8},{10,11... | collective-permute-start | bytes 1376264 | tf_op jit(solution)/shard_map/ppermute | solution.py:40
  112.9 5.0 %collective-permute-start.9 = (bf16[32,7168]{1,0:T(8,128)(2,1)S(1)}, bf16[32,7168]{1,0:T(8,128)(2,1)S(1)}, u32[]{:S(2)}, u32[]{:S(2)}) collective-permute-start(bf16[32,7168]{1,0:T(8,128)(2,1)S(1)} %collective-permute-done.7.refs_0_), channel_id=1, source_target_pairs={{0,1},{1,0},{2,3},{3,2},{4,5},{5,4},{6,7},{7,6},{8,9},{9,8},{10,11... | collective-permute-start | bytes 1376264 | tf_op jit(solution)/shard_map/ppermute | solution.py:40

commit v5 on v4

--- a/solution.py
+++ b/solution.py
@@ -205,15 +205,15 @@
 
 
 def first_sum_kernel(own, r1, r2, r3, total, out):
-    for m in range(0, 32, 4):
-        parts = []
-        for h in range(2):
-            n = (slice(m, m + 4), slice(h * FOLD, (h + 1) * FOLD))
-            rest = r1[n].astype(F32) + r2[n].astype(F32) + r3[n].astype(F32)
-            parts.append(own[n] + rest)
-        value = jnp.concatenate(parts, 0)
-        total[2 * m : 2 * m + 8, :] = value
-        out[2 * m : 2 * m + 8, :] = value.astype(BF16)
+    for m in range(0, 32, 8):
+        n = slice(m, m + 8)
+        value = own[n, :] + (r1[n, :].astype(F32) + r2[n, :].astype(F32) + r3[n, :].astype(F32))
+        for i in range(2):
+            rows = value[4 * i : 4 * i + 4]
+            folded = jnp.concatenate([rows[:, :FOLD], rows[:, FOLD:]], 0)
+            start = 2 * m + 8 * i
+            total[start : start + 8, :] = folded
+            out[start : start + 8, :] = folded.astype(BF16)
 
 
 def first_sum(own, parts):

time: 121 us -> 121 us (level)
  no operation moved by 1% of the time
where the time goes in v5:
time: 121 us; the launch traced here: 119 us
  starting transfers between devices  56.8 us (47%)
  waiting for transfers between devices  32.8 us (27%)
  blocking collectives  17 us (14%)
  Pallas kernels  9.52 us (8%)
  other arithmetic  1.29 us (1%)
    ppermute x13, starting transfers between devices, send(): return lax.ppermute(x, 'fsdp', perm(target))  45.3 us
    ppermute x13, waiting for transfers between devices, send(): return lax.ppermute(x, 'fsdp', perm(target))  22.1 us
    all_to_all x1, blocking collectives, swap(): return lax.all_to_all(x, 'fsdp', 0, 0, axis_index_groups=MIDDLE, tiled=True)  17 us
    all_to_all x1, waiting for transfers between devices, swap(): return lax.all_to_all(x, 'fsdp', 0, 0, axis_index_groups=MIDDLE, tiled=True)  8.37 us
    all_to_all x1, starting transfers between devices, swap(): return lax.all_to_all(x, 'fsdp', 0, 0, axis_index_groups=MIDDLE, tiled=True)  6.82 us
    all_to_all x1, starting transfers between devices, body(): lax.all_to_all(jnp.stack([dense_rows] * 8), 'expert', 0, 0, tiled=True)  4.74 us
    pallas_call x1, Pallas kernels, far_product(): pl.pallas_call(far_product_kernel, in_specs=[HBM, HBM], out_specs=HBM, ou...  3.11 us
    pallas_call x2, Pallas kernels, assemble(): pl.pallas_call(functools.partial(assemble_kernel, pieces), in_specs=[pl.B...  2.72 us
  transfers between devices with their start and end apart: 15, of which 7 were waited for; matrix products, arithmetic and copies ran while one was open for 2% of the time, Pallas kernels for 3%

profile of v5, /device:TPU:1, one launch (start us, length us, event | category | flops | bytes accessed | tf_op | source)
XLA Modules:
  0.0 119.1 jit_solution(12356194434667341245)
XLA Ops:
  0.7 3.1 %shard_map.76 = bf16[128,7168]{1,0:T(8,128)(2,1)} custom-call(bf16[128,128]{1,0:T(8,128)(2,1)} %bitcast.19, bf16[128,14336]{1,0:T(8,128)(2,1)} %bitcast.14), custom_call_target="tpu_custom_call" | custom-call | flops 234881024 | bytes 3670016 | tf_op jit(solution)/shard_map/pallas_call | solution.py:149
  3.8 8.8 %collective-permute-start = (bf16[128,7168]{1,0:T(8,128)(2,1)}, bf16[128,7168]{1,0:T(8,128)(2,1)S(1)}, u32[]{:S(2)}, u32[]{:S(2)}) collective-permute-start(bf16[128,7168]{1,0:T(8,128)(2,1)} %shard_map.76), channel_id=1, source_target_pairs={{0,1},{1,0},{2,3},{3,2},{4,5},{5,4},{6,7},{7,6},{8,9},{9,8},{10,11... | collective-permute-start | bytes 5505032 | tf_op jit(solution)/shard_map/ppermute | solution.py:40
  13.8 2.4 %collective-permute-done.far = bf16[128,7168]{1,0:T(8,128)(2,1)S(1)} collective-permute-done((bf16[128,7168]{1,0:T(8,128)(2,1)}, bf16[128,7168]{1,0:T(8,128)(2,1)S(1)}, u32[]{:S(2)}, u32[]{:S(2)}) %collective-permute-start) | collective-permute-done | bytes 1835040 | tf_op jit(solution)/shard_map/ppermute | solution.py:40
  17.3 5.2 %collective-permute-start.1 = (bf16[32,7168]{1,0:T(8,128)(2,1)}, bf16[32,7168]{1,0:T(8,128)(2,1)S(1)}, u32[]{:S(2)}, u32[]{:S(2)}) collective-permute-start(bf16[32,7168]{1,0:T(8,128)(2,1)} %get-tuple-element.15), channel_id=1, source_target_pairs={{0,8},{1,33},{2,10},{3,35},{4,12},{5,37},{6,14},{7,39},{8,0},{9,41... | collective-permute-start | bytes 1376264 | tf_op jit(solution)/shard_map/ppermute | solution.py:40
  22.5 4.0 %collective-permute-start.2 = (bf16[32,7168]{1,0:T(8,128)(2,1)S(1)}, bf16[32,7168]{1,0:T(8,128)(2,1)S(1)}, u32[]{:S(2)}, u32[]{:S(2)}) collective-permute-start(bf16[32,7168]{1,0:T(8,128)(2,1)S(1)} %get-tuple-element.16), channel_id=1, source_target_pairs={{0,4},{1,17},{2,6},{3,19},{4,0},{5,21},{6,2},{7,23},{8,12},{9,25},... | collective-permute-start | bytes 1376264 | tf_op jit(solution)/shard_map/ppermute | solution.py:40
  26.6 2.1 %collective-permute-start.3 = (bf16[32,7168]{1,0:T(8,128)(2,1)S(1)}, bf16[32,7168]{1,0:T(8,128)(2,1)S(1)}, u32[]{:S(2)}, u32[]{:S(2)}) collective-permute-start(bf16[32,7168]{1,0:T(8,128)(2,1)S(1)} %get-tuple-element.17), channel_id=1, source_target_pairs={{0,12},{1,49},{2,14},{3,51},{4,8},{5,53},{6,10},{7,55},{8,4},{9,57... | collective-permute-start | bytes 1376264 | tf_op jit(solution)/shard_map/ppermute | solution.py:40
  29.3 4.7 %all-to-all-start = ((bf16[8,2,1792]{2,1,0:T(2,128)(2,1)}), bf16[8,2,1792]{2,1,0:T(2,128)(2,1)S(1)}, u32[]{:S(2)}, u32[]{:S(2)}) async-start(bf16[8,2,1792]{2,1,0:T(2,128)(2,1)} %stack.4), calls=%async_computation | async-start | bytes 114688 | tf_op jit(solution)/shard_map/all_to_all | solution.py:340
  34.1 10.1 %collective-permute-done.2.r2 = bf16[32,7168]{1,0:T(8,128)(2,1)S(1)} collective-permute-done((bf16[32,7168]{1,0:T(8,128)(2,1)S(1)}, bf16[32,7168]{1,0:T(8,128)(2,1)S(1)}, u32[]{:S(2)}, u32[]{:S(2)}) %collective-permute-start.2) | collective-permute-done | bytes 458784 | tf_op jit(solution)/shard_map/ppermute | solution.py:40
  45.2 2.3 %all-to-all-done = bf16[8,2,1792]{2,1,0:T(2,128)(2,1)S(1)} async-done(((bf16[8,2,1792]{2,1,0:T(2,128)(2,1)}), bf16[8,2,1792]{2,1,0:T(2,128)(2,1)S(1)}, u32[]{:S(2)}, u32[]{:S(2)}) %all-to-all-start) | async-done | bytes 57376 | tf_op jit(solution)/shard_map/all_to_all | solution.py:340
  47.5 6.8 %all-to-all-start.1 = ((bf16[8,8,3584]{2,1,0:T(8,128)(2,1)}), bf16[8,8,3584]{2,1,0:T(8,128)(2,1)S(1)}, u32[]{:S(2)}, u32[]{:S(2)}) async-start(bf16[8,8,3584]{2,1,0:T(8,128)(2,1)} %bitcast.4), calls=%async_computation.1 | async-start | bytes 917504 | tf_op jit(solution)/shard_map/all_to_all | solution.py:61
  54.4 1.9 %collective-permute-start.4 = (bf16[2,2,7168]{2,1,0:T(2,128)(2,1)S(1)}, bf16[2,2,7168]{2,1,0:T(2,128)(2,1)S(1)}, u32[]{:S(2)}, u32[]{:S(2)}) collective-permute-start(bf16[2,2,7168]{2,1,0:T(2,128)(2,1)S(1)} %get-tuple-element.29), channel_id=1, source_target_pairs={{0,1},{1,0},{2,3},{3,2},{4,5},{5,4},{6,7},{7,6},{8,9},{9,8},{10,11... | collective-permute-start | bytes 172040 | tf_op jit(solution)/shard_map/ppermute | solution.py:40
  57.6 8.4 %all-to-all-done.1 = bf16[8,8,3584]{2,1,0:T(8,128)(2,1)S(1)} async-done(((bf16[8,8,3584]{2,1,0:T(8,128)(2,1)}), bf16[8,8,3584]{2,1,0:T(8,128)(2,1)S(1)}, u32[]{:S(2)}, u32[]{:S(2)}) %all-to-all-start.1) | async-done | bytes 458784 | tf_op jit(solution)/shard_map/all_to_all | solution.py:61
  66.2 17.0 %all_to_all.27 = bf16[8,8,3584]{2,1,0:T(8,128)(2,1)S(1)} all-to-all(bf16[8,8,3584]{2,1,0:T(8,128)(2,1)S(1)} %bitcast.18), channel_id=1, replica_groups={{0,2,16,18,32,34,48,50},{4,6,20,22,36,38,52,54},{8,10,24,26,40,42,56,58..., dimensions={0} | all-to-all | bytes 917504 | tf_op jit(solution)/shard_map/all_to_all | solution.py:61
  83.4 3.1 %collective-permute-start.5 = (bf16[32,7168]{1,0:T(8,128)(2,1)S(1)}, bf16[32,7168]{1,0:T(8,128)(2,1)S(1)}, u32[]{:S(2)}, u32[]{:S(2)}) collective-permute-start(bf16[32,7168]{1,0:T(8,128)(2,1)S(1)} %shard_map.80.refs_0_), channel_id=1, source_target_pairs={{0,4},{1,17},{2,6},{3,19},{4,0},{5,21},{6,2},{7,23},{8,12},{9,25},... | collective-permute-start | bytes 1376264 | tf_op jit(solution)/shard_map/ppermute | solution.py:40
  86.6 4.3 %collective-permute-start.8 = (bf16[32,7168]{1,0:T(8,128)(2,1)S(1)}, bf16[32,7168]{1,0:T(8,128)(2,1)S(1)}, u32[]{:S(2)}, u32[]{:S(2)}) collective-permute-start(bf16[32,7168]{1,0:T(8,128)(2,1)S(1)} %shard_map.80.refs_0_), channel_id=1, source_target_pairs={{0,12},{1,49},{2,14},{3,51},{4,8},{5,53},{6,10},{7,55},{8,4},{9,57... | collective-permute-start | bytes 1376264 | tf_op jit(solution)/shard_map/ppermute | solution.py:40
  90.9 3.9 %collective-permute-start.7 = (bf16[32,7168]{1,0:T(8,128)(2,1)S(1)}, bf16[32,7168]{1,0:T(8,128)(2,1)S(1)}, u32[]{:S(2)}, u32[]{:S(2)}) collective-permute-start(bf16[32,7168]{1,0:T(8,128)(2,1)S(1)} %shard_map.80.refs_0_), channel_id=1, source_target_pairs={{0,8},{1,33},{2,10},{3,35},{4,12},{5,37},{6,14},{7,39},{8,0},{9,41... | collective-permute-start | bytes 1376264 | tf_op jit(solution)/shard_map/ppermute | solution.py:40
  94.8 3.4 %collective-permute-done.5.refs_1_ = bf16[32,7168]{1,0:T(8,128)(2,1)S(1)} collective-permute-done((bf16[32,7168]{1,0:T(8,128)(2,1)S(1)}, bf16[32,7168]{1,0:T(8,128)(2,1)S(1)}, u32[]{:S(2)}, u32[]{:S(2)}) %collective-permute-start.5) | collective-permute-done | bytes 458784 | tf_op jit(solution)/shard_map/ppermute | solution.py:40
  98.2 3.2 %collective-permute-start.6 = (f32[2,7168]{1,0:T(2,128)S(1)}, f32[2,7168]{1,0:T(2,128)S(1)}, u32[]{:S(2)}, u32[]{:S(2)}) collective-permute-start(f32[2,7168]{1,0:T(2,128)S(1)} %get-tuple-element.23), channel_id=1, source_target_pairs={{0,1},{1,0},{2,3},{3,2},{4,5},{5,4},{6,7},{7,6},{8,9},{9,8},{10,11... | collective-permute-start | bytes 172040 | tf_op jit(solution)/shard_map/ppermute | solution.py:40
  101.4 1.9 %collective-permute-start.11 = (bf16[32,7168]{1,0:T(8,128)(2,1)S(1)}, bf16[32,7168]{1,0:T(8,128)(2,1)S(1)}, u32[]{:S(2)}, u32[]{:S(2)}) collective-permute-start(bf16[32,7168]{1,0:T(8,128)(2,1)S(1)} %shard_map.80.refs_0_), channel_id=1, source_target_pairs={{0,1},{1,0},{2,3},{3,2},{4,5},{5,4},{6,7},{7,6},{8,9},{9,8},{10,11... | collective-permute-start | bytes 1376264 | tf_op jit(solution)/shard_map/ppermute | solution.py:40
  103.3 2.4 %collective-permute-start.12 = (bf16[32,7168]{1,0:T(8,128)(2,1)S(1)}, bf16[32,7168]{1,0:T(8,128)(2,1)S(1)}, u32[]{:S(2)}, u32[]{:S(2)}) collective-permute-start(bf16[32,7168]{1,0:T(8,128)(2,1)S(1)} %collective-permute-done.5.refs_1_), channel_id=1, source_target_pairs={{0,1},{1,0},{2,3},{3,2},{4,5},{5,4},{6,7},{7,6},{8,9},{9,8},{10,11... | collective-permute-start | bytes 1376264 | tf_op jit(solution)/shard_map/ppermute | solution.py:40
  105.7 5.1 %collective-permute-done.8.refs_1_ = bf16[32,7168]{1,0:T(8,128)(2,1)S(1)} collective-permute-done((bf16[32,7168]{1,0:T(8,128)(2,1)S(1)}, bf16[32,7168]{1,0:T(8,128)(2,1)S(1)}, u32[]{:S(2)}, u32[]{:S(2)}) %collective-permute-start.8) | collective-permute-done | bytes 458784 | tf_op jit(solution)/shard_map/ppermute | solution.py:40
  110.8 1.9 %collective-permute-start.10 = (bf16[32,7168]{1,0:T(8,128)(2,1)S(1)}, bf16[32,7168]{1,0:T(8,128)(2,1)S(1)}, u32[]{:S(2)}, u32[]{:S(2)}) collective-permute-start(bf16[32,7168]{1,0:T(8,128)(2,1)S(1)} %collective-permute-done.8.refs_1_), channel_id=1, source_target_pairs={{0,1},{1,0},{2,3},{3,2},{4,5},{5,4},{6,7},{7,6},{8,9},{9,8},{10,11... | collective-permute-start | bytes 1376264 | tf_op jit(solution)/shard_map/ppermute | solution.py:40
  112.7 2.4 %collective-permute-start.9 = (bf16[32,7168]{1,0:T(8,128)(2,1)S(1)}, bf16[32,7168]{1,0:T(8,128)(2,1)S(1)}, u32[]{:S(2)}, u32[]{:S(2)}) collective-permute-start(bf16[32,7168]{1,0:T(8,128)(2,1)S(1)} %collective-permute-done.7.refs_0_), channel_id=1, source_target_pairs={{0,1},{1,0},{2,3},{3,2},{4,5},{5,4},{6,7},{7,6},{8,9},{9,8},{10,11... | collective-permute-start | bytes 1376264 | tf_op jit(solution)/shard_map/ppermute | solution.py:40
  117.7 1.4 %shard_map.82 = bf16[128,14336]{1,0:T(8,128)(2,1)} custom-call(bf16[32,7168]{1,0:T(8,128)(2,1)S(1)} %collective-permute-done.7.refs_0_, bf16[32,7168]{1,0:T(8,128)(2,1)S(1)} %collective-permute-done.8.refs_1_, bf16[32,7168]{1,0:T(8,128)(2,1)S(1)} %collective-permute-done.9.refs_2_, ...), custom_call_target="tpu_custom_call", output_to_operand_aliasing={{}: (4, {})} | custom-call | bytes 3670016 | tf_op jit(solution)/shard_map/pallas_call | solution.py:311
  (27 shorter events, 8.2 us)
Async XLA Ops:
  0.6 12.0 %copy-start = (bf16[1,128,14336]{2,1,0:T(8,128)(2,1)S(1)}, bf16[1,128,14336]{2,1,0:T(8,128)(2,1)}, u32[]{:S(2)}) copy-start(bf16[1,128,14336]{2,1,0:T(8,128)(2,1)} %param.7) | copy-start | bytes 11010052
  0.6 12.0 %copy-start.1 = (bf16[1,128,128]{2,1,0:T(8,128)(2,1)S(1)}, bf16[1,128,128]{2,1,0:T(8,128)(2,1)}, u32[]{:S(2)}) copy-start(bf16[1,128,128]{2,1,0:T(8,128)(2,1)} %param.6) | copy-start | bytes 98308
  3.8 24.9 %copy-start.3 = (bf16[2,1792]{1,0:T(2,128)(2,1)S(1)}, bf16[2,1792]{1,0:T(2,128)(2,1)}, u32[]{:S(2)}) copy-start(bf16[2,1792]{1,0:T(2,128)(2,1)} %param.4) | copy-start | bytes 21508
  3.8 12.4 %collective-permute-start = (bf16[128,7168]{1,0:T(8,128)(2,1)}, bf16[128,7168]{1,0:T(8,128)(2,1)S(1)}, u32[]{:S(2)}, u32[]{:S(2)}) collective-permute-start(bf16[128,7168]{1,0:T(8,128)(2,1)} %shard_map.76), channel_id=1, source_target_pairs={{0,1},{1,0},{2,3},{3,2},{4,5},{5,4},{6,7},{7,6},{8,9},{9,8},{10,11... | collective-permute-start | bytes 5505032 | tf_op jit(solution)/shard_map/ppermute | solution.py:40
  13.8 40.6 %copy-start.2 = (bf16[1,2,14336]{2,1,0:T(2,128)(2,1)S(1)}, bf16[1,2,14336]{2,1,0:T(2,128)(2,1)}, u32[]{:S(2)}) copy-start(bf16[1,2,14336]{2,1,0:T(2,128)(2,1)} %param.5) | copy-start | bytes 172036
  17.3 16.8 %collective-permute-start.1 = (bf16[32,7168]{1,0:T(8,128)(2,1)}, bf16[32,7168]{1,0:T(8,128)(2,1)S(1)}, u32[]{:S(2)}, u32[]{:S(2)}) collective-permute-start(bf16[32,7168]{1,0:T(8,128)(2,1)} %get-tuple-element.15), channel_id=1, source_target_pairs={{0,8},{1,33},{2,10},{3,35},{4,12},{5,37},{6,14},{7,39},{8,0},{9,41... | collective-permute-start | bytes 1376264 | tf_op jit(solution)/shard_map/ppermute | solution.py:40
  22.5 21.6 %collective-permute-start.2 = (bf16[32,7168]{1,0:T(8,128)(2,1)S(1)}, bf16[32,7168]{1,0:T(8,128)(2,1)S(1)}, u32[]{:S(2)}, u32[]{:S(2)}) collective-permute-start(bf16[32,7168]{1,0:T(8,128)(2,1)S(1)} %get-tuple-element.16), channel_id=1, source_target_pairs={{0,4},{1,17},{2,6},{3,19},{4,0},{5,21},{6,2},{7,23},{8,12},{9,25},... | collective-permute-start | bytes 1376264 | tf_op jit(solution)/shard_map/ppermute | solution.py:40
  26.6 17.6 %collective-permute-start.3 = (bf16[32,7168]{1,0:T(8,128)(2,1)S(1)}, bf16[32,7168]{1,0:T(8,128)(2,1)S(1)}, u32[]{:S(2)}, u32[]{:S(2)}) collective-permute-start(bf16[32,7168]{1,0:T(8,128)(2,1)S(1)} %get-tuple-element.17), channel_id=1, source_target_pairs={{0,12},{1,49},{2,14},{3,51},{4,8},{5,53},{6,10},{7,55},{8,4},{9,57... | collective-permute-start | bytes 1376264 | tf_op jit(solution)/shard_map/ppermute | solution.py:40
  29.3 18.2 %all-to-all-start = ((bf16[8,2,1792]{2,1,0:T(2,128)(2,1)}), bf16[8,2,1792]{2,1,0:T(2,128)(2,1)S(1)}, u32[]{:S(2)}, u32[]{:S(2)}) async-start(bf16[8,2,1792]{2,1,0:T(2,128)(2,1)} %stack.4), calls=%async_computation | async-start | bytes 114688 | tf_op jit(solution)/shard_map/all_to_all | solution.py:340
  47.5 18.5 %all-to-all-start.1 = ((bf16[8,8,3584]{2,1,0:T(8,128)(2,1)}), bf16[8,8,3584]{2,1,0:T(8,128)(2,1)S(1)}, u32[]{:S(2)}, u32[]{:S(2)}) async-start(bf16[8,8,3584]{2,1,0:T(8,128)(2,1)} %bitcast.4), calls=%async_computation.1 | async-start | bytes 917504 | tf_op jit(solution)/shard_map/all_to_all | solution.py:61
  54.4 3.1 %collective-permute-start.4 = (bf16[2,2,7168]{2,1,0:T(2,128)(2,1)S(1)}, bf16[2,2,7168]{2,1,0:T(2,128)(2,1)S(1)}, u32[]{:S(2)}, u32[]{:S(2)}) collective-permute-start(bf16[2,2,7168]{2,1,0:T(2,128)(2,1)S(1)} %get-tuple-element.29), channel_id=1, source_target_pairs={{0,1},{1,0},{2,3},{3,2},{4,5},{5,4},{6,7},{7,6},{8,9},{9,8},{10,11... | collective-permute-start | bytes 172040 | tf_op jit(solution)/shard_map/ppermute | solution.py:40
  83.4 14.8 %collective-permute-start.5 = (bf16[32,7168]{1,0:T(8,128)(2,1)S(1)}, bf16[32,7168]{1,0:T(8,128)(2,1)S(1)}, u32[]{:S(2)}, u32[]{:S(2)}) collective-permute-start(bf16[32,7168]{1,0:T(8,128)(2,1)S(1)} %shard_map.80.refs_0_), channel_id=1, source_target_pairs={{0,4},{1,17},{2,6},{3,19},{4,0},{5,21},{6,2},{7,23},{8,12},{9,25},... | collective-permute-start | bytes 1376264 | tf_op jit(solution)/shard_map/ppermute | solution.py:40
  86.6 24.2 %collective-permute-start.8 = (bf16[32,7168]{1,0:T(8,128)(2,1)S(1)}, bf16[32,7168]{1,0:T(8,128)(2,1)S(1)}, u32[]{:S(2)}, u32[]{:S(2)}) collective-permute-start(bf16[32,7168]{1,0:T(8,128)(2,1)S(1)} %shard_map.80.refs_0_), channel_id=1, source_target_pairs={{0,12},{1,49},{2,14},{3,51},{4,8},{5,53},{6,10},{7,55},{8,4},{9,57... | collective-permute-start | bytes 1376264 | tf_op jit(solution)/shard_map/ppermute | solution.py:40
  90.9 21.8 %collective-permute-start.7 = (bf16[32,7168]{1,0:T(8,128)(2,1)S(1)}, bf16[32,7168]{1,0:T(8,128)(2,1)S(1)}, u32[]{:S(2)}, u32[]{:S(2)}) collective-permute-start(bf16[32,7168]{1,0:T(8,128)(2,1)S(1)} %shard_map.80.refs_0_), channel_id=1, source_target_pairs={{0,8},{1,33},{2,10},{3,35},{4,12},{5,37},{6,14},{7,39},{8,0},{9,41... | collective-permute-start | bytes 1376264 | tf_op jit(solution)/shard_map/ppermute | solution.py:40
  98.2 16.9 %collective-permute-start.6 = (f32[2,7168]{1,0:T(2,128)S(1)}, f32[2,7168]{1,0:T(2,128)S(1)}, u32[]{:S(2)}, u32[]{:S(2)}) collective-permute-start(f32[2,7168]{1,0:T(2,128)S(1)} %get-tuple-element.23), channel_id=1, source_target_pairs={{0,1},{1,0},{2,3},{3,2},{4,5},{5,4},{6,7},{7,6},{8,9},{9,8},{10,11... | collective-permute-start | bytes 172040 | tf_op jit(solution)/shard_map/ppermute | solution.py:40
  101.4 14.9 %collective-permute-start.11 = (bf16[32,7168]{1,0:T(8,128)(2,1)S(1)}, bf16[32,7168]{1,0:T(8,128)(2,1)S(1)}, u32[]{:S(2)}, u32[]{:S(2)}) collective-permute-start(bf16[32,7168]{1,0:T(8,128)(2,1)S(1)} %shard_map.80.refs_0_), channel_id=1, source_target_pairs={{0,1},{1,0},{2,3},{3,2},{4,5},{5,4},{6,7},{7,6},{8,9},{9,8},{10,11... | collective-permute-start | bytes 1376264 | tf_op jit(solution)/shard_map/ppermute | solution.py:40
  103.3 13.0 %collective-permute-start.12 = (bf16[32,7168]{1,0:T(8,128)(2,1)S(1)}, bf16[32,7168]{1,0:T(8,128)(2,1)S(1)}, u32[]{:S(2)}, u32[]{:S(2)}) collective-permute-start(bf16[32,7168]{1,0:T(8,128)(2,1)S(1)} %collective-permute-done.5.refs_1_), channel_id=1, source_target_pairs={{0,1},{1,0},{2,3},{3,2},{4,5},{5,4},{6,7},{7,6},{8,9},{9,8},{10,11... | collective-permute-start | bytes 1376264 | tf_op jit(solution)/shard_map/ppermute | solution.py:40
  110.8 6.9 %collective-permute-start.10 = (bf16[32,7168]{1,0:T(8,128)(2,1)S(1)}, bf16[32,7168]{1,0:T(8,128)(2,1)S(1)}, u32[]{:S(2)}, u32[]{:S(2)}) collective-permute-start(bf16[32,7168]{1,0:T(8,128)(2,1)S(1)} %collective-permute-done.8.refs_1_), channel_id=1, source_target_pairs={{0,1},{1,0},{2,3},{3,2},{4,5},{5,4},{6,7},{7,6},{8,9},{9,8},{10,11... | collective-permute-start | bytes 1376264 | tf_op jit(solution)/shard_map/ppermute | solution.py:40
  112.7 5.0 %collective-permute-start.9 = (bf16[32,7168]{1,0:T(8,128)(2,1)S(1)}, bf16[32,7168]{1,0:T(8,128)(2,1)S(1)}, u32[]{:S(2)}, u32[]{:S(2)}) collective-permute-start(bf16[32,7168]{1,0:T(8,128)(2,1)S(1)} %collective-permute-done.7.refs_0_), channel_id=1, source_target_pairs={{0,1},{1,0},{2,3},{3,2},{4,5},{5,4},{6,7},{7,6},{8,9},{9,8},{10,11... | collective-permute-start | bytes 1376264 | tf_op jit(solution)/shard_map/ppermute | solution.py:40

commit v6 on v4

--- a/solution.py
+++ b/solution.py
@@ -334,7 +334,7 @@
     far = send(far_product(features[0], grads), other_core)
     near = near_product(features[0], grads)
     own, *chunks = chip_sum(near, far)
-    got = [send(chunks[k - 1], wide(k)) for k in (2, 1, 3)]
+    got = [send(chunks[k - 1], wide(k)) for k in (1, 3, 2)]
     total, rounded = first_sum(own, got)
 
     dense = lax.all_to_all(jnp.stack([dense_rows] * 8), "expert", 0, 0, tiled=True)

time: 121 us -> 122 us (level)
  the two profiles are of different devices: /device:TPU:1 before, /device:TPU:55 now
where the time goes in v6:
time: 122 us; the launch traced here: 121 us
  starting transfers between devices  69.6 us (57%)
  waiting for transfers between devices  22.8 us (19%)
  blocking collectives  16.3 us (13%)
  Pallas kernels  9.7 us (8%)
  other arithmetic  1.28 us (1%)
    ppermute x13, starting transfers between devices, send(): return lax.ppermute(x, 'fsdp', perm(target))  58 us
    ppermute x13, waiting for transfers between devices, send(): return lax.ppermute(x, 'fsdp', perm(target))  18.8 us
    all_to_all x1, blocking collectives, swap(): return lax.all_to_all(x, 'fsdp', 0, 0, axis_index_groups=MIDDLE, tiled=True)  16.3 us
    all_to_all x1, starting transfers between devices, swap(): return lax.all_to_all(x, 'fsdp', 0, 0, axis_index_groups=MIDDLE, tiled=True)  6.42 us
    all_to_all x1, starting transfers between devices, body(): lax.all_to_all(jnp.stack([dense_rows] * 8), 'expert', 0, 0, tiled=True)  5.12 us
    all_to_all x1, waiting for transfers between devices, swap(): return lax.all_to_all(x, 'fsdp', 0, 0, axis_index_groups=MIDDLE, tiled=True)  4.03 us
    pallas_call x1, Pallas kernels, far_product(): pl.pallas_call(far_product_kernel, in_specs=[HBM, HBM], out_specs=HBM, ou...  3.11 us
    pallas_call x2, Pallas kernels, assemble(): pl.pallas_call(functools.partial(assemble_kernel, pieces), in_specs=[pl.B...  2.72 us
  transfers between devices with their start and end apart: 15, of which 6 were waited for; matrix products, arithmetic and copies ran while one was open for 2% of the time, Pallas kernels for 3%

profile of v6, /device:TPU:55, one launch (start us, length us, event | category | flops | bytes accessed | tf_op | source)
XLA Modules:
  0.0 121.2 jit_solution(10609769860351958450)
XLA Ops:
  0.7 3.1 %shard_map.76 = bf16[128,7168]{1,0:T(8,128)(2,1)} custom-call(bf16[128,128]{1,0:T(8,128)(2,1)} %bitcast.19, bf16[128,14336]{1,0:T(8,128)(2,1)} %bitcast.14), custom_call_target="tpu_custom_call" | custom-call | flops 234881024 | bytes 3670016 | tf_op jit(solution)/shard_map/pallas_call | solution.py:149
  3.8 2.6 %collective-permute-start = (bf16[128,7168]{1,0:T(8,128)(2,1)}, bf16[128,7168]{1,0:T(8,128)(2,1)S(1)}, u32[]{:S(2)}, u32[]{:S(2)}) collective-permute-start(bf16[128,7168]{1,0:T(8,128)(2,1)} %shard_map.76), channel_id=1, source_target_pairs={{0,1},{1,0},{2,3},{3,2},{4,5},{5,4},{6,7},{7,6},{8,9},{9,8},{10,11... | collective-permute-start | bytes 5505032 | tf_op jit(solution)/shard_map/ppermute | solution.py:40
  7.6 2.4 %collective-permute-done.far = bf16[128,7168]{1,0:T(8,128)(2,1)S(1)} collective-permute-done((bf16[128,7168]{1,0:T(8,128)(2,1)}, bf16[128,7168]{1,0:T(8,128)(2,1)S(1)}, u32[]{:S(2)}, u32[]{:S(2)}) %collective-permute-start) | collective-permute-done | bytes 1835040 | tf_op jit(solution)/shard_map/ppermute | solution.py:40
  11.1 5.8 %collective-permute-start.1 = (bf16[32,7168]{1,0:T(8,128)(2,1)}, bf16[32,7168]{1,0:T(8,128)(2,1)S(1)}, u32[]{:S(2)}, u32[]{:S(2)}) collective-permute-start(bf16[32,7168]{1,0:T(8,128)(2,1)} %get-tuple-element.15), channel_id=1, source_target_pairs={{0,4},{1,17},{2,6},{3,19},{4,0},{5,21},{6,2},{7,23},{8,12},{9,25},... | collective-permute-start | bytes 1376264 | tf_op jit(solution)/shard_map/ppermute | solution.py:40
  16.9 7.0 %collective-permute-start.2 = (bf16[32,7168]{1,0:T(8,128)(2,1)S(1)}, bf16[32,7168]{1,0:T(8,128)(2,1)S(1)}, u32[]{:S(2)}, u32[]{:S(2)}) collective-permute-start(bf16[32,7168]{1,0:T(8,128)(2,1)S(1)} %get-tuple-element.16), channel_id=1, source_target_pairs={{0,12},{1,49},{2,14},{3,51},{4,8},{5,53},{6,10},{7,55},{8,4},{9,57... | collective-permute-start | bytes 1376264 | tf_op jit(solution)/shard_map/ppermute | solution.py:40
  23.9 3.7 %collective-permute-start.3 = (bf16[32,7168]{1,0:T(8,128)(2,1)S(1)}, bf16[32,7168]{1,0:T(8,128)(2,1)S(1)}, u32[]{:S(2)}, u32[]{:S(2)}) collective-permute-start(bf16[32,7168]{1,0:T(8,128)(2,1)S(1)} %get-tuple-element.17), channel_id=1, source_target_pairs={{0,8},{1,33},{2,10},{3,35},{4,12},{5,37},{6,14},{7,39},{8,0},{9,41... | collective-permute-start | bytes 1376264 | tf_op jit(solution)/shard_map/ppermute | solution.py:40
  28.3 5.1 %all-to-all-start = ((bf16[8,2,1792]{2,1,0:T(2,128)(2,1)}), bf16[8,2,1792]{2,1,0:T(2,128)(2,1)S(1)}, u32[]{:S(2)}, u32[]{:S(2)}) async-start(bf16[8,2,1792]{2,1,0:T(2,128)(2,1)} %stack.4), calls=%async_computation | async-start | bytes 114688 | tf_op jit(solution)/shard_map/all_to_all | solution.py:340
  33.4 10.6 %collective-permute-done.2.r2 = bf16[32,7168]{1,0:T(8,128)(2,1)S(1)} collective-permute-done((bf16[32,7168]{1,0:T(8,128)(2,1)S(1)}, bf16[32,7168]{1,0:T(8,128)(2,1)S(1)}, u32[]{:S(2)}, u32[]{:S(2)}) %collective-permute-start.2) | collective-permute-done | bytes 458784 | tf_op jit(solution)/shard_map/ppermute | solution.py:40
  45.3 6.4 %all-to-all-start.1 = ((bf16[8,8,3584]{2,1,0:T(8,128)(2,1)}), bf16[8,8,3584]{2,1,0:T(8,128)(2,1)S(1)}, u32[]{:S(2)}, u32[]{:S(2)}) async-start(bf16[8,8,3584]{2,1,0:T(8,128)(2,1)} %bitcast.4), calls=%async_computation.1 | async-start | bytes 917504 | tf_op jit(solution)/shard_map/all_to_all | solution.py:61
  51.8 4.6 %collective-permute-start.4 = (bf16[2,2,7168]{2,1,0:T(2,128)(2,1)S(1)}, bf16[2,2,7168]{2,1,0:T(2,128)(2,1)S(1)}, u32[]{:S(2)}, u32[]{:S(2)}) collective-permute-start(bf16[2,2,7168]{2,1,0:T(2,128)(2,1)S(1)} %get-tuple-element.29), channel_id=1, source_target_pairs={{0,1},{1,0},{2,3},{3,2},{4,5},{5,4},{6,7},{7,6},{8,9},{9,8},{10,11... | collective-permute-start | bytes 172040 | tf_op jit(solution)/shard_map/ppermute | solution.py:40
  57.3 4.0 %all-to-all-done.1 = bf16[8,8,3584]{2,1,0:T(8,128)(2,1)S(1)} async-done(((bf16[8,8,3584]{2,1,0:T(8,128)(2,1)}), bf16[8,8,3584]{2,1,0:T(8,128)(2,1)S(1)}, u32[]{:S(2)}, u32[]{:S(2)}) %all-to-all-start.1) | async-done | bytes 458784 | tf_op jit(solution)/shard_map/all_to_all | solution.py:61
  61.6 16.3 %all_to_all.27 = bf16[8,8,3584]{2,1,0:T(8,128)(2,1)S(1)} all-to-all(bf16[8,8,3584]{2,1,0:T(8,128)(2,1)S(1)} %bitcast.18), channel_id=1, replica_groups={{0,2,16,18,32,34,48,50},{4,6,20,22,36,38,52,54},{8,10,24,26,40,42,56,58..., dimensions={0} | all-to-all | bytes 917504 | tf_op jit(solution)/shard_map/all_to_all | solution.py:61
  78.0 4.9 %collective-permute-start.5 = (bf16[32,7168]{1,0:T(8,128)(2,1)S(1)}, bf16[32,7168]{1,0:T(8,128)(2,1)S(1)}, u32[]{:S(2)}, u32[]{:S(2)}) collective-permute-start(bf16[32,7168]{1,0:T(8,128)(2,1)S(1)} %shard_map.80.refs_0_), channel_id=1, source_target_pairs={{0,4},{1,17},{2,6},{3,19},{4,0},{5,21},{6,2},{7,23},{8,12},{9,25},... | collective-permute-start | bytes 1376264 | tf_op jit(solution)/shard_map/ppermute | solution.py:40
  82.9 3.5 %collective-permute-start.8 = (bf16[32,7168]{1,0:T(8,128)(2,1)S(1)}, bf16[32,7168]{1,0:T(8,128)(2,1)S(1)}, u32[]{:S(2)}, u32[]{:S(2)}) collective-permute-start(bf16[32,7168]{1,0:T(8,128)(2,1)S(1)} %shard_map.80.refs_0_), channel_id=1, source_target_pairs={{0,12},{1,49},{2,14},{3,51},{4,8},{5,53},{6,10},{7,55},{8,4},{9,57... | collective-permute-start | bytes 1376264 | tf_op jit(solution)/shard_map/ppermute | solution.py:40
  86.5 4.0 %collective-permute-start.7 = (bf16[32,7168]{1,0:T(8,128)(2,1)S(1)}, bf16[32,7168]{1,0:T(8,128)(2,1)S(1)}, u32[]{:S(2)}, u32[]{:S(2)}) collective-permute-start(bf16[32,7168]{1,0:T(8,128)(2,1)S(1)} %shard_map.80.refs_0_), channel_id=1, source_target_pairs={{0,8},{1,33},{2,10},{3,35},{4,12},{5,37},{6,14},{7,39},{8,0},{9,41... | collective-permute-start | bytes 1376264 | tf_op jit(solution)/shard_map/ppermute | solution.py:40
  90.5 1.6 %collective-permute-done.5.refs_1_ = bf16[32,7168]{1,0:T(8,128)(2,1)S(1)} collective-permute-done((bf16[32,7168]{1,0:T(8,128)(2,1)S(1)}, bf16[32,7168]{1,0:T(8,128)(2,1)S(1)}, u32[]{:S(2)}, u32[]{:S(2)}) %collective-permute-start.5) | collective-permute-done | bytes 458784 | tf_op jit(solution)/shard_map/ppermute | solution.py:40
  92.1 7.0 %collective-permute-start.6 = (f32[2,7168]{1,0:T(2,128)S(1)}, f32[2,7168]{1,0:T(2,128)S(1)}, u32[]{:S(2)}, u32[]{:S(2)}) collective-permute-start(f32[2,7168]{1,0:T(2,128)S(1)} %get-tuple-element.23), channel_id=1, source_target_pairs={{0,1},{1,0},{2,3},{3,2},{4,5},{5,4},{6,7},{7,6},{8,9},{9,8},{10,11... | collective-permute-start | bytes 172040 | tf_op jit(solution)/shard_map/ppermute | solution.py:40
  99.0 1.9 %collective-permute-start.11 = (bf16[32,7168]{1,0:T(8,128)(2,1)S(1)}, bf16[32,7168]{1,0:T(8,128)(2,1)S(1)}, u32[]{:S(2)}, u32[]{:S(2)}) collective-permute-start(bf16[32,7168]{1,0:T(8,128)(2,1)S(1)} %shard_map.80.refs_0_), channel_id=1, source_target_pairs={{0,1},{1,0},{2,3},{3,2},{4,5},{5,4},{6,7},{7,6},{8,9},{9,8},{10,11... | collective-permute-start | bytes 1376264 | tf_op jit(solution)/shard_map/ppermute | solution.py:40
  101.0 2.4 %collective-permute-start.12 = (bf16[32,7168]{1,0:T(8,128)(2,1)S(1)}, bf16[32,7168]{1,0:T(8,128)(2,1)S(1)}, u32[]{:S(2)}, u32[]{:S(2)}) collective-permute-start(bf16[32,7168]{1,0:T(8,128)(2,1)S(1)} %collective-permute-done.5.refs_1_), channel_id=1, source_target_pairs={{0,1},{1,0},{2,3},{3,2},{4,5},{5,4},{6,7},{7,6},{8,9},{9,8},{10,11... | collective-permute-start | bytes 1376264 | tf_op jit(solution)/shard_map/ppermute | solution.py:40
  103.4 3.3 %collective-permute-done.8.refs_1_ = bf16[32,7168]{1,0:T(8,128)(2,1)S(1)} collective-permute-done((bf16[32,7168]{1,0:T(8,128)(2,1)S(1)}, bf16[32,7168]{1,0:T(8,128)(2,1)S(1)}, u32[]{:S(2)}, u32[]{:S(2)}) %collective-permute-start.8) | collective-permute-done | bytes 458784 | tf_op jit(solution)/shard_map/ppermute | solution.py:40
  106.7 8.6 %collective-permute-start.10 = (bf16[32,7168]{1,0:T(8,128)(2,1)S(1)}, bf16[32,7168]{1,0:T(8,128)(2,1)S(1)}, u32[]{:S(2)}, u32[]{:S(2)}) collective-permute-start(bf16[32,7168]{1,0:T(8,128)(2,1)S(1)} %collective-permute-done.8.refs_1_), channel_id=1, source_target_pairs={{0,1},{1,0},{2,3},{3,2},{4,5},{5,4},{6,7},{7,6},{8,9},{9,8},{10,11... | collective-permute-start | bytes 1376264 | tf_op jit(solution)/shard_map/ppermute | solution.py:40
  115.3 1.9 %collective-permute-start.9 = (bf16[32,7168]{1,0:T(8,128)(2,1)S(1)}, bf16[32,7168]{1,0:T(8,128)(2,1)S(1)}, u32[]{:S(2)}, u32[]{:S(2)}) collective-permute-start(bf16[32,7168]{1,0:T(8,128)(2,1)S(1)} %collective-permute-done.7.refs_0_), channel_id=1, source_target_pairs={{0,1},{1,0},{2,3},{3,2},{4,5},{5,4},{6,7},{7,6},{8,9},{9,8},{10,11... | collective-permute-start | bytes 1376264 | tf_op jit(solution)/shard_map/ppermute | solution.py:40
  118.4 1.3 %shard_map.81.refs_4_ = bf16[128,14336]{1,0:T(8,128)(2,1)} custom-call(bf16[32,7168]{1,0:T(8,128)(2,1)S(1)} %shard_map.80.refs_0_, bf16[32,7168]{1,0:T(8,128)(2,1)S(1)} %collective-permute-done.5.refs_1_, bf16[32,7168]{1,0:T(8,128)(2,1)S(1)} %collective-permute-done.11.refs_2_, bf16[32,7168]{1,0:T(8,128)(2,1)S(1)} %collective-permute-done.12.refs_3_), custom_call_target="tpu_custom_call" | custom-call | bytes 3670016 | tf_op jit(solution)/shard_map/pallas_call | solution.py:311
  119.8 1.4 %shard_map.82 = bf16[128,14336]{1,0:T(8,128)(2,1)} custom-call(bf16[32,7168]{1,0:T(8,128)(2,1)S(1)} %collective-permute-done.7.refs_0_, bf16[32,7168]{1,0:T(8,128)(2,1)S(1)} %collective-permute-done.8.refs_1_, bf16[32,7168]{1,0:T(8,128)(2,1)S(1)} %collective-permute-done.9.refs_2_, ...), custom_call_target="tpu_custom_call", output_to_operand_aliasing={{}: (4, {})} | custom-call | bytes 3670016 | tf_op jit(solution)/shard_map/pallas_call | solution.py:311
  (27 shorter events, 6.7 us)
Async XLA Ops:
  0.6 5.7 %copy-start = (bf16[1,128,14336]{2,1,0:T(8,128)(2,1)S(1)}, bf16[1,128,14336]{2,1,0:T(8,128)(2,1)}, u32[]{:S(2)}) copy-start(bf16[1,128,14336]{2,1,0:T(8,128)(2,1)} %param.7) | copy-start | bytes 11010052
  0.6 5.7 %copy-start.1 = (bf16[1,128,128]{2,1,0:T(8,128)(2,1)S(1)}, bf16[1,128,128]{2,1,0:T(8,128)(2,1)}, u32[]{:S(2)}) copy-start(bf16[1,128,128]{2,1,0:T(8,128)(2,1)} %param.6) | copy-start | bytes 98308
  3.8 23.9 %copy-start.3 = (bf16[2,1792]{1,0:T(2,128)(2,1)S(1)}, bf16[2,1792]{1,0:T(2,128)(2,1)}, u32[]{:S(2)}) copy-start(bf16[2,1792]{1,0:T(2,128)(2,1)} %param.4) | copy-start | bytes 21508
  3.8 6.2 %collective-permute-start = (bf16[128,7168]{1,0:T(8,128)(2,1)}, bf16[128,7168]{1,0:T(8,128)(2,1)S(1)}, u32[]{:S(2)}, u32[]{:S(2)}) collective-permute-start(bf16[128,7168]{1,0:T(8,128)(2,1)} %shard_map.76), channel_id=1, source_target_pairs={{0,1},{1,0},{2,3},{3,2},{4,5},{5,4},{6,7},{7,6},{8,9},{9,8},{10,11... | collective-permute-start | bytes 5505032 | tf_op jit(solution)/shard_map/ppermute | solution.py:40
  7.5 44.1 %copy-start.2 = (bf16[1,2,14336]{2,1,0:T(2,128)(2,1)S(1)}, bf16[1,2,14336]{2,1,0:T(2,128)(2,1)}, u32[]{:S(2)}) copy-start(bf16[1,2,14336]{2,1,0:T(2,128)(2,1)} %param.5) | copy-start | bytes 172036
  11.1 22.4 %collective-permute-start.1 = (bf16[32,7168]{1,0:T(8,128)(2,1)}, bf16[32,7168]{1,0:T(8,128)(2,1)S(1)}, u32[]{:S(2)}, u32[]{:S(2)}) collective-permute-start(bf16[32,7168]{1,0:T(8,128)(2,1)} %get-tuple-element.15), channel_id=1, source_target_pairs={{0,4},{1,17},{2,6},{3,19},{4,0},{5,21},{6,2},{7,23},{8,12},{9,25},... | collective-permute-start | bytes 1376264 | tf_op jit(solution)/shard_map/ppermute | solution.py:40
  16.9 27.2 %collective-permute-start.2 = (bf16[32,7168]{1,0:T(8,128)(2,1)S(1)}, bf16[32,7168]{1,0:T(8,128)(2,1)S(1)}, u32[]{:S(2)}, u32[]{:S(2)}) collective-permute-start(bf16[32,7168]{1,0:T(8,128)(2,1)S(1)} %get-tuple-element.16), channel_id=1, source_target_pairs={{0,12},{1,49},{2,14},{3,51},{4,8},{5,53},{6,10},{7,55},{8,4},{9,57... | collective-permute-start | bytes 1376264 | tf_op jit(solution)/shard_map/ppermute | solution.py:40
  23.9 20.2 %collective-permute-start.3 = (bf16[32,7168]{1,0:T(8,128)(2,1)S(1)}, bf16[32,7168]{1,0:T(8,128)(2,1)S(1)}, u32[]{:S(2)}, u32[]{:S(2)}) collective-permute-start(bf16[32,7168]{1,0:T(8,128)(2,1)S(1)} %get-tuple-element.17), channel_id=1, source_target_pairs={{0,8},{1,33},{2,10},{3,35},{4,12},{5,37},{6,14},{7,39},{8,0},{9,41... | collective-permute-start | bytes 1376264 | tf_op jit(solution)/shard_map/ppermute | solution.py:40
  28.3 16.9 %all-to-all-start = ((bf16[8,2,1792]{2,1,0:T(2,128)(2,1)}), bf16[8,2,1792]{2,1,0:T(2,128)(2,1)S(1)}, u32[]{:S(2)}, u32[]{:S(2)}) async-start(bf16[8,2,1792]{2,1,0:T(2,128)(2,1)} %stack.4), calls=%async_computation | async-start | bytes 114688 | tf_op jit(solution)/shard_map/all_to_all | solution.py:340
  45.3 16.1 %all-to-all-start.1 = ((bf16[8,8,3584]{2,1,0:T(8,128)(2,1)}), bf16[8,8,3584]{2,1,0:T(8,128)(2,1)S(1)}, u32[]{:S(2)}, u32[]{:S(2)}) async-start(bf16[8,8,3584]{2,1,0:T(8,128)(2,1)} %bitcast.4), calls=%async_computation.1 | async-start | bytes 917504 | tf_op jit(solution)/shard_map/all_to_all | solution.py:61
  51.8 5.5 %collective-permute-start.4 = (bf16[2,2,7168]{2,1,0:T(2,128)(2,1)S(1)}, bf16[2,2,7168]{2,1,0:T(2,128)(2,1)S(1)}, u32[]{:S(2)}, u32[]{:S(2)}) collective-permute-start(bf16[2,2,7168]{2,1,0:T(2,128)(2,1)S(1)} %get-tuple-element.29), channel_id=1, source_target_pairs={{0,1},{1,0},{2,3},{3,2},{4,5},{5,4},{6,7},{7,6},{8,9},{9,8},{10,11... | collective-permute-start | bytes 172040 | tf_op jit(solution)/shard_map/ppermute | solution.py:40
  78.0 14.0 %collective-permute-start.5 = (bf16[32,7168]{1,0:T(8,128)(2,1)S(1)}, bf16[32,7168]{1,0:T(8,128)(2,1)S(1)}, u32[]{:S(2)}, u32[]{:S(2)}) collective-permute-start(bf16[32,7168]{1,0:T(8,128)(2,1)S(1)} %shard_map.80.refs_0_), channel_id=1, source_target_pairs={{0,4},{1,17},{2,6},{3,19},{4,0},{5,21},{6,2},{7,23},{8,12},{9,25},... | collective-permute-start | bytes 1376264 | tf_op jit(solution)/shard_map/ppermute | solution.py:40
  82.9 23.7 %collective-permute-start.8 = (bf16[32,7168]{1,0:T(8,128)(2,1)S(1)}, bf16[32,7168]{1,0:T(8,128)(2,1)S(1)}, u32[]{:S(2)}, u32[]{:S(2)}) collective-permute-start(bf16[32,7168]{1,0:T(8,128)(2,1)S(1)} %shard_map.80.refs_0_), channel_id=1, source_target_pairs={{0,12},{1,49},{2,14},{3,51},{4,8},{5,53},{6,10},{7,55},{8,4},{9,57... | collective-permute-start | bytes 1376264 | tf_op jit(solution)/shard_map/ppermute | solution.py:40
  86.5 28.8 %collective-permute-start.7 = (bf16[32,7168]{1,0:T(8,128)(2,1)S(1)}, bf16[32,7168]{1,0:T(8,128)(2,1)S(1)}, u32[]{:S(2)}, u32[]{:S(2)}) collective-permute-start(bf16[32,7168]{1,0:T(8,128)(2,1)S(1)} %shard_map.80.refs_0_), channel_id=1, source_target_pairs={{0,8},{1,33},{2,10},{3,35},{4,12},{5,37},{6,14},{7,39},{8,0},{9,41... | collective-permute-start | bytes 1376264 | tf_op jit(solution)/shard_map/ppermute | solution.py:40
  92.1 25.2 %collective-permute-start.6 = (f32[2,7168]{1,0:T(2,128)S(1)}, f32[2,7168]{1,0:T(2,128)S(1)}, u32[]{:S(2)}, u32[]{:S(2)}) collective-permute-start(f32[2,7168]{1,0:T(2,128)S(1)} %get-tuple-element.23), channel_id=1, source_target_pairs={{0,1},{1,0},{2,3},{3,2},{4,5},{5,4},{6,7},{7,6},{8,9},{9,8},{10,11... | collective-permute-start | bytes 172040 | tf_op jit(solution)/shard_map/ppermute | solution.py:40
  99.0 19.4 %collective-permute-start.11 = (bf16[32,7168]{1,0:T(8,128)(2,1)S(1)}, bf16[32,7168]{1,0:T(8,128)(2,1)S(1)}, u32[]{:S(2)}, u32[]{:S(2)}) collective-permute-start(bf16[32,7168]{1,0:T(8,128)(2,1)S(1)} %shard_map.80.refs_0_), channel_id=1, source_target_pairs={{0,1},{1,0},{2,3},{3,2},{4,5},{5,4},{6,7},{7,6},{8,9},{9,8},{10,11... | collective-permute-start | bytes 1376264 | tf_op jit(solution)/shard_map/ppermute | solution.py:40
  101.0 17.5 %collective-permute-start.12 = (bf16[32,7168]{1,0:T(8,128)(2,1)S(1)}, bf16[32,7168]{1,0:T(8,128)(2,1)S(1)}, u32[]{:S(2)}, u32[]{:S(2)}) collective-permute-start(bf16[32,7168]{1,0:T(8,128)(2,1)S(1)} %collective-permute-done.5.refs_1_), channel_id=1, source_target_pairs={{0,1},{1,0},{2,3},{3,2},{4,5},{5,4},{6,7},{7,6},{8,9},{9,8},{10,11... | collective-permute-start | bytes 1376264 | tf_op jit(solution)/shard_map/ppermute | solution.py:40
  106.7 13.1 %collective-permute-start.10 = (bf16[32,7168]{1,0:T(8,128)(2,1)S(1)}, bf16[32,7168]{1,0:T(8,128)(2,1)S(1)}, u32[]{:S(2)}, u32[]{:S(2)}) collective-permute-start(bf16[32,7168]{1,0:T(8,128)(2,1)S(1)} %collective-permute-done.8.refs_1_), channel_id=1, source_target_pairs={{0,1},{1,0},{2,3},{3,2},{4,5},{5,4},{6,7},{7,6},{8,9},{9,8},{10,11... | collective-permute-start | bytes 1376264 | tf_op jit(solution)/shard_map/ppermute | solution.py:40
  115.3 4.5 %collective-permute-start.9 = (bf16[32,7168]{1,0:T(8,128)(2,1)S(1)}, bf16[32,7168]{1,0:T(8,128)(2,1)S(1)}, u32[]{:S(2)}, u32[]{:S(2)}) collective-permute-start(bf16[32,7168]{1,0:T(8,128)(2,1)S(1)} %collective-permute-done.7.refs_0_), channel_id=1, source_target_pairs={{0,1},{1,0},{2,3},{3,2},{4,5},{5,4},{6,7},{7,6},{8,9},{9,8},{10,11... | collective-permute-start | bytes 1376264 | tf_op jit(solution)/shard_map/ppermute | solution.py:40
